TPU v7x, 256 devices: a whole 4x4x8 slice. The times are simulated.
256 devices in a mesh: dp: 16 (over y, x), expert: 16 (over z, core).
Axes of the slice: x: 4, y: 4, z: 8, core: 2. Of those that a mesh axis runs over, the one named last changes fastest.
Arguments:
- tokens: bfloat16 [32768, 1024], P(('dp', 'expert')), may hold values from -6 to 6
- cotangent: bfloat16 [32768, 1024], P(('dp', 'expert')), may hold values from -6 to 6
- expert_ids: int32 [32768, 8], P(('dp', 'expert')), may hold values from 0 to 31, all different within a row; in each aligned block of 128 rows (0 to 127, 128 to 255, ...) at most 40 rows name the same one
- gate_probs: bfloat16 [32768, 8], P(('dp', 'expert')), may hold values from 0.049804688 to 0.5
- gate_up: bfloat16 [32, 1024, 1024], P('expert', 'dp'), may hold values from -0.1875 to 0.1875
- down_proj: bfloat16 [32, 512, 1024], P('expert', 'dp'), may hold values from -0.25 to 0.25
Outputs:
- grad_tokens: bfloat16 [32768, 1024], P(('dp', 'expert'))
- grad_gates: bfloat16 [32768, 8], P(('dp', 'expert'))
- grad_gate_up: float32 [32, 1024, 1024], P('expert', 'dp')
- grad_down: float32 [32, 512, 1024], P('expert', 'dp')
Inputs may be any that keep to these rules, and one draw needn't show every extreme that they name: `expert_ids`: each token names 8 different experts. Among the 128 tokens of one device (aligned blocks of rows) no expert is named more than 40 times, and in every draw some expert is named exactly 40 times by the tokens of some device.
All inputs are finite; a program needn't handle non-finite values.
Results may differ from a plain program's by a relative error of at most 0.0058.
Values may be sent and summed in bfloat16 or wider, within the bound.
No kernel may reach another device: no remote copies, remote signals or barrier semaphores. Data moves between devices by JAX's collectives and lax.ppermute only.
A program may use at most 128 MiB of HBM per device.

v0:
```python
import functools

import jax
import jax.numpy as jnp
from jax import lax
from jax.experimental import pallas as pl
from jax.experimental.pallas import tpu as pltpu
from jax.sharding import Mesh
from jax.sharding import PartitionSpec as P

BF16 = jnp.bfloat16
F32 = jnp.float32
TOP = 8
CAP = 40
TOK = 128
WIDTH = 1024
HID = 512
ROWS_IN = 64
ROWS_OUT = 32
ROWS = ROWS_IN + ROWS_OUT
CHIPS = 8
PAIR = 2 * CAP
SLOTS = CHIPS * PAIR
MIB = 1024 * 1024

UP = [(i, (i + 1) % 4) for i in range(4)]
DOWN = [(i, (i - 1) % 4) for i in range(4)]
ACROSS = [(i, (i + 2) % 4) for i in range(4)]


def dot(a, b, dims):
    return lax.dot_general(a, b, (dims, ((), ())), preferred_element_type=F32)


NN = ((1,), (0,))
NT = ((1,), (1,))
TN = ((0,), (0,))


def call(kernel, name, out_shape, *args, scalars=0, specs=None, out_specs=None, scratch=(), cost=None, limit=8, **more):
    vmem = pl.BlockSpec(memory_space=pltpu.VMEM)
    smem = pl.BlockSpec(memory_space=pltpu.SMEM)
    n = len(args) - scalars
    many = isinstance(out_shape, list)
    return pl.pallas_call(
        kernel,
        name=name,
        in_specs=[smem] * scalars + (specs or [vmem] * n),
        out_specs=out_specs or ([vmem] * len(out_shape) if many else vmem),
        out_shape=out_shape,
        scratch_shapes=list(scratch),
        compiler_params=pltpu.CompilerParams(vmem_limit_bytes=limit * MIB),
        cost_estimate=cost,
        **more,
    )(*args)


def cost(flops, nbytes):
    return pl.CostEstimate(flops=flops, bytes_accessed=nbytes, transcendentals=0)


def shape(*dims, dtype=BF16):
    return jax.ShapeDtypeStruct(dims, dtype)


ANY = pl.BlockSpec(memory_space=pl.ANY)
HBM = pl.BlockSpec(memory_space=pltpu.HBM)
VM = pl.BlockSpec(memory_space=pltpu.VMEM)


def pack_kernel(tok, cot, ids, probs, gu, dn, pay, own0, own1, buf, meta, wbuf, sem):
    halves = [
        pltpu.make_async_copy(tok, buf.at[0], sem.at[0]),
        pltpu.make_async_copy(cot, buf.at[1], sem.at[1]),
    ]
    weights = [
        pltpu.make_async_copy(gu, wbuf.at[:, pl.ds(0, ROWS_IN)], sem.at[2]),
        pltpu.make_async_copy(dn, wbuf.at[:, pl.ds(ROWS_IN, ROWS_OUT)], sem.at[3]),
    ]
    for copy in halves + weights:
        copy.start()
    meta[...] = jnp.zeros_like(meta)
    meta[:, 0:TOK] = ids[...].astype(F32).astype(BF16)
    meta[:, TOK : 2 * TOK] = probs[...]
    out = [pltpu.make_async_copy(meta, pay.at[pl.ds(2 * TOK, TOP)], sem.at[4])]
    out[0].start()
    for i in range(2):
        halves[i].wait()
        out.append(pltpu.make_async_copy(buf.at[i], pay.at[pl.ds(i * TOK, TOK)], sem.at[5 + i]))
        out[-1].start()
    for copy in weights:
        copy.wait()
    for i in range(4):
        own0[i] = wbuf[0]
        own1[i] = wbuf[1]
    for copy in out:
        copy.wait()


def pack(tokens, cotangent, ids, probs, gate_up, down_proj):
    return call(
        pack_kernel,
        "pack",
        [shape(2 * TOK + TOP, WIDTH), shape(4, ROWS, WIDTH), shape(4, ROWS, WIDTH)],
        tokens,
        cotangent,
        ids,
        probs,
        gate_up,
        down_proj,
        specs=[HBM, HBM, VM, VM, HBM, HBM],
        out_specs=[HBM, VM, VM],
        limit=60,
        scratch=[
            pltpu.VMEM((2, TOK, WIDTH), BF16),
            pltpu.VMEM((TOP, WIDTH), BF16),
            pltpu.VMEM((2, ROWS, WIDTH), BF16),
            pltpu.SemaphoreType.DMA((7,)),
        ],
        cost=cost(0, 2_000_000),
    )


PIECES = ((4, ROWS, WIDTH),) * 3 + ((2, ROWS, WIDTH),) * 2
TILE = 256
START_AT = 2


def load_weights(e, outer_pos, pieces, w_in, w_out, sem):
    own, below, above, far_a, far_b = pieces
    copies = []
    for offset, lo, src in ((0, 0, own), (1, 0, below), (3, 0, above), (2, 0, far_a), (2, 2, far_b)):
        outer = lax.rem(outer_pos + 4 - offset, 4)
        inner = pl.ds(lo, src.shape[0])
        for rows, dst in ((pl.ds(0, ROWS_IN), w_in), (pl.ds(ROWS_IN, ROWS_OUT), w_out)):
            at = dst.at[outer, inner] if e == 0 else dst.at[inner, outer]
            copies.append(pltpu.make_async_copy(src.at[:, rows], at, sem.at[len(copies)]))
    return copies


def route_pair(p, first, pay, x_ref, dy_ref, gate_ref, sel_ref, upper, slot):
    named, weights = [], []
    for e in range(2):
        expert = (first + e).astype(F32)
        for c in range(2):
            part = pay[2 * p + c, 2 * TOK : 2 * TOK + TOP, 0 : 2 * TOK]
            hit = jnp.where(part[:, :TOK].astype(F32) == expert, 1.0, 0.0)
            named.append(jnp.sum(hit, axis=0, keepdims=True))
            weights.append(jnp.sum(hit * part[:, TOK:].astype(F32), axis=0, keepdims=True))
    marks = jnp.concatenate(named + named, axis=0)
    ranks = dot(marks.astype(BF16), upper, NN)
    picks = []
    for e in range(2):
        halves = []
        for c in range(2):
            i = 2 * e + c
            at = jnp.where(marks[i : i + 1] > 0.5, ranks[i : i + 1] + float(CAP * c), -1.0)
            halves.append(jnp.where(slot == at, 1.0, 0.0))
        pick = jnp.concatenate(halves, axis=1)
        prob = jnp.concatenate([weights[2 * e], weights[2 * e + 1]], axis=1)
        column = jnp.sum(pick * prob, axis=1, keepdims=True)
        gate_ref[e, PAIR * p : PAIR * (p + 1)] = jnp.broadcast_to(column, (PAIR, TOK))
        picks.append(pick)
    sel = jnp.concatenate(picks, axis=0).astype(BF16)
    sel_ref[p] = sel
    rows = pl.ds(PAIR * p, PAIR)
    for lo, out in ((0, x_ref), (TOK, dy_ref)):
        both = jnp.concatenate([pay[2 * p, lo : lo + TOK], pay[2 * p + 1, lo : lo + TOK]], axis=0)
        routed = dot(sel, both, NN).astype(BF16)
        out[0, rows] = routed[:PAIR]
        out[1, rows] = routed[PAIR:]


def stores_of(held, grads, sem):
    own, up, down, far_a, far_b = grads
    return [
        pltpu.make_async_copy(held.at[2, pl.ds(0, 2)], far_a, sem.at[0]),
        pltpu.make_async_copy(held.at[2, pl.ds(2, 2)], far_b, sem.at[1]),
        pltpu.make_async_copy(held.at[1], up, sem.at[2]),
        pltpu.make_async_copy(held.at[3], down, sem.at[3]),
        pltpu.make_async_copy(held.at[0], own, sem.at[4]),
    ]


def expert_step(
    first, outer_pos, inner_pos, x, dy, gate, w_in, w_out, held, dx, sg,
    pre, act, xt, at, gin, gout,
):
    def flip(i, _):
        c = pl.multiple_of(i * 128, 128)
        xt[pl.ds(c, 128), :] = x[:, pl.ds(c, 128)].T
        return 0

    lax.fori_loop(0, WIDTH // 128, flip, 0, unroll=True)
    sg[...] = jnp.zeros_like(sg)

    def forward(i, _):
        lo = pl.multiple_of(i * TILE, TILE)
        hi = pl.multiple_of(HID + i * TILE, TILE)
        wg = w_in[:, :, :, pl.ds(lo, TILE)].reshape(WIDTH, TILE)
        wu = w_in[:, :, :, pl.ds(hi, TILE)].reshape(WIDTH, TILE)
        wd = w_out[pl.ds(2 * i, 2)].reshape(TILE, WIDTH)
        gate_pre = dot(x[...], wg, NN)
        up_pre = dot(x[...], wu, NN)
        raw = dot(dy[...], wd, NT)
        prob = gate[:, 0:1]
        s = jax.nn.sigmoid(gate_pre)
        silu = gate_pre * s
        activation = silu * up_pre
        act_grad = prob * raw
        d_gate = act_grad * up_pre * s * (1.0 + gate_pre * (1.0 - s))
        pre[:, pl.ds(lo, TILE)] = d_gate.astype(BF16)
        pre[:, pl.ds(hi, TILE)] = (act_grad * silu).astype(BF16)
        act[:, pl.ds(lo, TILE)] = (prob * activation).astype(BF16)
        total = jnp.sum(activation * raw, axis=1, keepdims=True)
        sg[...] += jnp.broadcast_to(total, sg.shape)
        return 0

    lax.fori_loop(0, HID // TILE, forward, 0, unroll=True)

    def flip_act(i, _):
        c = pl.multiple_of(i * 128, 128)
        at[pl.ds(c, 128), :] = act[:, pl.ds(c, 128)].T
        return 0

    lax.fori_loop(0, HID // 128, flip_act, 0, unroll=True)

    def backward(i, _):
        cols = pl.ds(pl.multiple_of(i * TILE, TILE), TILE)
        gin[...] = dot(xt[...], pre[:, cols], NN).astype(BF16).reshape(gin.shape)
        gout[...] = dot(at[...], dy[:, cols], NN).astype(BF16).reshape(gout.shape)
        for oj in range(4):
            for ij in range(4):
                outer = lax.rem(outer_pos + oj, 4)
                inner = lax.rem(inner_pos + ij, 4)
                b = jnp.where(first, outer * 4 + inner, inner * 4 + outer)
                held[oj, ij, 0:ROWS_IN, cols] = gin[b]
                held[oj, ij, ROWS_IN:ROWS, cols] = gout[b]
        return 0

    lax.fori_loop(0, WIDTH // TILE, backward, 0, unroll=True)

    def input_grad(i, _):
        w = w_in[i].reshape(TILE, WIDTH)
        lo = pl.multiple_of(i * TILE, TILE)
        dx[:, pl.ds(lo, TILE)] = dot(pre[...], w, NT).astype(BF16)
        return 0

    lax.fori_loop(0, WIDTH // TILE, input_grad, 0, unroll=True)


def combine_pair(p, first, pay, sel_ref, dx, sg, part):
    sel = sel_ref[p]
    at = pl.ds(PAIR * p, PAIR)
    rows = jnp.concatenate([dx[0, at], dx[1, at]], axis=0)
    back = dot(sel, rows, TN).astype(BF16)
    sums = jnp.concatenate([sg[0, at, 0:1], sg[1, at, 0:1]], axis=0)
    sums = sums.astype(BF16).astype(F32)
    spread = sel.astype(F32) * sums
    totals = [
        jnp.sum(spread[:PAIR], axis=0, keepdims=True),
        jnp.sum(spread[PAIR:], axis=0, keepdims=True),
    ]
    for c in range(2):
        part[c, 0:TOK] = back[c * TOK : (c + 1) * TOK]
        ids = pay[2 * p + c, 2 * TOK : 2 * TOK + TOP, 0:TOK].astype(F32)
        value = jnp.zeros((TOP, TOK), F32)
        for e in range(2):
            hit = ids == (first + e).astype(F32)
            value = value + jnp.where(hit, totals[e][:, c * TOK : (c + 1) * TOK], 0.0)
        part[c, TOK : TOK + TOP] = jnp.zeros((TOP, WIDTH), BF16)
        part[c, TOK : TOK + TOP, 0:TOK] = value.astype(BF16)


def experts_kernel(where, pay_hbm, *refs):
    pieces = refs[0:5], refs[5:10]
    grads = refs[10:15], refs[15:20]
    keep, send = refs[20:22]
    pay, x, dy, gate, sel, dx, sg, w_in, w_out, pre, act, xt, at, gin, gout, part = refs[22:38]
    held, psem, wsem, gsem, csem = refs[38:]
    first, core, iy, ix = where[0], where[1], where[2], where[3]
    loads = [
        pltpu.make_async_copy(pay_hbm.at[pl.ds(2 * p, 2)], pay.at[pl.ds(2 * p, 2)], psem.at[p])
        for p in range(CHIPS)
    ]
    for copy in loads:
        copy.start()
    weights = [
        load_weights(e, (iy, ix)[e], pieces[e], w_in.at[e], w_out.at[e], wsem.at[e])
        for e in range(2)
    ]
    upper = (
        lax.broadcasted_iota(jnp.int32, (TOK, TOK), 0)
        < lax.broadcasted_iota(jnp.int32, (TOK, TOK), 1)
    ).astype(BF16)
    slot = lax.broadcasted_iota(jnp.int32, (PAIR, TOK), 0).astype(F32)
    for p in range(CHIPS):
        loads[p].wait()
        if p == START_AT:
            for copy in weights[0]:
                copy.start()
        route_pair(p, first, pay, x, dy, gate, sel, upper, slot)

    def one(e, _):
        for n in range(10):
            src = pieces[0][(0, 0, 0, 3, 3)[n // 2]]
            rows, dst = ((pl.ds(0, ROWS_IN), w_in), (pl.ds(ROWS_IN, ROWS_OUT), w_out))[n % 2]
            inner = pl.ds(0, src.shape[0])
            pltpu.make_async_copy(src.at[:, rows], dst.at[e, 0, inner], wsem.at[e, n]).wait()

        @pl.when(e == 0)
        def _():
            for copy in weights[1]:
                copy.start()

        outer_pos = jnp.where(e == 0, iy, ix)
        inner_pos = jnp.where(e == 0, ix, iy)
        expert_step(
            e == 0, outer_pos, inner_pos, x.at[e], dy.at[e], gate.at[e], w_in.at[e], w_out.at[e],
            held.at[e], dx.at[e], sg.at[e], pre, act, xt, at, gin, gout,
        )
        for i in range(2):

            @pl.when(e == i)
            def _():
                for copy in stores_of(held.at[i], grads[i], gsem.at[i]):
                    copy.start()

        return 0

    lax.fori_loop(0, 2, one, 0)
    outs = []
    for p in range(CHIPS):
        combine_pair(p, first, pay, sel, dx, sg, part.at[p])
        for i, (c, out) in enumerate(((core, keep), (1 - core, send))):
            copy = pltpu.make_async_copy(part.at[p, c], out.at[p], csem.at[2 * p + i])
            copy.start()
            outs.append(copy)
    for e in range(2):
        outs += stores_of(held.at[e], grads[e], gsem.at[e])
    for copy in outs:
        copy.wait()


def experts(where, pay, pieces0, pieces1):
    near = pltpu.VMEM((4, ROWS, WIDTH), BF16)
    return call(
        experts_kernel,
        "experts",
        [shape(4, ROWS, WIDTH), near, near, *[shape(2, ROWS, WIDTH)] * 2] * 2
        + [pltpu.VMEM((CHIPS, TOK + TOP, WIDTH), BF16), shape(CHIPS, TOK + TOP, WIDTH)],
        where,
        pay,
        *pieces0,
        *pieces1,
        scalars=1,
        specs=[HBM] + [HBM] * 10,
        out_specs=[HBM, VM, VM, HBM, HBM] * 2 + [VM, HBM],
        scratch=[
            pltpu.VMEM((2 * CHIPS, 2 * TOK + TOP, WIDTH), BF16),
            pltpu.VMEM((2, SLOTS, WIDTH), BF16),
            pltpu.VMEM((2, SLOTS, WIDTH), BF16),
            pltpu.VMEM((2, SLOTS, TOK), F32),
            pltpu.VMEM((CHIPS, 2 * PAIR, 2 * TOK), BF16),
            pltpu.VMEM((2, SLOTS, WIDTH), BF16),
            pltpu.VMEM((2, SLOTS, TOK), F32),
            pltpu.VMEM((2, 4, 4, ROWS_IN, WIDTH), BF16),
            pltpu.VMEM((2, 4, 4, ROWS_OUT, WIDTH), BF16),
            pltpu.VMEM((SLOTS, WIDTH), BF16),
            pltpu.VMEM((SLOTS, HID), BF16),
            pltpu.VMEM((WIDTH, SLOTS), BF16),
            pltpu.VMEM((HID, SLOTS), BF16),
            pltpu.VMEM((16, ROWS_IN, TILE), BF16),
            pltpu.VMEM((16, ROWS_OUT, TILE), BF16),
            pltpu.VMEM((CHIPS, 2, TOK + TOP, WIDTH), BF16),
            pltpu.VMEM((2, 4, 4, ROWS, WIDTH), BF16),
            pltpu.SemaphoreType.DMA((CHIPS,)),
            pltpu.SemaphoreType.DMA((2, 10)),
            pltpu.SemaphoreType.DMA((2, 5)),
            pltpu.SemaphoreType.DMA((2 * CHIPS,)),
        ],
        cost=cost(4 * 640 * 1024 * 4096, 20_000_000),
        limit=50,
    )


def add(a, b):
    return a.astype(F32) + b.astype(F32)


def fold_kernel(*refs):
    blocks, arrived, (keep, got) = refs[0:4], refs[4:8], refs[8:10]
    outs, pair = refs[10:14], refs[14]
    block_buf, pair_buf, sem = refs[15:]
    pair_buf[...] = add(keep[...], got[...]).astype(BF16)
    stores = [pltpu.make_async_copy(pair_buf, pair, sem.at[4])]
    stores[0].start()
    for i in range(4):
        lo = 2 * (i % 2)
        block_buf[i, lo : lo + 2] = add(blocks[i][lo : lo + 2], arrived[i][...]).astype(BF16)
        block_buf[i, 2 - lo : 4 - lo] = blocks[i][2 - lo : 4 - lo]
        stores.append(pltpu.make_async_copy(block_buf.at[i], outs[i], sem.at[i]))
        stores[-1].start()
    for copy in stores:
        copy.wait()


def fold(*parts):
    return call(
        fold_kernel,
        "fold",
        [shape(4, ROWS, WIDTH)] * 4 + [shape(CHIPS, TOK + TOP, WIDTH)],
        *parts,
        out_specs=[HBM] * 5,
        scratch=[
            pltpu.VMEM((4, 4, ROWS, WIDTH), BF16),
            pltpu.VMEM((CHIPS, TOK + TOP, WIDTH), BF16),
            pltpu.SemaphoreType.DMA((5,)),
        ],
        cost=cost(0, 1024),
        limit=16,
    )


def total_kernel(*refs):
    for e in range(2):
        own, below, above = refs[3 * e : 3 * e + 3]
        outs = refs[6 + 4 * e : 10 + 4 * e]
        for i in range(4):
            value = add(own[i], below[i]) + above[i].astype(F32)
            outs[i][...] = value if i == 0 else value.astype(BF16)


def totals_of(*parts):
    outs = [shape(ROWS, WIDTH, dtype=F32)] + [shape(ROWS, WIDTH)] * 3
    return call(total_kernel, "total", outs * 2, *parts, cost=cost(0, 1024))


def finish_kernel(*refs):
    done = refs[8]
    d_tok, d_gate, d_in, d_out = refs[9:]
    for e in range(2):
        kept, a, b, c = refs[4 * e : 4 * e + 4]
        total = kept[...] + a[...].astype(F32) + b[...].astype(F32) + c[...].astype(F32)
        d_in[e] = total[:ROWS_IN]
        d_out[e] = total[ROWS_IN:]
    d_tok[...] = done[:TOK]
    d_gate[...] = done[TOK:, :TOK]


def finish(*parts):
    return call(
        finish_kernel,
        "finish",
        [
            shape(TOK, WIDTH),
            shape(TOP, TOK),
            shape(2, ROWS_IN, WIDTH, dtype=F32),
            shape(2, ROWS_OUT, WIDTH, dtype=F32),
        ],
        *parts,
        cost=cost(0, 1024),
    )


def gather_ring(block, axis):
    half = block.shape[0] // 2
    below = lax.ppermute(block, axis, UP)
    above = lax.ppermute(block, axis, DOWN)
    far_a = lax.ppermute(below[:half], axis, UP)
    far_b = lax.ppermute(above[half:], axis, DOWN)
    return block, below, above, far_a, far_b


def gather_weights(own, inner, outer):
    return gather_ring(lax.all_to_all(own, inner, split_axis=0, concat_axis=0, tiled=True), outer)


def swap(a, b, axis):
    return lax.ppermute(a, axis, UP), lax.ppermute(b, axis, DOWN)


def spread(parts, axis):
    kept, up, far, down = parts
    up, down = swap(up, down, axis)
    return kept, up, lax.ppermute(far, axis, ACROSS), down


def body(tokens, cotangent, expert_ids, gate_probs, gate_up, down_proj):
    ix = lax.axis_index("x").astype(jnp.int32)
    iy = lax.axis_index("y").astype(jnp.int32)
    core = lax.axis_index("core").astype(jnp.int32)
    first = (2 * (2 * lax.axis_index("z") + core)).astype(jnp.int32)
    where, ids = lax.optimization_barrier((jnp.stack([first, core, iy, ix]), expert_ids.T))
    pay, own0, own1 = pack(tokens, cotangent, ids, gate_probs.T, gate_up, down_proj)
    pay = lax.all_gather(pay, ("z", "core"), axis=0, tiled=False)
    pieces0 = gather_weights(own0, "x", "y")
    pieces1 = gather_weights(own1, "y", "x")

    out = experts(where, pay, pieces0, pieces1)
    mine0, up0, dn0, a0, b0 = out[:5]
    mine1, up1, dn1, a1, b1 = out[5:10]
    keep, send = out[10:]
    got = lax.ppermute(send, "core", [(0, 1), (1, 0)])
    below0, above0 = swap(a0, b0, "y")
    below1, above1 = swap(a1, b1, "x")
    up0, dn0, up1, dn1, pair = fold(
        up0, dn0, up1, dn1, below0, above0, below1, above1, keep, got
    )
    below0, above0 = swap(up0, dn0, "y")
    below1, above1 = swap(up1, dn1, "x")
    done = lax.psum_scatter(
        pair.reshape(CHIPS * (TOK + TOP), WIDTH), "z", scatter_dimension=0, tiled=True
    )
    out = totals_of(mine0, below0, above0, mine1, below1, above1)
    grad_tokens, grad_gates, grad_gate_up, grad_down = finish(
        *spread(out[:4], "x"), *spread(out[4:], "y"), done
    )
    return grad_tokens, grad_gates.T, grad_gate_up, grad_down


def solution(mesh):
    grid = Mesh(mesh.devices.reshape(4, 4, 8, 2), ("y", "x", "z", "core"))
    rows = P(("y", "x", "z", "core"), None)
    held = P(("z", "core"), ("y", "x"), None)
    return jax.shard_map(
        body,
        mesh=grid,
        in_specs=(rows, rows, rows, rows, held, held),
        out_specs=(rows, rows, held, held),
        check_vma=False,
    )
```

profile of v0, /device:TPU:24, one launch (start us, length us, event | category | flops | bytes accessed | tf_op | source)
XLA Modules:
  0.0 167.4 jit_solution(16838388887920693134)
XLA Ops:
  7.2 0.0 all-gather.3.cloned.1.call-start
  7.2 0.6 pad_add_fusion.where
  7.8 3.7 %pack.1 = (bf16[264,1024]{1,0:T(8,128)(2,1)}, bf16[4,96,1024]{2,1,0:T(8,128)(2,1)}, bf16[4,96,1024]{2,1,0:T(8,128)(2,1)}) custom-call(bf16[128,1024]{1,0:T(8,128)(2,1)} %tok.1, bf16[128,1024]{1,0:T(8,128)(2,1)} %cot.1, s32[8,128]{1,0:T(8,128)} %bitcast.9, bf16[8,128]{1,0:T(8,128)(2,1)} %bitcast.10, bf16[2,64,1024]{2,1,0:T(8,128)(2,1)} %gu.1, ...), custom_call_target="tpu_custom_call" | custom-call | bytes 2000000 | tf_op jit(solution)/shard_map/pack/pallas_call | solution.py:45
  11.5 0.0 all-gather.3.cloned.1.call-update
  11.6 14.9 %all_to_all.10.refs_5_ = bf16[4,96,1024]{2,1,0:T(8,128)(2,1)S(1)} all-to-all(bf16[4,96,1024]{2,1,0:T(8,128)(2,1)} %get-tuple-element.42), channel_id=1, replica_groups=mesh['y'=4,'x'=4,'z'=8,'core'=2] {'y'}, dimensions={0} | all-to-all | bytes 1572864 | tf_op jit(solution)/shard_map/all_to_all | solution.py:476
  26.5 4.3 %all-to-all-start = ((bf16[4,96,1024]{2,1,0:T(8,128)(2,1)}), bf16[4,96,1024]{2,1,0:T(8,128)(2,1)S(1)}, u32[]{:S(2)}, u32[]{:S(2)}) async-start(bf16[4,96,1024]{2,1,0:T(8,128)(2,1)} %get-tuple-element.41), calls=%async_computation | async-start | bytes 1572864 | tf_op jit(solution)/shard_map/all_to_all | solution.py:476
  30.8 3.2 %collective-permute-start.5 = (bf16[4,96,1024]{2,1,0:T(8,128)(2,1)S(1)}, bf16[4,96,1024]{2,1,0:T(8,128)(2,1)S(1)}, u32[]{:S(2)}, u32[]{:S(2)}) collective-permute-start(bf16[4,96,1024]{2,1,0:T(8,128)(2,1)S(1)} %all_to_all.10.refs_5_), channel_id=1, source_target_pairs={{0,48},{16,0},{32,16},{48,32},{1,49},{17,1},{33,17},{49,33},{2,50}... | collective-permute-start | bytes 2359304 | tf_op jit(solution)/shard_map/ppermute | solution.py:469
  34.0 0.0 collective-permute-start.4
  34.0 10.5 %all-to-all-done.refs_0_ = bf16[4,96,1024]{2,1,0:T(8,128)(2,1)S(1)} async-done(((bf16[4,96,1024]{2,1,0:T(8,128)(2,1)}), bf16[4,96,1024]{2,1,0:T(8,128)(2,1)S(1)}, u32[]{:S(2)}, u32[]{:S(2)}) %all-to-all-start) | async-done | bytes 786464 | tf_op jit(solution)/shard_map/all_to_all | solution.py:476
  44.5 0.2 collective-permute-start.1
  44.8 3.0 %collective-permute-start = (bf16[4,96,1024]{2,1,0:T(8,128)(2,1)S(1)}, bf16[4,96,1024]{2,1,0:T(8,128)(2,1)S(1)}, u32[]{:S(2)}, u32[]{:S(2)}) collective-permute-start(bf16[4,96,1024]{2,1,0:T(8,128)(2,1)S(1)} %all-to-all-done.refs_0_), channel_id=1, source_target_pairs={{0,64},{64,128},{128,192},{192,0},{1,65},{65,129},{129,193},{193,1... | collective-permute-start | bytes 2359304 | tf_op jit(solution)/shard_map/ppermute | solution.py:468
  47.8 9.4 %collective-permute-done.5.refs_7_ = bf16[4,96,1024]{2,1,0:T(8,128)(2,1)S(1)} collective-permute-done((bf16[4,96,1024]{2,1,0:T(8,128)(2,1)S(1)}, bf16[4,96,1024]{2,1,0:T(8,128)(2,1)S(1)}, u32[]{:S(2)}, u32[]{:S(2)}) %collective-permute-start.5) | collective-permute-done | bytes 786464 | tf_op jit(solution)/shard_map/ppermute | solution.py:469
  57.3 1.8 %collective-permute-start.7 = (bf16[2,96,1024]{2,1,0:T(8,128)(2,1)S(1)}, bf16[2,96,1024]{2,1,0:T(8,128)(2,1)S(1)}, u32[]{:S(2)}, u32[]{:S(2)}) collective-permute-start(bf16[2,96,1024]{2,1,0:T(8,128)(2,1)S(1)} %slice.19), channel_id=1, source_target_pairs={{0,48},{16,0},{32,16},{48,32},{1,49},{17,1},{33,17},{49,33},{2,50}... | collective-permute-start | bytes 1179656 | tf_op jit(solution)/shard_map/ppermute | solution.py:471
  59.0 0.0 collective-permute-done.4.refs_6_
  59.1 0.4 collective-permute-start.6
  59.5 0.3 collective-permute-done.1.refs_2_
  59.8 0.1 collective-permute-start.3
  59.9 0.8 copy-done.9
  60.6 0.0 collective-permute-done.refs_1_
  60.7 2.7 %collective-permute-start.2 = (bf16[2,96,1024]{2,1,0:T(8,128)(2,1)S(1)}, bf16[2,96,1024]{2,1,0:T(8,128)(2,1)}, u32[]{:S(2)}, u32[]{:S(2)}) collective-permute-start(bf16[2,96,1024]{2,1,0:T(8,128)(2,1)S(1)} %slice.16), channel_id=1, source_target_pairs={{0,64},{64,128},{128,192},{192,0},{1,65},{65,129},{129,193},{193,1... | collective-permute-start | bytes 1179656 | tf_op jit(solution)/shard_map/ppermute | solution.py:470
  63.4 2.5 %collective-permute-done.7.refs_9_ = bf16[2,96,1024]{2,1,0:T(8,128)(2,1)S(1)} collective-permute-done((bf16[2,96,1024]{2,1,0:T(8,128)(2,1)S(1)}, bf16[2,96,1024]{2,1,0:T(8,128)(2,1)S(1)}, u32[]{:S(2)}, u32[]{:S(2)}) %collective-permute-start.7) | collective-permute-done | bytes 393248 | tf_op jit(solution)/shard_map/ppermute | solution.py:471
  65.9 3.5 %collective-permute-done.6.refs_8_ = bf16[2,96,1024]{2,1,0:T(8,128)(2,1)S(1)} collective-permute-done((bf16[2,96,1024]{2,1,0:T(8,128)(2,1)S(1)}, bf16[2,96,1024]{2,1,0:T(8,128)(2,1)S(1)}, u32[]{:S(2)}, u32[]{:S(2)}) %collective-permute-start.6) | collective-permute-done | bytes 393248 | tf_op jit(solution)/shard_map/ppermute | solution.py:470
  69.4 0.1 collective-permute-done.3.refs_4_
  69.5 0.6 copy-done.12
  70.1 0.7 copy-done.13
  70.9 0.0 collective-permute-done.2.refs_3_
  70.9 0.7 all-gather.3.cloned.1.call-done
  71.6 23.6 %experts.1 = (bf16[4,96,1024]{2,1,0:T(8,128)(2,1)}, bf16[4,96,1024]{2,1,0:T(8,128)(2,1)S(1)}, bf16[4,96,1024]{2,1,0:T(8,128)(2,1)S(1)}, bf16[2,96,1024]{2,1,0:T(...) custom-call(s32[4]{0:T(128)} %pad_add_fusion.where, ...), custom_call_target="tpu_custom_call" | custom-call | flops 10737418240 | bytes 20000000 | tf_op jit(solution)/shard_map/experts/pallas_call | solution.py:45
  95.1 0.3 collective-permute-start.12
  95.5 1.2 collective-permute-start.8
  96.7 0.8 collective-permute-start.9
  97.5 1.5 collective-permute-start.10
  99.0 1.8 %collective-permute-start.11 = (bf16[2,96,1024]{2,1,0:T(8,128)(2,1)}, bf16[2,96,1024]{2,1,0:T(8,128)(2,1)S(1)}, u32[]{:S(2)}, u32[]{:S(2)}) collective-permute-start(bf16[2,96,1024]{2,1,0:T(8,128)(2,1)} %get-tuple-element.51), channel_id=1, source_target_pairs={{0,48},{16,0},{32,16},{48,32},{1,49},{17,1},{33,17},{49,33},{2,50}... | collective-permute-start | bytes 1179656 | tf_op jit(solution)/shard_map/ppermute | solution.py:480
  100.7 6.2 %collective-permute-done.8.refs_4_ = bf16[2,96,1024]{2,1,0:T(8,128)(2,1)S(1)} collective-permute-done((bf16[2,96,1024]{2,1,0:T(8,128)(2,1)}, bf16[2,96,1024]{2,1,0:T(8,128)(2,1)S(1)}, u32[]{:S(2)}, u32[]{:S(2)}) %collective-permute-start.8) | collective-permute-done | bytes 393248 | tf_op jit(solution)/shard_map/ppermute | solution.py:480
  107.0 2.3 %collective-permute-done.9.refs_5_ = bf16[2,96,1024]{2,1,0:T(8,128)(2,1)S(1)} collective-permute-done((bf16[2,96,1024]{2,1,0:T(8,128)(2,1)}, bf16[2,96,1024]{2,1,0:T(8,128)(2,1)S(1)}, u32[]{:S(2)}, u32[]{:S(2)}) %collective-permute-start.9) | collective-permute-done | bytes 393248 | tf_op jit(solution)/shard_map/ppermute | solution.py:480
  109.3 0.4 collective-permute-done.10.refs_6_
  109.6 0.0 collective-permute-done.11.refs_7_
  109.7 0.0 collective-permute-done.12.refs_9_
  109.7 1.9 %fold.1 = (bf16[4,96,1024]{2,1,0:T(8,128)(2,1)S(1)}, bf16[4,96,1024]{2,1,0:T(8,128)(2,1)S(1)}, bf16[4,96,1024]{2,1,0:T(8,128)(2,1)S(1)}, bf16[4,96,1024]{2,1,0:T(8,128)(2,1)S(1)}, bf16[8,136,1024]{2,1,0:T(8,128)(2,1)}) custom-call(bf16[4,96,1024]{2,1,0:T(8,128)(2,1)S(1)} %get-tuple-element.44.refs_0_, bf16[4,96,1024]{2,1,0:T(8,128)(2,1)S(1)} %get-tuple-element.45.refs_1_, ...), custom_call_target="tpu_custom_call" | custom-call | bytes 1024 | tf_op jit(solution)/shard_map/fold/pallas_call | solution.py:45
  111.6 0.9 copy-done.3
  112.5 0.9 copy-done.4
  113.4 0.0 reduce-scatter.2.cloned.1.call-update
  113.4 2.7 %collective-permute-start.13 = (bf16[4,96,1024]{2,1,0:T(8,128)(2,1)}, bf16[4,96,1024]{2,1,0:T(8,128)(2,1)S(1)}, u32[]{:S(2)}, u32[]{:S(2)}) collective-permute-start(bf16[4,96,1024]{2,1,0:T(8,128)(2,1)} %copy-done.4), channel_id=1, source_target_pairs={{0,64},{64,128},{128,192},{192,0},{1,65},{65,129},{129,193},{193,1... | collective-permute-start | bytes 2359304 | tf_op jit(solution)/shard_map/ppermute | solution.py:480
  116.1 0.0 collective-permute-start.14
  116.1 1.1 collective-permute-start.15
  117.1 2.2 %collective-permute-start.16 = (bf16[4,96,1024]{2,1,0:T(8,128)(2,1)S(1)}, bf16[4,96,1024]{2,1,0:T(8,128)(2,1)S(1)}, u32[]{:S(2)}, u32[]{:S(2)}) collective-permute-start(bf16[4,96,1024]{2,1,0:T(8,128)(2,1)S(1)} %get-tuple-element.58), channel_id=1, source_target_pairs={{0,48},{16,0},{32,16},{48,32},{1,49},{17,1},{33,17},{49,33},{2,50}... | collective-permute-start | bytes 2359304 | tf_op jit(solution)/shard_map/ppermute | solution.py:480
  119.3 13.0 %collective-permute-done.13.refs_1_ = bf16[4,96,1024]{2,1,0:T(8,128)(2,1)S(1)} collective-permute-done((bf16[4,96,1024]{2,1,0:T(8,128)(2,1)}, bf16[4,96,1024]{2,1,0:T(8,128)(2,1)S(1)}, u32[]{:S(2)}, u32[]{:S(2)}) %collective-permute-start.13) | collective-permute-done | bytes 786464 | tf_op jit(solution)/shard_map/ppermute | solution.py:480
  132.3 3.3 %collective-permute-done.14.refs_2_ = bf16[4,96,1024]{2,1,0:T(8,128)(2,1)S(1)} collective-permute-done((bf16[4,96,1024]{2,1,0:T(8,128)(2,1)}, bf16[4,96,1024]{2,1,0:T(8,128)(2,1)S(1)}, u32[]{:S(2)}, u32[]{:S(2)}) %collective-permute-start.14) | collective-permute-done | bytes 786464 | tf_op jit(solution)/shard_map/ppermute | solution.py:480
  135.7 0.0 collective-permute-done.16.refs_5_
  135.7 0.6 total.1
  136.2 1.1 collective-permute-start.17
  137.4 3.1 %collective-permute-start.18 = (bf16[96,1024]{1,0:T(8,128)(2,1)S(1)}, bf16[96,1024]{1,0:T(8,128)(2,1)S(1)}, u32[]{:S(2)}, u32[]{:S(2)}) collective-permute-start(bf16[96,1024]{1,0:T(8,128)(2,1)S(1)} %get-tuple-element.61), channel_id=1, source_target_pairs={{0,32},{16,48},{32,0},{48,16},{1,33},{17,49},{33,1},{49,17},{2,34}... | collective-permute-start | bytes 589832 | tf_op jit(solution)/shard_map/ppermute | solution.py:486
  140.5 1.0 collective-permute-start.19
  141.5 2.8 %collective-permute-start.20 = (bf16[96,1024]{1,0:T(8,128)(2,1)S(1)}, bf16[96,1024]{1,0:T(8,128)(2,1)S(1)}, u32[]{:S(2)}, u32[]{:S(2)}) collective-permute-start(bf16[96,1024]{1,0:T(8,128)(2,1)S(1)} %get-tuple-element.64), channel_id=1, source_target_pairs={{0,64},{64,128},{128,192},{192,0},{1,65},{65,129},{129,193},{193,1... | collective-permute-start | bytes 589832 | tf_op jit(solution)/shard_map/ppermute | solution.py:480
  144.3 0.0 collective-permute-start.21
  144.3 0.7 collective-permute-done.17.refs_1_
  145.0 0.1 collective-permute-start.22
  145.1 2.0 %collective-permute-done.18.refs_2_ = bf16[96,1024]{1,0:T(8,128)(2,1)S(1)} collective-permute-done((bf16[96,1024]{1,0:T(8,128)(2,1)S(1)}, bf16[96,1024]{1,0:T(8,128)(2,1)S(1)}, u32[]{:S(2)}, u32[]{:S(2)}) %collective-permute-start.18) | collective-permute-done | bytes 196640 | tf_op jit(solution)/shard_map/ppermute | solution.py:486
  147.1 2.5 %collective-permute-done.20.refs_5_ = bf16[96,1024]{1,0:T(8,128)(2,1)S(1)} collective-permute-done((bf16[96,1024]{1,0:T(8,128)(2,1)S(1)}, bf16[96,1024]{1,0:T(8,128)(2,1)S(1)}, u32[]{:S(2)}, u32[]{:S(2)}) %collective-permute-start.20) | collective-permute-done | bytes 196640 | tf_op jit(solution)/shard_map/ppermute | solution.py:480
  149.6 1.9 %collective-permute-done.21.refs_6_ = bf16[96,1024]{1,0:T(8,128)(2,1)S(1)} collective-permute-done((bf16[96,1024]{1,0:T(8,128)(2,1)S(1)}, bf16[96,1024]{1,0:T(8,128)(2,1)S(1)}, u32[]{:S(2)}, u32[]{:S(2)}) %collective-permute-start.21) | collective-permute-done | bytes 196640 | tf_op jit(solution)/shard_map/ppermute | solution.py:486
  151.6 2.0 %collective-permute-done.22.refs_7_ = bf16[96,1024]{1,0:T(8,128)(2,1)S(1)} collective-permute-done((bf16[96,1024]{1,0:T(8,128)(2,1)S(1)}, bf16[96,1024]{1,0:T(8,128)(2,1)S(1)}, u32[]{:S(2)}, u32[]{:S(2)}) %collective-permute-start.22) | collective-permute-done | bytes 196640 | tf_op jit(solution)/shard_map/ppermute | solution.py:480
  153.6 4.9 %reduce-scatter.2.cloned.1.call-done.refs_8_ = bf16[136,1024]{1,0:T(8,128)(2,1)} async-done(((bf16[1088,1024]{1,0:T(8,128)(2,1)}), bf16[136,1024]{1,0:T(8,128)(2,1)}) %reduce-scatter.2.cloned.1.call-update) | async-done | bytes 278544 | tf_op jit(solution)/shard_map/reduce_scatter | solution.py:512
  158.5 1.0 copy-done.2
  159.4 1.1 finish.1
  (29 shorter events, 0.2 us)
Async XLA Ops:
  7.2 64.4 %all-gather.3.cloned.1.call-start = ((), (), s32[]{:S(2)}) async-start(), calls=%async_computation.4 | async-start | bytes 9191424 | tf_op jit(solution)/shard_map/all_gather | solution.py:496
  26.5 34.2 %copy-start.5 = (bf16[4,96,1024]{2,1,0:T(8,128)(2,1)}, bf16[4,96,1024]{2,1,0:T(8,128)(2,1)S(1)}, u32[]{:S(2)}) copy-start(bf16[4,96,1024]{2,1,0:T(8,128)(2,1)S(1)} %all_to_all.10.refs_5_) | copy-start | bytes 2359300
  26.5 18.0 %all-to-all-start = ((bf16[4,96,1024]{2,1,0:T(8,128)(2,1)}), bf16[4,96,1024]{2,1,0:T(8,128)(2,1)S(1)}, u32[]{:S(2)}, u32[]{:S(2)}) async-start(bf16[4,96,1024]{2,1,0:T(8,128)(2,1)} %get-tuple-element.41), calls=%async_computation | async-start | bytes 1572864 | tf_op jit(solution)/shard_map/all_to_all | solution.py:476
  30.8 127.7 %reduce-scatter.2.cloned.1.call-start = ((), (), s32[]{:S(2)}) async-start(), calls=%async_computation.3 | async-start | bytes 2506752 | tf_op jit(solution)/shard_map/reduce_scatter | solution.py:512
  30.8 26.4 %collective-permute-start.5 = (bf16[4,96,1024]{2,1,0:T(8,128)(2,1)S(1)}, bf16[4,96,1024]{2,1,0:T(8,128)(2,1)S(1)}, u32[]{:S(2)}, u32[]{:S(2)}) collective-permute-start(bf16[4,96,1024]{2,1,0:T(8,128)(2,1)S(1)} %all_to_all.10.refs_5_), channel_id=1, source_target_pairs={{0,48},{16,0},{32,16},{48,32},{1,49},{17,1},{33,17},{49,33},{2,50}... | collective-permute-start | bytes 2359304 | tf_op jit(solution)/shard_map/ppermute | solution.py:469
  34.0 25.0 %collective-permute-start.4 = (bf16[4,96,1024]{2,1,0:T(8,128)(2,1)S(1)}, bf16[4,96,1024]{2,1,0:T(8,128)(2,1)S(1)}, u32[]{:S(2)}, u32[]{:S(2)}) collective-permute-start(bf16[4,96,1024]{2,1,0:T(8,128)(2,1)S(1)} %all_to_all.10.refs_5_), channel_id=1, source_target_pairs={{0,16},{16,32},{32,48},{48,0},{1,17},{17,33},{33,49},{49,1},{2,18}... | collective-permute-start | bytes 2359304 | tf_op jit(solution)/shard_map/ppermute | solution.py:468
  44.5 27.0 %copy-start.6 = (bf16[4,96,1024]{2,1,0:T(8,128)(2,1)}, bf16[4,96,1024]{2,1,0:T(8,128)(2,1)S(1)}, u32[]{:S(2)}) copy-start(bf16[4,96,1024]{2,1,0:T(8,128)(2,1)S(1)} %all-to-all-done.refs_0_) | copy-start | bytes 2359300
  44.5 15.2 %collective-permute-start.1 = (bf16[4,96,1024]{2,1,0:T(8,128)(2,1)S(1)}, bf16[4,96,1024]{2,1,0:T(8,128)(2,1)S(1)}, u32[]{:S(2)}, u32[]{:S(2)}) collective-permute-start(bf16[4,96,1024]{2,1,0:T(8,128)(2,1)S(1)} %all-to-all-done.refs_0_), channel_id=1, source_target_pairs={{0,192},{64,0},{128,64},{192,128},{1,193},{65,1},{129,65},{193,129... | collective-permute-start | bytes 2359304 | tf_op jit(solution)/shard_map/ppermute | solution.py:469
  44.8 15.9 %collective-permute-start = (bf16[4,96,1024]{2,1,0:T(8,128)(2,1)S(1)}, bf16[4,96,1024]{2,1,0:T(8,128)(2,1)S(1)}, u32[]{:S(2)}, u32[]{:S(2)}) collective-permute-start(bf16[4,96,1024]{2,1,0:T(8,128)(2,1)S(1)} %all-to-all-done.refs_0_), channel_id=1, source_target_pairs={{0,64},{64,128},{128,192},{192,0},{1,65},{65,129},{129,193},{193,1... | collective-permute-start | bytes 2359304 | tf_op jit(solution)/shard_map/ppermute | solution.py:468
  57.2 14.3 %copy-start.7 = (bf16[4,96,1024]{2,1,0:T(8,128)(2,1)}, bf16[4,96,1024]{2,1,0:T(8,128)(2,1)S(1)}, u32[]{:S(2)}) copy-start(bf16[4,96,1024]{2,1,0:T(8,128)(2,1)S(1)} %collective-permute-done.5.refs_7_) | copy-start | bytes 2359300
  57.3 8.6 %collective-permute-start.7 = (bf16[2,96,1024]{2,1,0:T(8,128)(2,1)S(1)}, bf16[2,96,1024]{2,1,0:T(8,128)(2,1)S(1)}, u32[]{:S(2)}, u32[]{:S(2)}) collective-permute-start(bf16[2,96,1024]{2,1,0:T(8,128)(2,1)S(1)} %slice.19), channel_id=1, source_target_pairs={{0,48},{16,0},{32,16},{48,32},{1,49},{17,1},{33,17},{49,33},{2,50}... | collective-permute-start | bytes 1179656 | tf_op jit(solution)/shard_map/ppermute | solution.py:471
  59.0 12.5 %copy-start.8 = (bf16[4,96,1024]{2,1,0:T(8,128)(2,1)}, bf16[4,96,1024]{2,1,0:T(8,128)(2,1)S(1)}, u32[]{:S(2)}) copy-start(bf16[4,96,1024]{2,1,0:T(8,128)(2,1)S(1)} %collective-permute-done.4.refs_6_) | copy-start | bytes 2359300
  59.1 10.3 %collective-permute-start.6 = (bf16[2,96,1024]{2,1,0:T(8,128)(2,1)S(1)}, bf16[2,96,1024]{2,1,0:T(8,128)(2,1)S(1)}, u32[]{:S(2)}, u32[]{:S(2)}) collective-permute-start(bf16[2,96,1024]{2,1,0:T(8,128)(2,1)S(1)} %slice.18), channel_id=1, source_target_pairs={{0,16},{16,32},{32,48},{48,0},{1,17},{17,33},{33,49},{49,1},{2,18}... | collective-permute-start | bytes 1179656 | tf_op jit(solution)/shard_map/ppermute | solution.py:470
  59.7 0.9 copy-start.9
  59.8 9.7 %collective-permute-start.3 = (bf16[2,96,1024]{2,1,0:T(8,128)(2,1)S(1)}, bf16[2,96,1024]{2,1,0:T(8,128)(2,1)S(1)}, u32[]{:S(2)}, u32[]{:S(2)}) collective-permute-start(bf16[2,96,1024]{2,1,0:T(8,128)(2,1)S(1)} %slice.17), channel_id=1, source_target_pairs={{0,192},{64,0},{128,64},{192,128},{1,193},{65,1},{129,65},{193,129... | collective-permute-start | bytes 1179656 | tf_op jit(solution)/shard_map/ppermute | solution.py:471
  60.6 8.9 %copy-start.10 = (bf16[4,96,1024]{2,1,0:T(8,128)(2,1)}, bf16[4,96,1024]{2,1,0:T(8,128)(2,1)S(1)}, u32[]{:S(2)}) copy-start(bf16[4,96,1024]{2,1,0:T(8,128)(2,1)S(1)} %collective-permute-done.refs_1_) | copy-start | bytes 2359300
  60.7 10.2 %collective-permute-start.2 = (bf16[2,96,1024]{2,1,0:T(8,128)(2,1)S(1)}, bf16[2,96,1024]{2,1,0:T(8,128)(2,1)}, u32[]{:S(2)}, u32[]{:S(2)}) collective-permute-start(bf16[2,96,1024]{2,1,0:T(8,128)(2,1)S(1)} %slice.16), channel_id=1, source_target_pairs={{0,64},{64,128},{128,192},{192,0},{1,65},{65,129},{129,193},{193,1... | collective-permute-start | bytes 1179656 | tf_op jit(solution)/shard_map/ppermute | solution.py:470
  65.9 5.7 %copy-start.11 = (bf16[2,96,1024]{2,1,0:T(8,128)(2,1)}, bf16[2,96,1024]{2,1,0:T(8,128)(2,1)S(1)}, u32[]{:S(2)}) copy-start(bf16[2,96,1024]{2,1,0:T(8,128)(2,1)S(1)} %collective-permute-done.7.refs_9_) | copy-start | bytes 1179652
  69.4 0.8 copy-start.12
  70.1 0.7 copy-start.13
  95.1 14.5 %collective-permute-start.12 = (bf16[8,136,1024]{2,1,0:T(8,128)(2,1)}, bf16[8,136,1024]{2,1,0:T(8,128)(2,1)S(1)}, u32[]{:S(2)}, u32[]{:S(2)}) collective-permute-start(bf16[8,136,1024]{2,1,0:T(8,128)(2,1)} %get-tuple-element.53), channel_id=1, source_target_pairs={{0,1},{1,0},{2,3},{3,2},{4,5},{5,4},{6,7},{7,6},{8,9},{9,8},{10,11... | collective-permute-start | bytes 6684680 | tf_op jit(solution)/shard_map/ppermute | solution.py:504
  95.5 11.5 %collective-permute-start.8 = (bf16[2,96,1024]{2,1,0:T(8,128)(2,1)}, bf16[2,96,1024]{2,1,0:T(8,128)(2,1)S(1)}, u32[]{:S(2)}, u32[]{:S(2)}) collective-permute-start(bf16[2,96,1024]{2,1,0:T(8,128)(2,1)} %get-tuple-element.48), channel_id=1, source_target_pairs={{0,64},{64,128},{128,192},{192,0},{1,65},{65,129},{129,193},{193,1... | collective-permute-start | bytes 1179656 | tf_op jit(solution)/shard_map/ppermute | solution.py:480
  96.7 12.6 %collective-permute-start.9 = (bf16[2,96,1024]{2,1,0:T(8,128)(2,1)}, bf16[2,96,1024]{2,1,0:T(8,128)(2,1)S(1)}, u32[]{:S(2)}, u32[]{:S(2)}) collective-permute-start(bf16[2,96,1024]{2,1,0:T(8,128)(2,1)} %get-tuple-element.49), channel_id=1, source_target_pairs={{0,192},{64,0},{128,64},{192,128},{1,193},{65,1},{129,65},{193,129... | collective-permute-start | bytes 1179656 | tf_op jit(solution)/shard_map/ppermute | solution.py:480
  97.5 12.1 %collective-permute-start.10 = (bf16[2,96,1024]{2,1,0:T(8,128)(2,1)}, bf16[2,96,1024]{2,1,0:T(8,128)(2,1)S(1)}, u32[]{:S(2)}, u32[]{:S(2)}) collective-permute-start(bf16[2,96,1024]{2,1,0:T(8,128)(2,1)} %get-tuple-element.50), channel_id=1, source_target_pairs={{0,16},{16,32},{32,48},{48,0},{1,17},{17,33},{33,49},{49,1},{2,18}... | collective-permute-start | bytes 1179656 | tf_op jit(solution)/shard_map/ppermute | solution.py:480
  99.0 10.7 %collective-permute-start.11 = (bf16[2,96,1024]{2,1,0:T(8,128)(2,1)}, bf16[2,96,1024]{2,1,0:T(8,128)(2,1)S(1)}, u32[]{:S(2)}, u32[]{:S(2)}) collective-permute-start(bf16[2,96,1024]{2,1,0:T(8,128)(2,1)} %get-tuple-element.51), channel_id=1, source_target_pairs={{0,48},{16,0},{32,16},{48,32},{1,49},{17,1},{33,17},{49,33},{2,50}... | collective-permute-start | bytes 1179656 | tf_op jit(solution)/shard_map/ppermute | solution.py:480
  111.6 0.9 copy-start.3
  112.5 0.9 copy-start.4
  113.4 22.3 %copy-start = (bf16[4,96,1024]{2,1,0:T(8,128)(2,1)S(1)}, bf16[4,96,1024]{2,1,0:T(8,128)(2,1)}, u32[]{:S(2)}) copy-start(bf16[4,96,1024]{2,1,0:T(8,128)(2,1)} %get-tuple-element.43.refs_0_) | copy-start | bytes 2359300
  113.4 22.3 %copy-start.1 = (bf16[4,96,1024]{2,1,0:T(8,128)(2,1)S(1)}, bf16[4,96,1024]{2,1,0:T(8,128)(2,1)}, u32[]{:S(2)}) copy-start(bf16[4,96,1024]{2,1,0:T(8,128)(2,1)} %get-tuple-element.56.refs_3_) | copy-start | bytes 2359300
  113.4 19.0 %collective-permute-start.13 = (bf16[4,96,1024]{2,1,0:T(8,128)(2,1)}, bf16[4,96,1024]{2,1,0:T(8,128)(2,1)S(1)}, u32[]{:S(2)}, u32[]{:S(2)}) collective-permute-start(bf16[4,96,1024]{2,1,0:T(8,128)(2,1)} %copy-done.4), channel_id=1, source_target_pairs={{0,64},{64,128},{128,192},{192,0},{1,65},{65,129},{129,193},{193,1... | collective-permute-start | bytes 2359304 | tf_op jit(solution)/shard_map/ppermute | solution.py:480
  116.1 19.6 %collective-permute-start.14 = (bf16[4,96,1024]{2,1,0:T(8,128)(2,1)}, bf16[4,96,1024]{2,1,0:T(8,128)(2,1)S(1)}, u32[]{:S(2)}, u32[]{:S(2)}) collective-permute-start(bf16[4,96,1024]{2,1,0:T(8,128)(2,1)} %copy-done.3), channel_id=1, source_target_pairs={{0,192},{64,0},{128,64},{192,128},{1,193},{65,1},{129,65},{193,129... | collective-permute-start | bytes 2359304 | tf_op jit(solution)/shard_map/ppermute | solution.py:480
  116.1 19.6 %collective-permute-start.15 = (bf16[4,96,1024]{2,1,0:T(8,128)(2,1)S(1)}, bf16[4,96,1024]{2,1,0:T(8,128)(2,1)S(1)}, u32[]{:S(2)}, u32[]{:S(2)}) collective-permute-start(bf16[4,96,1024]{2,1,0:T(8,128)(2,1)S(1)} %get-tuple-element.57), channel_id=1, source_target_pairs={{0,16},{16,32},{32,48},{48,0},{1,17},{17,33},{33,49},{49,1},{2,18}... | collective-permute-start | bytes 2359304 | tf_op jit(solution)/shard_map/ppermute | solution.py:480
  117.1 18.5 %collective-permute-start.16 = (bf16[4,96,1024]{2,1,0:T(8,128)(2,1)S(1)}, bf16[4,96,1024]{2,1,0:T(8,128)(2,1)S(1)}, u32[]{:S(2)}, u32[]{:S(2)}) collective-permute-start(bf16[4,96,1024]{2,1,0:T(8,128)(2,1)S(1)} %get-tuple-element.58), channel_id=1, source_target_pairs={{0,48},{16,0},{32,16},{48,32},{1,49},{17,1},{33,17},{49,33},{2,50}... | collective-permute-start | bytes 2359304 | tf_op jit(solution)/shard_map/ppermute | solution.py:480
  136.2 8.8 %collective-permute-start.17 = (bf16[96,1024]{1,0:T(8,128)(2,1)S(1)}, bf16[96,1024]{1,0:T(8,128)(2,1)S(1)}, u32[]{:S(2)}, u32[]{:S(2)}) collective-permute-start(bf16[96,1024]{1,0:T(8,128)(2,1)S(1)} %get-tuple-element.60), channel_id=1, source_target_pairs={{0,16},{16,32},{32,48},{48,0},{1,17},{17,33},{33,49},{49,1},{2,18}... | collective-permute-start | bytes 589832 | tf_op jit(solution)/shard_map/ppermute | solution.py:480
  137.4 9.8 %collective-permute-start.18 = (bf16[96,1024]{1,0:T(8,128)(2,1)S(1)}, bf16[96,1024]{1,0:T(8,128)(2,1)S(1)}, u32[]{:S(2)}, u32[]{:S(2)}) collective-permute-start(bf16[96,1024]{1,0:T(8,128)(2,1)S(1)} %get-tuple-element.61), channel_id=1, source_target_pairs={{0,32},{16,48},{32,0},{48,16},{1,33},{17,49},{33,1},{49,17},{2,34}... | collective-permute-start | bytes 589832 | tf_op jit(solution)/shard_map/ppermute | solution.py:486
  140.5 6.6 %collective-permute-start.19 = (bf16[96,1024]{1,0:T(8,128)(2,1)S(1)}, bf16[96,1024]{1,0:T(8,128)(2,1)S(1)}, u32[]{:S(2)}, u32[]{:S(2)}) collective-permute-start(bf16[96,1024]{1,0:T(8,128)(2,1)S(1)} %get-tuple-element.62), channel_id=1, source_target_pairs={{0,48},{16,0},{32,16},{48,32},{1,49},{17,1},{33,17},{49,33},{2,50}... | collective-permute-start | bytes 589832 | tf_op jit(solution)/shard_map/ppermute | solution.py:480
  141.5 8.1 %collective-permute-start.20 = (bf16[96,1024]{1,0:T(8,128)(2,1)S(1)}, bf16[96,1024]{1,0:T(8,128)(2,1)S(1)}, u32[]{:S(2)}, u32[]{:S(2)}) collective-permute-start(bf16[96,1024]{1,0:T(8,128)(2,1)S(1)} %get-tuple-element.64), channel_id=1, source_target_pairs={{0,64},{64,128},{128,192},{192,0},{1,65},{65,129},{129,193},{193,1... | collective-permute-start | bytes 589832 | tf_op jit(solution)/shard_map/ppermute | solution.py:480
  144.3 7.3 %collective-permute-start.21 = (bf16[96,1024]{1,0:T(8,128)(2,1)S(1)}, bf16[96,1024]{1,0:T(8,128)(2,1)S(1)}, u32[]{:S(2)}, u32[]{:S(2)}) collective-permute-start(bf16[96,1024]{1,0:T(8,128)(2,1)S(1)} %get-tuple-element.65), channel_id=1, source_target_pairs={{0,128},{64,192},{128,0},{192,64},{1,129},{65,193},{129,1},{193,65... | collective-permute-start | bytes 589832 | tf_op jit(solution)/shard_map/ppermute | solution.py:486
  145.0 8.5 %collective-permute-start.22 = (bf16[96,1024]{1,0:T(8,128)(2,1)S(1)}, bf16[96,1024]{1,0:T(8,128)(2,1)S(1)}, u32[]{:S(2)}, u32[]{:S(2)}) collective-permute-start(bf16[96,1024]{1,0:T(8,128)(2,1)S(1)} %get-tuple-element.66), channel_id=1, source_target_pairs={{0,192},{64,0},{128,64},{192,128},{1,193},{65,1},{129,65},{193,129... | collective-permute-start | bytes 589832 | tf_op jit(solution)/shard_map/ppermute | solution.py:480
  158.5 1.0 copy-start.2
Sparse Core Ops, SparseCore 0:
  11.7 59.8 all-gather.2
  113.5 44.9 reduce-scatter.1
where the time goes:
time: 168 us; the launch traced here: 167 us
  waiting for transfers between devices  66.4 us (40%)
  starting transfers between devices  35.4 us (21%)
  Pallas kernels  30.8 us (18%)
  blocking collectives  14.9 us (9%)
  between operations  14.2 us (8%)
  local copies, waits for them, and re-layouts  4.96 us (3%)
    pallas_call x5, Pallas kernels, call(): pl.pallas_call(kernel, name=name, in_specs=[smem] * scalars + (specs or [...  30.8 us
    ppermute x12, waiting for transfers between devices, swap(): return (lax.ppermute(a, axis, UP), lax.ppermute(b, axis, DOWN))  30.5 us
    ppermute x12, starting transfers between devices, swap(): return (lax.ppermute(a, axis, UP), lax.ppermute(b, axis, DOWN))  16.2 us
    all_to_all x1, blocking collectives, gather_weights(): lax.all_to_all(own, inner, split_axis=0, concat_axis=0, tiled=True)  14.9 us
    all_to_all x1, waiting for transfers between devices, gather_weights(): lax.all_to_all(own, inner, split_axis=0, concat_axis=0, tiled=True)  10.5 us
    ppermute x2, waiting for transfers between devices, gather_ring(): above = lax.ppermute(block, axis, DOWN)  9.7 us
    reduce_scatter x1, waiting for transfers between devices, body(): lax.psum_scatter(pair.reshape(CHIPS * (TOK + TOP), WIDTH), 'z', scatter_d...  4.92 us
    unnamed x28, local copies, waits for them, and re-layouts  4.86 us
  transfers between devices with their start and end apart: 26, of which 18 were waited for; matrix products, arithmetic and copies ran while one was open for 0% of the time, Pallas kernels for 0%

commit v1 on v0

--- a/solution.py
+++ b/solution.py
@@ -68,60 +68,79 @@
 VM = pl.BlockSpec(memory_space=pltpu.VMEM)
 
 
-def pack_kernel(tok, cot, ids, probs, gu, dn, pay, own0, own1, buf, meta, wbuf, sem):
+def pack_kernel(tok, cot, ids, probs, pay, buf, meta, sem):
     halves = [
         pltpu.make_async_copy(tok, buf.at[0], sem.at[0]),
         pltpu.make_async_copy(cot, buf.at[1], sem.at[1]),
     ]
-    weights = [
-        pltpu.make_async_copy(gu, wbuf.at[:, pl.ds(0, ROWS_IN)], sem.at[2]),
-        pltpu.make_async_copy(dn, wbuf.at[:, pl.ds(ROWS_IN, ROWS_OUT)], sem.at[3]),
-    ]
-    for copy in halves + weights:
+    for copy in halves:
         copy.start()
     meta[...] = jnp.zeros_like(meta)
     meta[:, 0:TOK] = ids[...].astype(F32).astype(BF16)
     meta[:, TOK : 2 * TOK] = probs[...]
-    out = [pltpu.make_async_copy(meta, pay.at[pl.ds(2 * TOK, TOP)], sem.at[4])]
+    out = [pltpu.make_async_copy(meta, pay.at[pl.ds(2 * TOK, TOP)], sem.at[2])]
     out[0].start()
     for i in range(2):
         halves[i].wait()
-        out.append(pltpu.make_async_copy(buf.at[i], pay.at[pl.ds(i * TOK, TOK)], sem.at[5 + i]))
+        out.append(pltpu.make_async_copy(buf.at[i], pay.at[pl.ds(i * TOK, TOK)], sem.at[3 + i]))
         out[-1].start()
-    for copy in weights:
-        copy.wait()
-    for i in range(4):
-        own0[i] = wbuf[0]
-        own1[i] = wbuf[1]
     for copy in out:
         copy.wait()
 
 
-def pack(tokens, cotangent, ids, probs, gate_up, down_proj):
+def pack(tokens, cotangent, ids, probs):
     return call(
         pack_kernel,
         "pack",
-        [shape(2 * TOK + TOP, WIDTH), shape(4, ROWS, WIDTH), shape(4, ROWS, WIDTH)],
+        shape(2 * TOK + TOP, WIDTH),
         tokens,
         cotangent,
         ids,
         probs,
-        gate_up,
-        down_proj,
-        specs=[HBM, HBM, VM, VM, HBM, HBM],
-        out_specs=[HBM, VM, VM],
+        specs=[HBM, HBM, VM, VM],
+        out_specs=HBM,
         limit=60,
         scratch=[
             pltpu.VMEM((2, TOK, WIDTH), BF16),
             pltpu.VMEM((TOP, WIDTH), BF16),
-            pltpu.VMEM((2, ROWS, WIDTH), BF16),
-            pltpu.SemaphoreType.DMA((7,)),
+            pltpu.SemaphoreType.DMA((5,)),
         ],
         cost=cost(0, 2_000_000),
     )
 
 
-PIECES = ((4, ROWS, WIDTH),) * 3 + ((2, ROWS, WIDTH),) * 2
+def rows_kernel(gu, dn, own0, own1):
+    for e, own in enumerate((own0, own1)):
+        own[0:ROWS_IN] = gu[e]
+        own[ROWS_IN:ROWS] = dn[e]
+
+
+def own_rows(gate_up, down_proj):
+    return call(
+        rows_kernel, "own_rows", [shape(ROWS, WIDTH)] * 2, gate_up, down_proj, cost=cost(0, 800_000)
+    )
+
+
+def place_kernel(index, me_ref, own, below, across, above, out):
+    for j, block in enumerate((own, below, across, above)):
+        out[lax.rem(me_ref[index] + 4 - j, 4)] = block[...]
+
+
+def place(index, where, own, below, across, above):
+    return call(
+        functools.partial(place_kernel, index),
+        "place",
+        shape(4, ROWS, WIDTH),
+        where,
+        own,
+        below,
+        across,
+        above,
+        scalars=1,
+        cost=cost(0, 1_600_000),
+    )
+
+
 TILE = 256
 START_AT = 2
 
@@ -159,11 +178,11 @@
         pick = jnp.concatenate(halves, axis=1)
         prob = jnp.concatenate([weights[2 * e], weights[2 * e + 1]], axis=1)
         column = jnp.sum(pick * prob, axis=1, keepdims=True)
-        gate_ref[e, PAIR * p : PAIR * (p + 1)] = jnp.broadcast_to(column, (PAIR, TOK))
+        gate_ref[e, pl.ds(pl.multiple_of(PAIR * p, PAIR), PAIR)] = jnp.broadcast_to(column, (PAIR, TOK))
         picks.append(pick)
     sel = jnp.concatenate(picks, axis=0).astype(BF16)
     sel_ref[p] = sel
-    rows = pl.ds(PAIR * p, PAIR)
+    rows = pl.ds(pl.multiple_of(PAIR * p, PAIR), PAIR)
     for lo, out in ((0, x_ref), (TOK, dy_ref)):
         both = jnp.concatenate([pay[2 * p, lo : lo + TOK], pay[2 * p + 1, lo : lo + TOK]], axis=0)
         routed = dot(sel, both, NN).astype(BF16)
@@ -251,7 +270,7 @@
 
 def combine_pair(p, first, pay, sel_ref, dx, sg, part):
     sel = sel_ref[p]
-    at = pl.ds(PAIR * p, PAIR)
+    at = pl.ds(pl.multiple_of(PAIR * p, PAIR), PAIR)
     rows = jnp.concatenate([dx[0, at], dx[1, at]], axis=0)
     back = dot(sel, rows, TN).astype(BF16)
     sums = jnp.concatenate([sg[0, at, 0:1], sg[1, at, 0:1]], axis=0)
@@ -294,12 +313,20 @@
         < lax.broadcasted_iota(jnp.int32, (TOK, TOK), 1)
     ).astype(BF16)
     slot = lax.broadcasted_iota(jnp.int32, (PAIR, TOK), 0).astype(F32)
-    for p in range(CHIPS):
-        loads[p].wait()
-        if p == START_AT:
+
+    def pair_in(p, _):
+        both = pl.ds(2 * p, 2)
+        pltpu.make_async_copy(pay_hbm.at[both], pay.at[both], psem.at[p]).wait()
+
+        @pl.when(p == START_AT)
+        def _():
             for copy in weights[0]:
                 copy.start()
+
         route_pair(p, first, pay, x, dy, gate, sel, upper, slot)
+        return 0
+
+    lax.fori_loop(0, CHIPS, pair_in, 0)
 
     def one(e, _):
         for n in range(10):
@@ -329,13 +356,20 @@
         return 0
 
     lax.fori_loop(0, 2, one, 0)
-    outs = []
-    for p in range(CHIPS):
+    def sends(p):
+        return [
+            pltpu.make_async_copy(part.at[p, core], keep.at[p], csem.at[p, 0]),
+            pltpu.make_async_copy(part.at[p, 1 - core], send.at[p], csem.at[p, 1]),
+        ]
+
+    def pair_out(p, _):
         combine_pair(p, first, pay, sel, dx, sg, part.at[p])
-        for i, (c, out) in enumerate(((core, keep), (1 - core, send))):
-            copy = pltpu.make_async_copy(part.at[p, c], out.at[p], csem.at[2 * p + i])
+        for copy in sends(p):
             copy.start()
-            outs.append(copy)
+        return 0
+
+    lax.fori_loop(0, CHIPS, pair_out, 0)
+    outs = [copy for p in range(CHIPS) for copy in sends(p)]
     for e in range(2):
         outs += stores_of(held.at[e], grads[e], gsem.at[e])
     for copy in outs:
@@ -343,11 +377,10 @@
 
 
 def experts(where, pay, pieces0, pieces1):
-    near = pltpu.VMEM((4, ROWS, WIDTH), BF16)
     return call(
         experts_kernel,
         "experts",
-        [shape(4, ROWS, WIDTH), near, near, *[shape(2, ROWS, WIDTH)] * 2] * 2
+        [*[shape(4, ROWS, WIDTH)] * 3, *[shape(2, ROWS, WIDTH)] * 2] * 2
         + [pltpu.VMEM((CHIPS, TOK + TOP, WIDTH), BF16), shape(CHIPS, TOK + TOP, WIDTH)],
         where,
         pay,
@@ -355,7 +388,7 @@
         *pieces1,
         scalars=1,
         specs=[HBM] + [HBM] * 10,
-        out_specs=[HBM, VM, VM, HBM, HBM] * 2 + [VM, HBM],
+        out_specs=[HBM] * 10 + [VM, HBM],
         scratch=[
             pltpu.VMEM((2 * CHIPS, 2 * TOK + TOP, WIDTH), BF16),
             pltpu.VMEM((2, SLOTS, WIDTH), BF16),
@@ -377,10 +410,10 @@
             pltpu.SemaphoreType.DMA((CHIPS,)),
             pltpu.SemaphoreType.DMA((2, 10)),
             pltpu.SemaphoreType.DMA((2, 5)),
-            pltpu.SemaphoreType.DMA((2 * CHIPS,)),
+            pltpu.SemaphoreType.DMA((CHIPS, 2)),
         ],
         cost=cost(4 * 640 * 1024 * 4096, 20_000_000),
-        limit=50,
+        limit=56,
     )
 
 
@@ -388,52 +421,63 @@
     return a.astype(F32) + b.astype(F32)
 
 
-def fold_kernel(*refs):
-    blocks, arrived, (keep, got) = refs[0:4], refs[4:8], refs[8:10]
-    outs, pair = refs[10:14], refs[14]
-    block_buf, pair_buf, sem = refs[15:]
-    pair_buf[...] = add(keep[...], got[...]).astype(BF16)
-    stores = [pltpu.make_async_copy(pair_buf, pair, sem.at[4])]
-    stores[0].start()
-    for i in range(4):
-        lo = 2 * (i % 2)
-        block_buf[i, lo : lo + 2] = add(blocks[i][lo : lo + 2], arrived[i][...]).astype(BF16)
-        block_buf[i, 2 - lo : 4 - lo] = blocks[i][2 - lo : 4 - lo]
-        stores.append(pltpu.make_async_copy(block_buf.at[i], outs[i], sem.at[i]))
+def fold_kernel(up, down, below, above, up_out, down_out, kept, got, sem):
+    moves = (up, below, up_out, pl.ds(0, 2)), (down, above, down_out, pl.ds(2, 2))
+    loads = []
+    for i, (block, arrived, _, half) in enumerate(moves):
+        loads.append(pltpu.make_async_copy(block.at[half], kept.at[i], sem.at[i]))
+        loads.append(pltpu.make_async_copy(arrived, got.at[i], sem.at[2 + i]))
+    for copy in loads:
+        copy.start()
+    stores = []
+    for i, (_, _, out, half) in enumerate(moves):
+        loads[2 * i].wait()
+        loads[2 * i + 1].wait()
+        kept[i] = add(kept[i], got[i]).astype(BF16)
+        stores.append(pltpu.make_async_copy(kept.at[i], out.at[half], sem.at[4 + i]))
         stores[-1].start()
     for copy in stores:
         copy.wait()
 
 
-def fold(*parts):
+def fold(up, down, below, above):
     return call(
         fold_kernel,
         "fold",
-        [shape(4, ROWS, WIDTH)] * 4 + [shape(CHIPS, TOK + TOP, WIDTH)],
-        *parts,
-        out_specs=[HBM] * 5,
+        [shape(4, ROWS, WIDTH)] * 2,
+        up,
+        down,
+        below,
+        above,
+        specs=[HBM] * 4,
+        out_specs=[HBM] * 2,
         scratch=[
-            pltpu.VMEM((4, 4, ROWS, WIDTH), BF16),
-            pltpu.VMEM((CHIPS, TOK + TOP, WIDTH), BF16),
-            pltpu.SemaphoreType.DMA((5,)),
+            pltpu.VMEM((2, 2, ROWS, WIDTH), BF16),
+            pltpu.VMEM((2, 2, ROWS, WIDTH), BF16),
+            pltpu.SemaphoreType.DMA((6,)),
         ],
         cost=cost(0, 1024),
-        limit=16,
-    )
-
-
-def total_kernel(*refs):
-    for e in range(2):
-        own, below, above = refs[3 * e : 3 * e + 3]
-        outs = refs[6 + 4 * e : 10 + 4 * e]
-        for i in range(4):
-            value = add(own[i], below[i]) + above[i].astype(F32)
-            outs[i][...] = value if i == 0 else value.astype(BF16)
-
-
-def totals_of(*parts):
+        input_output_aliases={0: 0, 1: 1},
+    )
+
+
+def join_kernel(a, b, out):
+    out[...] = add(a[...], b[...]).astype(BF16)
+
+
+def join(a, b):
+    return call(join_kernel, "join", shape(*a.shape), a, b, cost=cost(0, 1024))
+
+
+def total_kernel(own, below, above, *outs):
+    for i in range(4):
+        value = add(own[i], below[i]) + above[i].astype(F32)
+        outs[i][...] = value if i == 0 else value.astype(BF16)
+
+
+def total_of(own, below, above):
     outs = [shape(ROWS, WIDTH, dtype=F32)] + [shape(ROWS, WIDTH)] * 3
-    return call(total_kernel, "total", outs * 2, *parts, cost=cost(0, 1024))
+    return call(total_kernel, "total", outs, own, below, above, cost=cost(0, 1024))
 
 
 def finish_kernel(*refs):
@@ -472,8 +516,10 @@
     return block, below, above, far_a, far_b
 
 
-def gather_weights(own, inner, outer):
-    return gather_ring(lax.all_to_all(own, inner, split_axis=0, concat_axis=0, tiled=True), outer)
+def gather_weights(own, index, where, inner, outer):
+    below, above = swap(own, own, inner)
+    across = lax.ppermute(own, inner, ACROSS)
+    return gather_ring(place(index, where, own, below, across, above), outer)
 
 
 def swap(a, b, axis):
@@ -492,10 +538,11 @@
     core = lax.axis_index("core").astype(jnp.int32)
     first = (2 * (2 * lax.axis_index("z") + core)).astype(jnp.int32)
     where, ids = lax.optimization_barrier((jnp.stack([first, core, iy, ix]), expert_ids.T))
-    pay, own0, own1 = pack(tokens, cotangent, ids, gate_probs.T, gate_up, down_proj)
+    pay = pack(tokens, cotangent, ids, gate_probs.T)
     pay = lax.all_gather(pay, ("z", "core"), axis=0, tiled=False)
-    pieces0 = gather_weights(own0, "x", "y")
-    pieces1 = gather_weights(own1, "y", "x")
+    own0, own1 = own_rows(gate_up, down_proj)
+    pieces0 = gather_weights(own0, 3, where, "x", "y")
+    pieces1 = gather_weights(own1, 2, where, "y", "x")
 
     out = experts(where, pay, pieces0, pieces1)
     mine0, up0, dn0, a0, b0 = out[:5]
@@ -504,17 +551,14 @@
     got = lax.ppermute(send, "core", [(0, 1), (1, 0)])
     below0, above0 = swap(a0, b0, "y")
     below1, above1 = swap(a1, b1, "x")
-    up0, dn0, up1, dn1, pair = fold(
-        up0, dn0, up1, dn1, below0, above0, below1, above1, keep, got
-    )
-    below0, above0 = swap(up0, dn0, "y")
-    below1, above1 = swap(up1, dn1, "x")
-    done = lax.psum_scatter(
-        pair.reshape(CHIPS * (TOK + TOP), WIDTH), "z", scatter_dimension=0, tiled=True
-    )
-    out = totals_of(mine0, below0, above0, mine1, below1, above1)
+    below0, above0 = swap(*fold(up0, dn0, below0, above0), "y")
+    below1, above1 = swap(*fold(up1, dn1, below1, above1), "x")
+    pair = join(keep, got).reshape(CHIPS * (TOK + TOP), WIDTH)
+    done = lax.psum_scatter(pair, "z", scatter_dimension=0, tiled=True)
+    out0 = total_of(mine0, below0, above0)
+    out1 = total_of(mine1, below1, above1)
     grad_tokens, grad_gates, grad_gate_up, grad_down = finish(
-        *spread(out[:4], "x"), *spread(out[4:], "y"), done
+        *spread(out0, "x"), *spread(out1, "y"), done
     )
     return grad_tokens, grad_gates.T, grad_gate_up, grad_down
 

time: 168 us -> 161 us (0.958)
  blocking collectives: 14.9 us -> 0 us
  waiting for transfers between devices: 66.4 us -> 71.1 us
  starting transfers between devices: 35.4 us -> 37.9 us
  Pallas kernels: 30.8 us -> 33.3 us
    all_to_all x1 -> x0, blocking collectives: 14.9 us -> none  [gather_weights(): lax.all_to_all(own, inner, split_axis=0, concat_axis=0, tiled=True)]
    all_to_all x1 -> x0, waiting for transfers between devices: 10.5 us -> none  [gather_weights(): lax.all_to_all(own, inner, split_axis=0, concat_axis=0, tiled=True)]
    ppermute x12 -> x16, waiting for transfers between devices: 30.5 us -> 39.9 us  [swap(): return (lax.ppermute(a, axis, UP), lax.ppermute(b, axis, DOWN))]
    all_gather x1, waiting for transfers between devices: 0.71 us -> 9.44 us  [body(): pay = lax.all_gather(pay, ('z', 'core'), axis=0, tiled=False)]
    reduce_scatter x1, waiting for transfers between devices: 4.92 us -> 0.01 us  [body(): done = lax.psum_scatter(pair, 'z', scatter_dimension=0, tiled=True)]
    ppermute x1, waiting for transfers between devices: 0.01 us -> 4.31 us  [body(): got = lax.ppermute(send, 'core', [(0, 1), (1, 0)])]
    all_to_all x1 -> x0, starting transfers between devices: 4.28 us -> none  [gather_weights(): lax.all_to_all(own, inner, split_axis=0, concat_axis=0, tiled=True)]
    ppermute x2, waiting for transfers between devices: 3.94 us -> 0.01 us  [spread(): return (kept, up, lax.ppermute(far, axis, ACROSS), down)]
  transfers between devices with their start and end apart: 26 -> 31, of which waited for: 18 -> 18; matrix products, arithmetic and copies ran while one was open for 0% -> 0% of each run, Pallas kernels for 0% -> 3%
where the time goes in v1:
time: 161 us; the launch traced here: 160 us
  waiting for transfers between devices  71.1 us (44%)
  starting transfers between devices  37.9 us (24%)
  Pallas kernels  33.3 us (21%)
  between operations  14.3 us (9%)
  local copies, waits for them, and re-layouts  3.76 us (2%)
    ppermute x16, waiting for transfers between devices, swap(): return (lax.ppermute(a, axis, UP), lax.ppermute(b, axis, DOWN))  39.9 us
    pallas_call x11, Pallas kernels, call(): pl.pallas_call(kernel, name=name, in_specs=[smem] * scalars + (specs or [...  33.3 us
    ppermute x16, starting transfers between devices, swap(): return (lax.ppermute(a, axis, UP), lax.ppermute(b, axis, DOWN))  19.2 us
    ppermute x2, waiting for transfers between devices, gather_ring(): above = lax.ppermute(block, axis, DOWN)  11.3 us
    all_gather x1, waiting for transfers between devices, body(): pay = lax.all_gather(pay, ('z', 'core'), axis=0, tiled=False)  9.44 us
    ppermute x2, waiting for transfers between devices, gather_ring(): far_a = lax.ppermute(below[:half], axis, UP)  4.43 us
    ppermute x1, waiting for transfers between devices, body(): got = lax.ppermute(send, 'core', [(0, 1), (1, 0)])  4.31 us
    unnamed x40, local copies, waits for them, and re-layouts  3.65 us
  transfers between devices with their start and end apart: 31, of which 18 were waited for; matrix products, arithmetic and copies ran while one was open for 0% of the time, Pallas kernels for 3%

profile of v1, /device:TPU:24, one launch (start us, length us, event | category | flops | bytes accessed | tf_op | source)
XLA Modules:
  0.0 160.4 jit_solution(3793943923927970015)
XLA Ops:
  7.2 0.0 all-gather.3.cloned.1.call-start
  7.2 0.1 pad_add_fusion.me_ref.where
  7.3 2.5 %pack.1 = bf16[264,1024]{1,0:T(8,128)(2,1)} custom-call(bf16[128,1024]{1,0:T(8,128)(2,1)} %tok.1, bf16[128,1024]{1,0:T(8,128)(2,1)} %cot.1, s32[8,128]{1,0:T(8,128)} %bitcast.9, bf16[8,128]{1,0:T(8,128)(2,1)} %bitcast.10), custom_call_target="tpu_custom_call" | custom-call | bytes 2000000 | tf_op jit(solution)/shard_map/pack/pallas_call | solution.py:45
  9.8 0.0 all-gather.3.cloned.1.call-update
  9.8 0.0 reduce-scatter.2.cloned.1.call-start
  9.9 0.9 copy-done.9
  10.8 0.9 copy-done.10
  11.8 0.8 collective-permute-start.9
  12.6 2.7 %collective-permute-start.8 = (bf16[96,1024]{1,0:T(8,128)(2,1)S(1)}, bf16[96,1024]{1,0:T(8,128)(2,1)S(1)}, u32[]{:S(2)}, u32[]{:S(2)}) collective-permute-start(bf16[96,1024]{1,0:T(8,128)(2,1)S(1)} %get-tuple-element.39.own), channel_id=1, source_target_pairs={{0,128},{64,192},{128,0},{192,64},{1,129},{65,193},{129,1},{193,65... | collective-permute-start | bytes 589832 | tf_op jit(solution)/shard_map/ppermute | solution.py:521
  15.3 0.4 collective-permute-start.7
  15.7 2.8 %collective-permute-start.2 = (bf16[96,1024]{1,0:T(8,128)(2,1)S(1)}, bf16[96,1024]{1,0:T(8,128)(2,1)S(1)}, u32[]{:S(2)}, u32[]{:S(2)}) collective-permute-start(bf16[96,1024]{1,0:T(8,128)(2,1)S(1)} %get-tuple-element.38.own), channel_id=1, source_target_pairs={{0,48},{16,0},{32,16},{48,32},{1,49},{17,1},{33,17},{49,33},{2,50}... | collective-permute-start | bytes 589832 | tf_op jit(solution)/shard_map/ppermute | solution.py:526
  18.5 0.8 collective-permute-start.1
  19.3 4.6 %collective-permute-done.9.above = bf16[96,1024]{1,0:T(8,128)(2,1)S(1)} collective-permute-done((bf16[96,1024]{1,0:T(8,128)(2,1)S(1)}, bf16[96,1024]{1,0:T(8,128)(2,1)S(1)}, u32[]{:S(2)}, u32[]{:S(2)}) %collective-permute-start.9) | collective-permute-done | bytes 196640 | tf_op jit(solution)/shard_map/ppermute | solution.py:526
  23.9 1.5 collective-permute-start
  25.4 0.6 place.3.refs_5_
  26.0 2.0 %collective-permute-start.11 = (bf16[4,96,1024]{2,1,0:T(8,128)(2,1)S(1)}, bf16[4,96,1024]{2,1,0:T(8,128)(2,1)S(1)}, u32[]{:S(2)}, u32[]{:S(2)}) collective-permute-start(bf16[4,96,1024]{2,1,0:T(8,128)(2,1)S(1)} %place.3.refs_5_), channel_id=1, source_target_pairs={{0,48},{16,0},{32,16},{48,32},{1,49},{17,1},{33,17},{49,33},{2,50}... | collective-permute-start | bytes 2359304 | tf_op jit(solution)/shard_map/ppermute | solution.py:513
  28.0 0.1 collective-permute-start.10
  28.1 3.7 %collective-permute-done.below = bf16[96,1024]{1,0:T(8,128)(2,1)S(1)} collective-permute-done((bf16[96,1024]{1,0:T(8,128)(2,1)S(1)}, bf16[96,1024]{1,0:T(8,128)(2,1)S(1)}, u32[]{:S(2)}, u32[]{:S(2)}) %collective-permute-start) | collective-permute-done | bytes 196640 | tf_op jit(solution)/shard_map/ppermute | solution.py:526
  31.8 0.6 place.2.refs_0_
  32.4 0.1 collective-permute-start.4
  32.5 3.2 %collective-permute-start.3 = (bf16[4,96,1024]{2,1,0:T(8,128)(2,1)S(1)}, bf16[4,96,1024]{2,1,0:T(8,128)(2,1)S(1)}, u32[]{:S(2)}, u32[]{:S(2)}) collective-permute-start(bf16[4,96,1024]{2,1,0:T(8,128)(2,1)S(1)} %place.2.refs_0_), channel_id=1, source_target_pairs={{0,64},{64,128},{128,192},{192,0},{1,65},{65,129},{129,193},{193,1... | collective-permute-start | bytes 2359304 | tf_op jit(solution)/shard_map/ppermute | solution.py:512
  35.7 8.5 %collective-permute-done.11.refs_7_ = bf16[4,96,1024]{2,1,0:T(8,128)(2,1)S(1)} collective-permute-done((bf16[4,96,1024]{2,1,0:T(8,128)(2,1)S(1)}, bf16[4,96,1024]{2,1,0:T(8,128)(2,1)S(1)}, u32[]{:S(2)}, u32[]{:S(2)}) %collective-permute-start.11) | collective-permute-done | bytes 786464 | tf_op jit(solution)/shard_map/ppermute | solution.py:513
  44.3 3.4 %collective-permute-start.13 = (bf16[2,96,1024]{2,1,0:T(8,128)(2,1)S(1)}, bf16[2,96,1024]{2,1,0:T(8,128)(2,1)S(1)}, u32[]{:S(2)}, u32[]{:S(2)}) collective-permute-start(bf16[2,96,1024]{2,1,0:T(8,128)(2,1)S(1)} %slice.19), channel_id=1, source_target_pairs={{0,48},{16,0},{32,16},{48,32},{1,49},{17,1},{33,17},{49,33},{2,50}... | collective-permute-start | bytes 1179656 | tf_op jit(solution)/shard_map/ppermute | solution.py:515
  47.7 0.3 collective-permute-done.10.refs_6_
  48.1 0.1 collective-permute-start.12
  48.2 2.8 %collective-permute-done.4.refs_2_ = bf16[4,96,1024]{2,1,0:T(8,128)(2,1)S(1)} collective-permute-done((bf16[4,96,1024]{2,1,0:T(8,128)(2,1)S(1)}, bf16[4,96,1024]{2,1,0:T(8,128)(2,1)S(1)}, u32[]{:S(2)}, u32[]{:S(2)}) %collective-permute-start.4) | collective-permute-done | bytes 786464 | tf_op jit(solution)/shard_map/ppermute | solution.py:513
  51.0 0.1 collective-permute-start.6
  51.1 0.8 copy-done.14
  51.9 2.7 %collective-permute-start.5 = (bf16[2,96,1024]{2,1,0:T(8,128)(2,1)S(1)}, bf16[2,96,1024]{2,1,0:T(8,128)(2,1)}, u32[]{:S(2)}, u32[]{:S(2)}) collective-permute-start(bf16[2,96,1024]{2,1,0:T(8,128)(2,1)S(1)} %slice.16), channel_id=1, source_target_pairs={{0,64},{64,128},{128,192},{192,0},{1,65},{65,129},{129,193},{193,1... | collective-permute-start | bytes 1179656 | tf_op jit(solution)/shard_map/ppermute | solution.py:514
  54.6 4.3 %collective-permute-done.12.refs_8_ = bf16[2,96,1024]{2,1,0:T(8,128)(2,1)S(1)} collective-permute-done((bf16[2,96,1024]{2,1,0:T(8,128)(2,1)S(1)}, bf16[2,96,1024]{2,1,0:T(8,128)(2,1)S(1)}, u32[]{:S(2)}, u32[]{:S(2)}) %collective-permute-start.12) | collective-permute-done | bytes 393248 | tf_op jit(solution)/shard_map/ppermute | solution.py:514
  58.9 1.3 collective-permute-done.6.refs_4_
  60.3 0.1 collective-permute-done.5.refs_3_
  60.4 9.4 %all-gather.3.cloned.1.call-done = bf16[4224,1024]{1,0:T(8,128)(2,1)} async-done(((bf16[264,1024]{1,0:T(8,128)(2,1)}), bf16[4224,1024]{1,0:T(8,128)(2,1)}) %all-gather.3.cloned.1.call-update) | async-done | bytes 8650768 | tf_op jit(solution)/shard_map/all_gather | solution.py:542
  69.9 23.3 %experts.1 = (bf16[4,96,1024]{2,1,0:T(8,128)(2,1)}, bf16[4,96,1024]{2,1,0:T(8,128)(2,1)}, bf16[4,96,1024]{2,1,0:T(8,128)(2,1)}, bf16[2,96,1024]{2,1,0:T(8,128)(2...) custom-call(s32[4]{0:T(128)} %copy-done.11, ...), custom_call_target="tpu_custom_call" | custom-call | flops 10737418240 | bytes 20000000 | tf_op jit(solution)/shard_map/experts/pallas_call | solution.py:45
  93.2 0.3 collective-permute-start.28
  93.5 4.3 %collective-permute-done.28.b = bf16[8,136,1024]{2,1,0:T(8,128)(2,1)S(1)} collective-permute-done((bf16[8,136,1024]{2,1,0:T(8,128)(2,1)}, bf16[8,136,1024]{2,1,0:T(8,128)(2,1)S(1)}, u32[]{:S(2)}, u32[]{:S(2)}) %collective-permute-start.28) | collective-permute-done | bytes 2228256 | tf_op jit(solution)/shard_map/ppermute | solution.py:551
  97.8 1.9 %join.1 = bf16[8,136,1024]{2,1,0:T(8,128)(2,1)} custom-call(bf16[8,136,1024]{2,1,0:T(8,128)(2,1)S(1)} %get-tuple-element.62.a, bf16[8,136,1024]{2,1,0:T(8,128)(2,1)S(1)} %collective-permute-done.28.b), custom_call_target="tpu_custom_call" | custom-call | bytes 1024 | tf_op jit(solution)/shard_map/join/pallas_call | solution.py:45
  99.7 1.5 collective-permute-start.21
  101.3 1.8 %collective-permute-start.22 = (bf16[2,96,1024]{2,1,0:T(8,128)(2,1)}, bf16[2,96,1024]{2,1,0:T(8,128)(2,1)S(1)}, u32[]{:S(2)}, u32[]{:S(2)}) collective-permute-start(bf16[2,96,1024]{2,1,0:T(8,128)(2,1)} %get-tuple-element.55), channel_id=1, source_target_pairs={{0,48},{16,0},{32,16},{48,32},{1,49},{17,1},{33,17},{49,33},{2,50}... | collective-permute-start | bytes 1179656 | tf_op jit(solution)/shard_map/ppermute | solution.py:526
  103.1 0.5 collective-permute-start.14
  103.6 1.5 collective-permute-start.15
  105.1 7.4 %collective-permute-done.21.below = bf16[2,96,1024]{2,1,0:T(8,128)(2,1)S(1)} collective-permute-done((bf16[2,96,1024]{2,1,0:T(8,128)(2,1)}, bf16[2,96,1024]{2,1,0:T(8,128)(2,1)S(1)}, u32[]{:S(2)}, u32[]{:S(2)}) %collective-permute-start.21) | collective-permute-done | bytes 393248 | tf_op jit(solution)/shard_map/ppermute | solution.py:526
  112.5 1.4 fold.3
  113.9 1.5 collective-permute-start.23
  115.4 1.8 %collective-permute-start.24 = (bf16[4,96,1024]{2,1,0:T(8,128)(2,1)S(1)}, bf16[4,96,1024]{2,1,0:T(8,128)(2,1)S(1)}, u32[]{:S(2)}, u32[]{:S(2)}) collective-permute-start(bf16[4,96,1024]{2,1,0:T(8,128)(2,1)S(1)} %get-tuple-element.57), channel_id=1, source_target_pairs={{0,48},{16,0},{32,16},{48,32},{1,49},{17,1},{33,17},{49,33},{2,50}... | collective-permute-start | bytes 2359304 | tf_op jit(solution)/shard_map/ppermute | solution.py:526
  117.3 1.4 fold.2
  118.6 0.6 collective-permute-start.16
  119.2 1.5 collective-permute-start.17
  120.7 13.3 %collective-permute-done.23.below = bf16[4,96,1024]{2,1,0:T(8,128)(2,1)S(1)} collective-permute-done((bf16[4,96,1024]{2,1,0:T(8,128)(2,1)S(1)}, bf16[4,96,1024]{2,1,0:T(8,128)(2,1)S(1)}, u32[]{:S(2)}, u32[]{:S(2)}) %collective-permute-start.23) | collective-permute-done | bytes 786464 | tf_op jit(solution)/shard_map/ppermute | solution.py:526
  134.1 0.3 total.3
  134.4 0.6 collective-permute-start.25
  134.9 2.4 %collective-permute-start.26 = (bf16[96,1024]{1,0:T(8,128)(2,1)S(1)}, bf16[96,1024]{1,0:T(8,128)(2,1)S(1)}, u32[]{:S(2)}, u32[]{:S(2)}) collective-permute-start(bf16[96,1024]{1,0:T(8,128)(2,1)S(1)} %get-tuple-element.60), channel_id=1, source_target_pairs={{0,128},{64,192},{128,0},{192,64},{1,129},{65,193},{129,1},{193,65... | collective-permute-start | bytes 589832 | tf_op jit(solution)/shard_map/ppermute | solution.py:532
  137.4 1.0 collective-permute-done.16.below
  138.3 2.9 %collective-permute-done.17.above = bf16[4,96,1024]{2,1,0:T(8,128)(2,1)S(1)} collective-permute-done((bf16[4,96,1024]{2,1,0:T(8,128)(2,1)S(1)}, bf16[4,96,1024]{2,1,0:T(8,128)(2,1)S(1)}, u32[]{:S(2)}, u32[]{:S(2)}) %collective-permute-start.17) | collective-permute-done | bytes 786464 | tf_op jit(solution)/shard_map/ppermute | solution.py:526
  141.2 0.3 total.2
  141.5 0.1 collective-permute-start.18
  141.6 0.6 collective-permute-start.19
  142.2 0.3 collective-permute-done.25.refs_5_
  142.5 2.3 %collective-permute-start.20 = (bf16[96,1024]{1,0:T(8,128)(2,1)S(1)}, bf16[96,1024]{1,0:T(8,128)(2,1)S(1)}, u32[]{:S(2)}, u32[]{:S(2)}) collective-permute-start(bf16[96,1024]{1,0:T(8,128)(2,1)S(1)} %get-tuple-element.50), channel_id=1, source_target_pairs={{0,48},{16,0},{32,16},{48,32},{1,49},{17,1},{33,17},{49,33},{2,50}... | collective-permute-start | bytes 589832 | tf_op jit(solution)/shard_map/ppermute | solution.py:526
  144.9 2.0 %collective-permute-done.27.refs_7_ = bf16[96,1024]{1,0:T(8,128)(2,1)S(1)} collective-permute-done((bf16[96,1024]{1,0:T(8,128)(2,1)S(1)}, bf16[96,1024]{1,0:T(8,128)(2,1)S(1)}, u32[]{:S(2)}, u32[]{:S(2)}) %collective-permute-start.27) | collective-permute-done | bytes 196640 | tf_op jit(solution)/shard_map/ppermute | solution.py:526
  146.9 3.7 %collective-permute-done.18.refs_1_ = bf16[96,1024]{1,0:T(8,128)(2,1)S(1)} collective-permute-done((bf16[96,1024]{1,0:T(8,128)(2,1)S(1)}, bf16[96,1024]{1,0:T(8,128)(2,1)S(1)}, u32[]{:S(2)}, u32[]{:S(2)}) %collective-permute-start.18) | collective-permute-done | bytes 196640 | tf_op jit(solution)/shard_map/ppermute | solution.py:526
  150.6 0.9 collective-permute-done.20.refs_3_
  151.5 1.0 copy-done.8
  152.5 1.1 finish.1
  (56 shorter events, 0.3 us)
Async XLA Ops:
  7.2 62.7 %all-gather.3.cloned.1.call-start = ((), (), s32[]{:S(2)}) async-start(), calls=%async_computation.2 | async-start | bytes 9191424 | tf_op jit(solution)/shard_map/all_gather | solution.py:542
  7.3 25.1 %copy-start.11 = (s32[4]{0:T(128)}, s32[4]{0:T(128)S(1)}, u32[]{:S(2)}) copy-start(s32[4]{0:T(128)S(1)} %pad_add_fusion.me_ref.where) | copy-start | bytes 52
  9.8 141.7 %reduce-scatter.2.cloned.1.call-start = ((), (), s32[]{:S(2)}) async-start(), calls=%async_computation.1 | async-start | bytes 2506752 | tf_op jit(solution)/shard_map/reduce_scatter | solution.py:557
  9.9 1.0 copy-start.9
  10.8 0.9 copy-start.10
  11.8 12.1 %collective-permute-start.9 = (bf16[96,1024]{1,0:T(8,128)(2,1)S(1)}, bf16[96,1024]{1,0:T(8,128)(2,1)S(1)}, u32[]{:S(2)}, u32[]{:S(2)}) collective-permute-start(bf16[96,1024]{1,0:T(8,128)(2,1)S(1)} %get-tuple-element.39.own), channel_id=1, source_target_pairs={{0,192},{64,0},{128,64},{192,128},{1,193},{65,1},{129,65},{193,129... | collective-permute-start | bytes 589832 | tf_op jit(solution)/shard_map/ppermute | solution.py:526
  12.6 12.8 %collective-permute-start.8 = (bf16[96,1024]{1,0:T(8,128)(2,1)S(1)}, bf16[96,1024]{1,0:T(8,128)(2,1)S(1)}, u32[]{:S(2)}, u32[]{:S(2)}) collective-permute-start(bf16[96,1024]{1,0:T(8,128)(2,1)S(1)} %get-tuple-element.39.own), channel_id=1, source_target_pairs={{0,128},{64,192},{128,0},{192,64},{1,129},{65,193},{129,1},{193,65... | collective-permute-start | bytes 589832 | tf_op jit(solution)/shard_map/ppermute | solution.py:521
  15.3 10.1 %collective-permute-start.7 = (bf16[96,1024]{1,0:T(8,128)(2,1)S(1)}, bf16[96,1024]{1,0:T(8,128)(2,1)S(1)}, u32[]{:S(2)}, u32[]{:S(2)}) collective-permute-start(bf16[96,1024]{1,0:T(8,128)(2,1)S(1)} %get-tuple-element.39.own), channel_id=1, source_target_pairs={{0,64},{64,128},{128,192},{192,0},{1,65},{65,129},{129,193},{193,1... | collective-permute-start | bytes 589832 | tf_op jit(solution)/shard_map/ppermute | solution.py:526
  15.7 12.4 %collective-permute-start.2 = (bf16[96,1024]{1,0:T(8,128)(2,1)S(1)}, bf16[96,1024]{1,0:T(8,128)(2,1)S(1)}, u32[]{:S(2)}, u32[]{:S(2)}) collective-permute-start(bf16[96,1024]{1,0:T(8,128)(2,1)S(1)} %get-tuple-element.38.own), channel_id=1, source_target_pairs={{0,48},{16,0},{32,16},{48,32},{1,49},{17,1},{33,17},{49,33},{2,50}... | collective-permute-start | bytes 589832 | tf_op jit(solution)/shard_map/ppermute | solution.py:526
  18.5 9.7 %collective-permute-start.1 = (bf16[96,1024]{1,0:T(8,128)(2,1)S(1)}, bf16[96,1024]{1,0:T(8,128)(2,1)S(1)}, u32[]{:S(2)}, u32[]{:S(2)}) collective-permute-start(bf16[96,1024]{1,0:T(8,128)(2,1)S(1)} %get-tuple-element.38.own), channel_id=1, source_target_pairs={{0,32},{16,48},{32,0},{48,16},{1,33},{17,49},{33,1},{49,17},{2,34}... | collective-permute-start | bytes 589832 | tf_op jit(solution)/shard_map/ppermute | solution.py:521
  23.9 7.9 %collective-permute-start = (bf16[96,1024]{1,0:T(8,128)(2,1)S(1)}, bf16[96,1024]{1,0:T(8,128)(2,1)S(1)}, u32[]{:S(2)}, u32[]{:S(2)}) collective-permute-start(bf16[96,1024]{1,0:T(8,128)(2,1)S(1)} %get-tuple-element.38.own), channel_id=1, source_target_pairs={{0,16},{16,32},{32,48},{48,0},{1,17},{17,33},{33,49},{49,1},{2,18}... | collective-permute-start | bytes 589832 | tf_op jit(solution)/shard_map/ppermute | solution.py:526
  26.0 25.9 %copy-start = (bf16[4,96,1024]{2,1,0:T(8,128)(2,1)}, bf16[4,96,1024]{2,1,0:T(8,128)(2,1)S(1)}, u32[]{:S(2)}) copy-start(bf16[4,96,1024]{2,1,0:T(8,128)(2,1)S(1)} %place.3.refs_5_) | copy-start | bytes 2359300
  26.0 18.2 %collective-permute-start.11 = (bf16[4,96,1024]{2,1,0:T(8,128)(2,1)S(1)}, bf16[4,96,1024]{2,1,0:T(8,128)(2,1)S(1)}, u32[]{:S(2)}, u32[]{:S(2)}) collective-permute-start(bf16[4,96,1024]{2,1,0:T(8,128)(2,1)S(1)} %place.3.refs_5_), channel_id=1, source_target_pairs={{0,48},{16,0},{32,16},{48,32},{1,49},{17,1},{33,17},{49,33},{2,50}... | collective-permute-start | bytes 2359304 | tf_op jit(solution)/shard_map/ppermute | solution.py:513
  28.0 20.0 %collective-permute-start.10 = (bf16[4,96,1024]{2,1,0:T(8,128)(2,1)S(1)}, bf16[4,96,1024]{2,1,0:T(8,128)(2,1)S(1)}, u32[]{:S(2)}, u32[]{:S(2)}) collective-permute-start(bf16[4,96,1024]{2,1,0:T(8,128)(2,1)S(1)} %place.3.refs_5_), channel_id=1, source_target_pairs={{0,16},{16,32},{32,48},{48,0},{1,17},{17,33},{33,49},{49,1},{2,18}... | collective-permute-start | bytes 2359304 | tf_op jit(solution)/shard_map/ppermute | solution.py:512
  32.4 37.4 %copy-start.1 = (bf16[4,96,1024]{2,1,0:T(8,128)(2,1)}, bf16[4,96,1024]{2,1,0:T(8,128)(2,1)S(1)}, u32[]{:S(2)}) copy-start(bf16[4,96,1024]{2,1,0:T(8,128)(2,1)S(1)} %place.2.refs_0_) | copy-start | bytes 2359300
  32.4 18.5 %collective-permute-start.4 = (bf16[4,96,1024]{2,1,0:T(8,128)(2,1)S(1)}, bf16[4,96,1024]{2,1,0:T(8,128)(2,1)S(1)}, u32[]{:S(2)}, u32[]{:S(2)}) collective-permute-start(bf16[4,96,1024]{2,1,0:T(8,128)(2,1)S(1)} %place.2.refs_0_), channel_id=1, source_target_pairs={{0,192},{64,0},{128,64},{192,128},{1,193},{65,1},{129,65},{193,129... | collective-permute-start | bytes 2359304 | tf_op jit(solution)/shard_map/ppermute | solution.py:513
  32.5 19.3 %collective-permute-start.3 = (bf16[4,96,1024]{2,1,0:T(8,128)(2,1)S(1)}, bf16[4,96,1024]{2,1,0:T(8,128)(2,1)S(1)}, u32[]{:S(2)}, u32[]{:S(2)}) collective-permute-start(bf16[4,96,1024]{2,1,0:T(8,128)(2,1)S(1)} %place.2.refs_0_), channel_id=1, source_target_pairs={{0,64},{64,128},{128,192},{192,0},{1,65},{65,129},{129,193},{193,1... | collective-permute-start | bytes 2359304 | tf_op jit(solution)/shard_map/ppermute | solution.py:512
  44.2 25.6 %copy-start.12 = (bf16[4,96,1024]{2,1,0:T(8,128)(2,1)}, bf16[4,96,1024]{2,1,0:T(8,128)(2,1)S(1)}, u32[]{:S(2)}) copy-start(bf16[4,96,1024]{2,1,0:T(8,128)(2,1)S(1)} %collective-permute-done.11.refs_7_) | copy-start | bytes 2359300
  44.3 10.3 %collective-permute-start.13 = (bf16[2,96,1024]{2,1,0:T(8,128)(2,1)S(1)}, bf16[2,96,1024]{2,1,0:T(8,128)(2,1)S(1)}, u32[]{:S(2)}, u32[]{:S(2)}) collective-permute-start(bf16[2,96,1024]{2,1,0:T(8,128)(2,1)S(1)} %slice.19), channel_id=1, source_target_pairs={{0,48},{16,0},{32,16},{48,32},{1,49},{17,1},{33,17},{49,33},{2,50}... | collective-permute-start | bytes 1179656 | tf_op jit(solution)/shard_map/ppermute | solution.py:515
  48.0 21.8 %copy-start.13 = (bf16[4,96,1024]{2,1,0:T(8,128)(2,1)}, bf16[4,96,1024]{2,1,0:T(8,128)(2,1)S(1)}, u32[]{:S(2)}) copy-start(bf16[4,96,1024]{2,1,0:T(8,128)(2,1)S(1)} %collective-permute-done.10.refs_6_) | copy-start | bytes 2359300
  48.1 10.9 %collective-permute-start.12 = (bf16[2,96,1024]{2,1,0:T(8,128)(2,1)S(1)}, bf16[2,96,1024]{2,1,0:T(8,128)(2,1)S(1)}, u32[]{:S(2)}, u32[]{:S(2)}) collective-permute-start(bf16[2,96,1024]{2,1,0:T(8,128)(2,1)S(1)} %slice.18), channel_id=1, source_target_pairs={{0,16},{16,32},{32,48},{48,0},{1,17},{17,33},{33,49},{49,1},{2,18}... | collective-permute-start | bytes 1179656 | tf_op jit(solution)/shard_map/ppermute | solution.py:514
  51.0 0.9 copy-start.14
  51.0 9.3 %collective-permute-start.6 = (bf16[2,96,1024]{2,1,0:T(8,128)(2,1)S(1)}, bf16[2,96,1024]{2,1,0:T(8,128)(2,1)S(1)}, u32[]{:S(2)}, u32[]{:S(2)}) collective-permute-start(bf16[2,96,1024]{2,1,0:T(8,128)(2,1)S(1)} %slice.17), channel_id=1, source_target_pairs={{0,192},{64,0},{128,64},{192,128},{1,193},{65,1},{129,65},{193,129... | collective-permute-start | bytes 1179656 | tf_op jit(solution)/shard_map/ppermute | solution.py:515
  51.9 8.4 %copy-start.15 = (bf16[4,96,1024]{2,1,0:T(8,128)(2,1)}, bf16[4,96,1024]{2,1,0:T(8,128)(2,1)S(1)}, u32[]{:S(2)}) copy-start(bf16[4,96,1024]{2,1,0:T(8,128)(2,1)S(1)} %collective-permute-done.3.refs_1_) | copy-start | bytes 2359300
  51.9 8.5 %collective-permute-start.5 = (bf16[2,96,1024]{2,1,0:T(8,128)(2,1)S(1)}, bf16[2,96,1024]{2,1,0:T(8,128)(2,1)}, u32[]{:S(2)}, u32[]{:S(2)}) collective-permute-start(bf16[2,96,1024]{2,1,0:T(8,128)(2,1)S(1)} %slice.16), channel_id=1, source_target_pairs={{0,64},{64,128},{128,192},{192,0},{1,65},{65,129},{129,193},{193,1... | collective-permute-start | bytes 1179656 | tf_op jit(solution)/shard_map/ppermute | solution.py:514
  54.6 15.2 %copy-start.17 = (bf16[2,96,1024]{2,1,0:T(8,128)(2,1)}, bf16[2,96,1024]{2,1,0:T(8,128)(2,1)S(1)}, u32[]{:S(2)}) copy-start(bf16[2,96,1024]{2,1,0:T(8,128)(2,1)S(1)} %collective-permute-done.13.refs_9_) | copy-start | bytes 1179652
  58.9 10.9 %copy-start.18 = (bf16[2,96,1024]{2,1,0:T(8,128)(2,1)}, bf16[2,96,1024]{2,1,0:T(8,128)(2,1)S(1)}, u32[]{:S(2)}) copy-start(bf16[2,96,1024]{2,1,0:T(8,128)(2,1)S(1)} %collective-permute-done.12.refs_8_) | copy-start | bytes 1179652
  60.3 9.6 %copy-start.19 = (bf16[2,96,1024]{2,1,0:T(8,128)(2,1)}, bf16[2,96,1024]{2,1,0:T(8,128)(2,1)S(1)}, u32[]{:S(2)}) copy-start(bf16[2,96,1024]{2,1,0:T(8,128)(2,1)S(1)} %collective-permute-done.6.refs_4_) | copy-start | bytes 1179652
  93.2 4.6 %collective-permute-start.28 = (bf16[8,136,1024]{2,1,0:T(8,128)(2,1)}, bf16[8,136,1024]{2,1,0:T(8,128)(2,1)S(1)}, u32[]{:S(2)}, u32[]{:S(2)}) collective-permute-start(bf16[8,136,1024]{2,1,0:T(8,128)(2,1)} %get-tuple-element.63), channel_id=1, source_target_pairs={{0,1},{1,0},{2,3},{3,2},{4,5},{5,4},{6,7},{7,6},{8,9},{9,8},{10,11... | collective-permute-start | bytes 6684680 | tf_op jit(solution)/shard_map/ppermute | solution.py:551
  99.7 3.9 %copy-start.16 = (bf16[2,96,1024]{2,1,0:T(8,128)(2,1)S(1)}, bf16[2,96,1024]{2,1,0:T(8,128)(2,1)}, u32[]{:S(2)}) copy-start(bf16[2,96,1024]{2,1,0:T(8,128)(2,1)} %get-tuple-element.44) | copy-start | bytes 1179652
  99.7 12.8 %copy-start.6 = (bf16[4,96,1024]{2,1,0:T(8,128)(2,1)S(1)}, bf16[4,96,1024]{2,1,0:T(8,128)(2,1)}, u32[]{:S(2)}) copy-start(bf16[4,96,1024]{2,1,0:T(8,128)(2,1)} %get-tuple-element.52.up) | copy-start | bytes 2359300
  99.7 12.8 %copy-start.7 = (bf16[4,96,1024]{2,1,0:T(8,128)(2,1)S(1)}, bf16[4,96,1024]{2,1,0:T(8,128)(2,1)}, u32[]{:S(2)}) copy-start(bf16[4,96,1024]{2,1,0:T(8,128)(2,1)} %get-tuple-element.53.down) | copy-start | bytes 2359300
  99.7 17.5 %copy-start.4 = (bf16[4,96,1024]{2,1,0:T(8,128)(2,1)S(1)}, bf16[4,96,1024]{2,1,0:T(8,128)(2,1)}, u32[]{:S(2)}) copy-start(bf16[4,96,1024]{2,1,0:T(8,128)(2,1)} %get-tuple-element.41.up) | copy-start | bytes 2359300
  99.7 17.5 %copy-start.5 = (bf16[4,96,1024]{2,1,0:T(8,128)(2,1)S(1)}, bf16[4,96,1024]{2,1,0:T(8,128)(2,1)}, u32[]{:S(2)}) copy-start(bf16[4,96,1024]{2,1,0:T(8,128)(2,1)} %get-tuple-element.42.down) | copy-start | bytes 2359300
  99.7 12.8 %collective-permute-start.21 = (bf16[2,96,1024]{2,1,0:T(8,128)(2,1)}, bf16[2,96,1024]{2,1,0:T(8,128)(2,1)S(1)}, u32[]{:S(2)}, u32[]{:S(2)}) collective-permute-start(bf16[2,96,1024]{2,1,0:T(8,128)(2,1)} %get-tuple-element.54), channel_id=1, source_target_pairs={{0,16},{16,32},{32,48},{48,0},{1,17},{17,33},{33,49},{49,1},{2,18}... | collective-permute-start | bytes 1179656 | tf_op jit(solution)/shard_map/ppermute | solution.py:526
  101.3 11.2 %collective-permute-start.22 = (bf16[2,96,1024]{2,1,0:T(8,128)(2,1)}, bf16[2,96,1024]{2,1,0:T(8,128)(2,1)S(1)}, u32[]{:S(2)}, u32[]{:S(2)}) collective-permute-start(bf16[2,96,1024]{2,1,0:T(8,128)(2,1)} %get-tuple-element.55), channel_id=1, source_target_pairs={{0,48},{16,0},{32,16},{48,32},{1,49},{17,1},{33,17},{49,33},{2,50}... | collective-permute-start | bytes 1179656 | tf_op jit(solution)/shard_map/ppermute | solution.py:526
  103.1 14.2 %collective-permute-start.14 = (bf16[2,96,1024]{2,1,0:T(8,128)(2,1)}, bf16[2,96,1024]{2,1,0:T(8,128)(2,1)S(1)}, u32[]{:S(2)}, u32[]{:S(2)}) collective-permute-start(bf16[2,96,1024]{2,1,0:T(8,128)(2,1)} %get-tuple-element.43), channel_id=1, source_target_pairs={{0,64},{64,128},{128,192},{192,0},{1,65},{65,129},{129,193},{193,1... | collective-permute-start | bytes 1179656 | tf_op jit(solution)/shard_map/ppermute | solution.py:526
  103.6 13.7 %collective-permute-start.15 = (bf16[2,96,1024]{2,1,0:T(8,128)(2,1)S(1)}, bf16[2,96,1024]{2,1,0:T(8,128)(2,1)S(1)}, u32[]{:S(2)}, u32[]{:S(2)}) collective-permute-start(bf16[2,96,1024]{2,1,0:T(8,128)(2,1)S(1)} %copy-done.16), channel_id=1, source_target_pairs={{0,192},{64,0},{128,64},{192,128},{1,193},{65,1},{129,65},{193,129... | collective-permute-start | bytes 1179656 | tf_op jit(solution)/shard_map/ppermute | solution.py:526
  112.5 21.6 %copy-start.3 = (bf16[4,96,1024]{2,1,0:T(8,128)(2,1)S(1)}, bf16[4,96,1024]{2,1,0:T(8,128)(2,1)}, u32[]{:S(2)}) copy-start(bf16[4,96,1024]{2,1,0:T(8,128)(2,1)} %get-tuple-element.51.own) | copy-start | bytes 2359300
  113.9 20.2 %collective-permute-start.23 = (bf16[4,96,1024]{2,1,0:T(8,128)(2,1)S(1)}, bf16[4,96,1024]{2,1,0:T(8,128)(2,1)S(1)}, u32[]{:S(2)}, u32[]{:S(2)}) collective-permute-start(bf16[4,96,1024]{2,1,0:T(8,128)(2,1)S(1)} %get-tuple-element.56), channel_id=1, source_target_pairs={{0,16},{16,32},{32,48},{48,0},{1,17},{17,33},{33,49},{49,1},{2,18}... | collective-permute-start | bytes 2359304 | tf_op jit(solution)/shard_map/ppermute | solution.py:526
  115.4 18.7 %collective-permute-start.24 = (bf16[4,96,1024]{2,1,0:T(8,128)(2,1)S(1)}, bf16[4,96,1024]{2,1,0:T(8,128)(2,1)S(1)}, u32[]{:S(2)}, u32[]{:S(2)}) collective-permute-start(bf16[4,96,1024]{2,1,0:T(8,128)(2,1)S(1)} %get-tuple-element.57), channel_id=1, source_target_pairs={{0,48},{16,0},{32,16},{48,32},{1,49},{17,1},{33,17},{49,33},{2,50}... | collective-permute-start | bytes 2359304 | tf_op jit(solution)/shard_map/ppermute | solution.py:526
  117.2 24.0 %copy-start.2 = (bf16[4,96,1024]{2,1,0:T(8,128)(2,1)S(1)}, bf16[4,96,1024]{2,1,0:T(8,128)(2,1)}, u32[]{:S(2)}) copy-start(bf16[4,96,1024]{2,1,0:T(8,128)(2,1)} %get-tuple-element.40.own) | copy-start | bytes 2359300
  118.6 19.7 %collective-permute-start.16 = (bf16[4,96,1024]{2,1,0:T(8,128)(2,1)S(1)}, bf16[4,96,1024]{2,1,0:T(8,128)(2,1)S(1)}, u32[]{:S(2)}, u32[]{:S(2)}) collective-permute-start(bf16[4,96,1024]{2,1,0:T(8,128)(2,1)S(1)} %get-tuple-element.45), channel_id=1, source_target_pairs={{0,64},{64,128},{128,192},{192,0},{1,65},{65,129},{129,193},{193,1... | collective-permute-start | bytes 2359304 | tf_op jit(solution)/shard_map/ppermute | solution.py:526
  119.2 22.0 %collective-permute-start.17 = (bf16[4,96,1024]{2,1,0:T(8,128)(2,1)S(1)}, bf16[4,96,1024]{2,1,0:T(8,128)(2,1)S(1)}, u32[]{:S(2)}, u32[]{:S(2)}) collective-permute-start(bf16[4,96,1024]{2,1,0:T(8,128)(2,1)S(1)} %get-tuple-element.46), channel_id=1, source_target_pairs={{0,192},{64,0},{128,64},{192,128},{1,193},{65,1},{129,65},{193,129... | collective-permute-start | bytes 2359304 | tf_op jit(solution)/shard_map/ppermute | solution.py:526
  134.4 8.2 %collective-permute-start.25 = (bf16[96,1024]{1,0:T(8,128)(2,1)S(1)}, bf16[96,1024]{1,0:T(8,128)(2,1)S(1)}, u32[]{:S(2)}, u32[]{:S(2)}) collective-permute-start(bf16[96,1024]{1,0:T(8,128)(2,1)S(1)} %get-tuple-element.59), channel_id=1, source_target_pairs={{0,64},{64,128},{128,192},{192,0},{1,65},{65,129},{129,193},{193,1... | collective-permute-start | bytes 589832 | tf_op jit(solution)/shard_map/ppermute | solution.py:526
  134.9 9.9 %collective-permute-start.26 = (bf16[96,1024]{1,0:T(8,128)(2,1)S(1)}, bf16[96,1024]{1,0:T(8,128)(2,1)S(1)}, u32[]{:S(2)}, u32[]{:S(2)}) collective-permute-start(bf16[96,1024]{1,0:T(8,128)(2,1)S(1)} %get-tuple-element.60), channel_id=1, source_target_pairs={{0,128},{64,192},{128,0},{192,64},{1,129},{65,193},{129,1},{193,65... | collective-permute-start | bytes 589832 | tf_op jit(solution)/shard_map/ppermute | solution.py:532
  137.4 9.5 %collective-permute-start.27 = (bf16[96,1024]{1,0:T(8,128)(2,1)S(1)}, bf16[96,1024]{1,0:T(8,128)(2,1)S(1)}, u32[]{:S(2)}, u32[]{:S(2)}) collective-permute-start(bf16[96,1024]{1,0:T(8,128)(2,1)S(1)} %get-tuple-element.61), channel_id=1, source_target_pairs={{0,192},{64,0},{128,64},{192,128},{1,193},{65,1},{129,65},{193,129... | collective-permute-start | bytes 589832 | tf_op jit(solution)/shard_map/ppermute | solution.py:526
  141.5 9.1 %collective-permute-start.18 = (bf16[96,1024]{1,0:T(8,128)(2,1)S(1)}, bf16[96,1024]{1,0:T(8,128)(2,1)S(1)}, u32[]{:S(2)}, u32[]{:S(2)}) collective-permute-start(bf16[96,1024]{1,0:T(8,128)(2,1)S(1)} %get-tuple-element.48), channel_id=1, source_target_pairs={{0,16},{16,32},{32,48},{48,0},{1,17},{17,33},{33,49},{49,1},{2,18}... | collective-permute-start | bytes 589832 | tf_op jit(solution)/shard_map/ppermute | solution.py:526
  141.6 9.0 %collective-permute-start.19 = (bf16[96,1024]{1,0:T(8,128)(2,1)S(1)}, bf16[96,1024]{1,0:T(8,128)(2,1)S(1)}, u32[]{:S(2)}, u32[]{:S(2)}) collective-permute-start(bf16[96,1024]{1,0:T(8,128)(2,1)S(1)} %get-tuple-element.49), channel_id=1, source_target_pairs={{0,32},{16,48},{32,0},{48,16},{1,33},{17,49},{33,1},{49,17},{2,34}... | collective-permute-start | bytes 589832 | tf_op jit(solution)/shard_map/ppermute | solution.py:532
  142.5 9.0 %collective-permute-start.20 = (bf16[96,1024]{1,0:T(8,128)(2,1)S(1)}, bf16[96,1024]{1,0:T(8,128)(2,1)S(1)}, u32[]{:S(2)}, u32[]{:S(2)}) collective-permute-start(bf16[96,1024]{1,0:T(8,128)(2,1)S(1)} %get-tuple-element.50), channel_id=1, source_target_pairs={{0,48},{16,0},{32,16},{48,32},{1,49},{17,1},{33,17},{49,33},{2,50}... | collective-permute-start | bytes 589832 | tf_op jit(solution)/shard_map/ppermute | solution.py:526
  151.5 1.0 copy-start.8
Sparse Core Ops, SparseCore 0:
  10.0 59.8 all-gather.2
  99.9 41.1 reduce-scatter.1

commit v2 on v1

--- a/solution.py
+++ b/solution.py
@@ -142,6 +142,7 @@
 
 
 TILE = 256
+BACK_TILE = 512
 START_AT = 2
 
 
@@ -245,7 +246,7 @@
     lax.fori_loop(0, HID // 128, flip_act, 0, unroll=True)
 
     def backward(i, _):
-        cols = pl.ds(pl.multiple_of(i * TILE, TILE), TILE)
+        cols = pl.ds(pl.multiple_of(i * BACK_TILE, BACK_TILE), BACK_TILE)
         gin[...] = dot(xt[...], pre[:, cols], NN).astype(BF16).reshape(gin.shape)
         gout[...] = dot(at[...], dy[:, cols], NN).astype(BF16).reshape(gout.shape)
         for oj in range(4):
@@ -257,7 +258,7 @@
                 held[oj, ij, ROWS_IN:ROWS, cols] = gout[b]
         return 0
 
-    lax.fori_loop(0, WIDTH // TILE, backward, 0, unroll=True)
+    lax.fori_loop(0, WIDTH // BACK_TILE, backward, 0, unroll=True)
 
     def input_grad(i, _):
         w = w_in[i].reshape(TILE, WIDTH)
@@ -403,8 +404,8 @@
             pltpu.VMEM((SLOTS, HID), BF16),
             pltpu.VMEM((WIDTH, SLOTS), BF16),
             pltpu.VMEM((HID, SLOTS), BF16),
-            pltpu.VMEM((16, ROWS_IN, TILE), BF16),
-            pltpu.VMEM((16, ROWS_OUT, TILE), BF16),
+            pltpu.VMEM((16, ROWS_IN, BACK_TILE), BF16),
+            pltpu.VMEM((16, ROWS_OUT, BACK_TILE), BF16),
             pltpu.VMEM((CHIPS, 2, TOK + TOP, WIDTH), BF16),
             pltpu.VMEM((2, 4, 4, ROWS, WIDTH), BF16),
             pltpu.SemaphoreType.DMA((CHIPS,)),
@@ -480,28 +481,31 @@
     return call(total_kernel, "total", outs, own, below, above, cost=cost(0, 1024))
 
 
+def tokens_kernel(done, d_tok, d_gate):
+    d_tok[...] = done[:TOK]
+    d_gate[...] = done[TOK:, :TOK]
+
+
+def tokens_of(done):
+    return call(
+        tokens_kernel, "tokens", [shape(TOK, WIDTH), shape(TOP, TOK)], done, cost=cost(0, 1024)
+    )
+
+
 def finish_kernel(*refs):
-    done = refs[8]
-    d_tok, d_gate, d_in, d_out = refs[9:]
+    d_in, d_out = refs[8:]
     for e in range(2):
         kept, a, b, c = refs[4 * e : 4 * e + 4]
         total = kept[...] + a[...].astype(F32) + b[...].astype(F32) + c[...].astype(F32)
         d_in[e] = total[:ROWS_IN]
         d_out[e] = total[ROWS_IN:]
-    d_tok[...] = done[:TOK]
-    d_gate[...] = done[TOK:, :TOK]
 
 
 def finish(*parts):
     return call(
         finish_kernel,
         "finish",
-        [
-            shape(TOK, WIDTH),
-            shape(TOP, TOK),
-            shape(2, ROWS_IN, WIDTH, dtype=F32),
-            shape(2, ROWS_OUT, WIDTH, dtype=F32),
-        ],
+        [shape(2, ROWS_IN, WIDTH, dtype=F32), shape(2, ROWS_OUT, WIDTH, dtype=F32)],
         *parts,
         cost=cost(0, 1024),
     )
@@ -557,9 +561,12 @@
     done = lax.psum_scatter(pair, "z", scatter_dimension=0, tiled=True)
     out0 = total_of(mine0, below0, above0)
     out1 = total_of(mine1, below1, above1)
-    grad_tokens, grad_gates, grad_gate_up, grad_down = finish(
-        *spread(out0, "x"), *spread(out1, "y"), done
-    )
+    grad_tokens, grad_gates = tokens_of(done)
+    parts0 = spread(out0, "x")
+    kept0, grad_tokens, grad_gates = lax.optimization_barrier(
+        (parts0[0], grad_tokens, grad_gates)
+    )
+    grad_gate_up, grad_down = finish(kept0, *parts0[1:], *spread(out1, "y"))
     return grad_tokens, grad_gates.T, grad_gate_up, grad_down
 
 

time: 161 us -> 159 us (0.988)
  waiting for transfers between devices: 71.1 us -> 69.4 us
    ppermute x16, waiting for transfers between devices: 39.9 us -> 38.2 us  [swap(): return (lax.ppermute(a, axis, UP), lax.ppermute(b, axis, DOWN))]
    pallas_call x11 -> x12, Pallas kernels: 33.3 us -> 33.3 us  [call(): pl.pallas_call(kernel, name=name, in_specs=[smem] * scalars + (specs or [...]
where the time goes in v2:
time: 159 us
  waiting for transfers between devices  69.4 us (44%)
  starting transfers between devices  37.9 us (24%)
  Pallas kernels  33.3 us (21%)
  between operations  14.3 us (9%)
  local copies, waits for them, and re-layouts  3.74 us (2%)
    ppermute x16, waiting for transfers between devices, swap(): return (lax.ppermute(a, axis, UP), lax.ppermute(b, axis, DOWN))  38.2 us
    pallas_call x12, Pallas kernels, call(): pl.pallas_call(kernel, name=name, in_specs=[smem] * scalars + (specs or [...  33.3 us
    ppermute x16, starting transfers between devices, swap(): return (lax.ppermute(a, axis, UP), lax.ppermute(b, axis, DOWN))  19.3 us
    ppermute x2, waiting for transfers between devices, gather_ring(): above = lax.ppermute(block, axis, DOWN)  11.3 us
    all_gather x1, waiting for transfers between devices, body(): pay = lax.all_gather(pay, ('z', 'core'), axis=0, tiled=False)  9.45 us
    ppermute x2, waiting for transfers between devices, gather_ring(): far_a = lax.ppermute(below[:half], axis, UP)  4.43 us
    ppermute x1, waiting for transfers between devices, body(): got = lax.ppermute(send, 'core', [(0, 1), (1, 0)])  4.33 us
    unnamed x40, local copies, waits for them, and re-layouts  3.64 us
  transfers between devices with their start and end apart: 31, of which 18 were waited for; matrix products, arithmetic and copies ran while one was open for 0% of the time, Pallas kernels for 3%

profile of v2, /device:TPU:24, one launch (start us, length us, event | category | flops | bytes accessed | tf_op | source)
XLA Modules:
  0.0 158.7 jit_solution(10207623704257869744)
XLA Ops:
  7.2 0.0 all-gather.3.cloned.1.call-start
  7.2 0.1 pad_add_fusion.me_ref.where
  7.3 2.5 %pack.1 = bf16[264,1024]{1,0:T(8,128)(2,1)} custom-call(bf16[128,1024]{1,0:T(8,128)(2,1)} %tok.1, bf16[128,1024]{1,0:T(8,128)(2,1)} %cot.1, s32[8,128]{1,0:T(8,128)} %bitcast.9, bf16[8,128]{1,0:T(8,128)(2,1)} %bitcast.10), custom_call_target="tpu_custom_call" | custom-call | bytes 2000000 | tf_op jit(solution)/shard_map/pack/pallas_call | solution.py:45
  9.8 0.0 reduce-scatter.2.cloned.1.call-start
  9.9 0.9 copy-done.9
  10.8 0.9 copy-done.10
  11.8 0.8 collective-permute-start.9
  12.6 2.7 %collective-permute-start.8 = (bf16[96,1024]{1,0:T(8,128)(2,1)S(1)}, bf16[96,1024]{1,0:T(8,128)(2,1)S(1)}, u32[]{:S(2)}, u32[]{:S(2)}) collective-permute-start(bf16[96,1024]{1,0:T(8,128)(2,1)S(1)} %get-tuple-element.42.own), channel_id=1, source_target_pairs={{0,128},{64,192},{128,0},{192,64},{1,129},{65,193},{129,1},{193,65... | collective-permute-start | bytes 589832 | tf_op jit(solution)/shard_map/ppermute | solution.py:525
  15.3 0.4 collective-permute-start.7
  15.7 2.8 %collective-permute-start.2 = (bf16[96,1024]{1,0:T(8,128)(2,1)S(1)}, bf16[96,1024]{1,0:T(8,128)(2,1)S(1)}, u32[]{:S(2)}, u32[]{:S(2)}) collective-permute-start(bf16[96,1024]{1,0:T(8,128)(2,1)S(1)} %get-tuple-element.41.own), channel_id=1, source_target_pairs={{0,48},{16,0},{32,16},{48,32},{1,49},{17,1},{33,17},{49,33},{2,50}... | collective-permute-start | bytes 589832 | tf_op jit(solution)/shard_map/ppermute | solution.py:530
  18.5 0.8 collective-permute-start.1
  19.3 4.6 %collective-permute-done.9.above = bf16[96,1024]{1,0:T(8,128)(2,1)S(1)} collective-permute-done((bf16[96,1024]{1,0:T(8,128)(2,1)S(1)}, bf16[96,1024]{1,0:T(8,128)(2,1)S(1)}, u32[]{:S(2)}, u32[]{:S(2)}) %collective-permute-start.9) | collective-permute-done | bytes 196640 | tf_op jit(solution)/shard_map/ppermute | solution.py:530
  23.9 1.5 collective-permute-start
  25.4 0.6 place.3.refs_5_
  26.0 2.0 %collective-permute-start.11 = (bf16[4,96,1024]{2,1,0:T(8,128)(2,1)S(1)}, bf16[4,96,1024]{2,1,0:T(8,128)(2,1)S(1)}, u32[]{:S(2)}, u32[]{:S(2)}) collective-permute-start(bf16[4,96,1024]{2,1,0:T(8,128)(2,1)S(1)} %place.3.refs_5_), channel_id=1, source_target_pairs={{0,48},{16,0},{32,16},{48,32},{1,49},{17,1},{33,17},{49,33},{2,50}... | collective-permute-start | bytes 2359304 | tf_op jit(solution)/shard_map/ppermute | solution.py:517
  28.0 0.1 collective-permute-start.10
  28.1 3.7 %collective-permute-done.below = bf16[96,1024]{1,0:T(8,128)(2,1)S(1)} collective-permute-done((bf16[96,1024]{1,0:T(8,128)(2,1)S(1)}, bf16[96,1024]{1,0:T(8,128)(2,1)S(1)}, u32[]{:S(2)}, u32[]{:S(2)}) %collective-permute-start) | collective-permute-done | bytes 196640 | tf_op jit(solution)/shard_map/ppermute | solution.py:530
  31.8 0.6 place.2.refs_0_
  32.4 0.1 collective-permute-start.4
  32.5 3.2 %collective-permute-start.3 = (bf16[4,96,1024]{2,1,0:T(8,128)(2,1)S(1)}, bf16[4,96,1024]{2,1,0:T(8,128)(2,1)S(1)}, u32[]{:S(2)}, u32[]{:S(2)}) collective-permute-start(bf16[4,96,1024]{2,1,0:T(8,128)(2,1)S(1)} %place.2.refs_0_), channel_id=1, source_target_pairs={{0,64},{64,128},{128,192},{192,0},{1,65},{65,129},{129,193},{193,1... | collective-permute-start | bytes 2359304 | tf_op jit(solution)/shard_map/ppermute | solution.py:516
  35.7 8.5 %collective-permute-done.11.refs_7_ = bf16[4,96,1024]{2,1,0:T(8,128)(2,1)S(1)} collective-permute-done((bf16[4,96,1024]{2,1,0:T(8,128)(2,1)S(1)}, bf16[4,96,1024]{2,1,0:T(8,128)(2,1)S(1)}, u32[]{:S(2)}, u32[]{:S(2)}) %collective-permute-start.11) | collective-permute-done | bytes 786464 | tf_op jit(solution)/shard_map/ppermute | solution.py:517
  44.3 3.4 %collective-permute-start.13 = (bf16[2,96,1024]{2,1,0:T(8,128)(2,1)S(1)}, bf16[2,96,1024]{2,1,0:T(8,128)(2,1)S(1)}, u32[]{:S(2)}, u32[]{:S(2)}) collective-permute-start(bf16[2,96,1024]{2,1,0:T(8,128)(2,1)S(1)} %slice.19), channel_id=1, source_target_pairs={{0,48},{16,0},{32,16},{48,32},{1,49},{17,1},{33,17},{49,33},{2,50}... | collective-permute-start | bytes 1179656 | tf_op jit(solution)/shard_map/ppermute | solution.py:519
  47.7 0.3 collective-permute-done.10.refs_6_
  48.1 0.1 collective-permute-start.12
  48.2 2.8 %collective-permute-done.4.refs_2_ = bf16[4,96,1024]{2,1,0:T(8,128)(2,1)S(1)} collective-permute-done((bf16[4,96,1024]{2,1,0:T(8,128)(2,1)S(1)}, bf16[4,96,1024]{2,1,0:T(8,128)(2,1)S(1)}, u32[]{:S(2)}, u32[]{:S(2)}) %collective-permute-start.4) | collective-permute-done | bytes 786464 | tf_op jit(solution)/shard_map/ppermute | solution.py:517
  51.0 0.1 collective-permute-start.6
  51.1 0.8 copy-done.14
  51.9 2.7 %collective-permute-start.5 = (bf16[2,96,1024]{2,1,0:T(8,128)(2,1)S(1)}, bf16[2,96,1024]{2,1,0:T(8,128)(2,1)}, u32[]{:S(2)}, u32[]{:S(2)}) collective-permute-start(bf16[2,96,1024]{2,1,0:T(8,128)(2,1)S(1)} %slice.16), channel_id=1, source_target_pairs={{0,64},{64,128},{128,192},{192,0},{1,65},{65,129},{129,193},{193,1... | collective-permute-start | bytes 1179656 | tf_op jit(solution)/shard_map/ppermute | solution.py:518
  54.6 4.3 %collective-permute-done.12.refs_8_ = bf16[2,96,1024]{2,1,0:T(8,128)(2,1)S(1)} collective-permute-done((bf16[2,96,1024]{2,1,0:T(8,128)(2,1)S(1)}, bf16[2,96,1024]{2,1,0:T(8,128)(2,1)S(1)}, u32[]{:S(2)}, u32[]{:S(2)}) %collective-permute-start.12) | collective-permute-done | bytes 393248 | tf_op jit(solution)/shard_map/ppermute | solution.py:518
  58.9 1.3 collective-permute-done.6.refs_4_
  60.3 0.1 collective-permute-done.5.refs_3_
  60.4 9.4 %all-gather.3.cloned.1.call-done = bf16[4224,1024]{1,0:T(8,128)(2,1)} async-done(((bf16[264,1024]{1,0:T(8,128)(2,1)}), bf16[4224,1024]{1,0:T(8,128)(2,1)}) %all-gather.3.cloned.1.call-update) | async-done | bytes 8650768 | tf_op jit(solution)/shard_map/all_gather | solution.py:546
  69.9 22.7 %experts.1 = (bf16[4,96,1024]{2,1,0:T(8,128)(2,1)}, bf16[4,96,1024]{2,1,0:T(8,128)(2,1)}, bf16[4,96,1024]{2,1,0:T(8,128)(2,1)}, bf16[2,96,1024]{2,1,0:T(8,128)(2...) custom-call(s32[4]{0:T(128)} %copy-done.11, ...), custom_call_target="tpu_custom_call" | custom-call | flops 10737418240 | bytes 20000000 | tf_op jit(solution)/shard_map/experts/pallas_call | solution.py:45
  92.6 0.3 collective-permute-start.18
  92.9 4.3 %collective-permute-done.18.b = bf16[8,136,1024]{2,1,0:T(8,128)(2,1)S(1)} collective-permute-done((bf16[8,136,1024]{2,1,0:T(8,128)(2,1)}, bf16[8,136,1024]{2,1,0:T(8,128)(2,1)S(1)}, u32[]{:S(2)}, u32[]{:S(2)}) %collective-permute-start.18) | collective-permute-done | bytes 2228256 | tf_op jit(solution)/shard_map/ppermute | solution.py:555
  97.2 1.9 %join.1 = bf16[8,136,1024]{2,1,0:T(8,128)(2,1)} custom-call(bf16[8,136,1024]{2,1,0:T(8,128)(2,1)S(1)} %get-tuple-element.51.a, bf16[8,136,1024]{2,1,0:T(8,128)(2,1)S(1)} %collective-permute-done.18.b), custom_call_target="tpu_custom_call" | custom-call | bytes 1024 | tf_op jit(solution)/shard_map/join/pallas_call | solution.py:45
  99.1 1.5 collective-permute-start.22
  100.7 1.8 %collective-permute-start.23 = (bf16[2,96,1024]{2,1,0:T(8,128)(2,1)}, bf16[2,96,1024]{2,1,0:T(8,128)(2,1)S(1)}, u32[]{:S(2)}, u32[]{:S(2)}) collective-permute-start(bf16[2,96,1024]{2,1,0:T(8,128)(2,1)} %get-tuple-element.65), channel_id=1, source_target_pairs={{0,48},{16,0},{32,16},{48,32},{1,49},{17,1},{33,17},{49,33},{2,50}... | collective-permute-start | bytes 1179656 | tf_op jit(solution)/shard_map/ppermute | solution.py:530
  102.4 0.5 collective-permute-start.14
  103.0 1.5 collective-permute-start.15
  104.5 7.4 %collective-permute-done.22.below = bf16[2,96,1024]{2,1,0:T(8,128)(2,1)S(1)} collective-permute-done((bf16[2,96,1024]{2,1,0:T(8,128)(2,1)}, bf16[2,96,1024]{2,1,0:T(8,128)(2,1)S(1)}, u32[]{:S(2)}, u32[]{:S(2)}) %collective-permute-start.22) | collective-permute-done | bytes 393248 | tf_op jit(solution)/shard_map/ppermute | solution.py:530
  111.9 1.4 fold.3
  113.3 1.5 collective-permute-start.24
  114.8 1.8 %collective-permute-start.25 = (bf16[4,96,1024]{2,1,0:T(8,128)(2,1)S(1)}, bf16[4,96,1024]{2,1,0:T(8,128)(2,1)S(1)}, u32[]{:S(2)}, u32[]{:S(2)}) collective-permute-start(bf16[4,96,1024]{2,1,0:T(8,128)(2,1)S(1)} %get-tuple-element.67), channel_id=1, source_target_pairs={{0,48},{16,0},{32,16},{48,32},{1,49},{17,1},{33,17},{49,33},{2,50}... | collective-permute-start | bytes 2359304 | tf_op jit(solution)/shard_map/ppermute | solution.py:530
  116.6 1.4 fold.2
  118.0 0.6 collective-permute-start.16
  118.6 1.5 collective-permute-start.17
  120.1 13.3 %collective-permute-done.24.below = bf16[4,96,1024]{2,1,0:T(8,128)(2,1)S(1)} collective-permute-done((bf16[4,96,1024]{2,1,0:T(8,128)(2,1)S(1)}, bf16[4,96,1024]{2,1,0:T(8,128)(2,1)S(1)}, u32[]{:S(2)}, u32[]{:S(2)}) %collective-permute-start.24) | collective-permute-done | bytes 786464 | tf_op jit(solution)/shard_map/ppermute | solution.py:530
  133.4 0.3 total.3
  133.7 0.6 collective-permute-start.26
  134.3 2.4 %collective-permute-start.27 = (bf16[96,1024]{1,0:T(8,128)(2,1)S(1)}, bf16[96,1024]{1,0:T(8,128)(2,1)S(1)}, u32[]{:S(2)}, u32[]{:S(2)}) collective-permute-start(bf16[96,1024]{1,0:T(8,128)(2,1)S(1)} %get-tuple-element.70), channel_id=1, source_target_pairs={{0,128},{64,192},{128,0},{192,64},{1,129},{65,193},{129,1},{193,65... | collective-permute-start | bytes 589832 | tf_op jit(solution)/shard_map/ppermute | solution.py:536
  136.7 1.0 collective-permute-done.16.below
  137.7 2.9 %collective-permute-done.17.above = bf16[4,96,1024]{2,1,0:T(8,128)(2,1)S(1)} collective-permute-done((bf16[4,96,1024]{2,1,0:T(8,128)(2,1)S(1)}, bf16[4,96,1024]{2,1,0:T(8,128)(2,1)S(1)}, u32[]{:S(2)}, u32[]{:S(2)}) %collective-permute-start.17) | collective-permute-done | bytes 786464 | tf_op jit(solution)/shard_map/ppermute | solution.py:530
  140.6 0.3 total.2
  140.9 0.1 collective-permute-start.19
  141.0 0.6 collective-permute-start.20
  141.6 0.3 collective-permute-done.26.refs_5_
  141.9 2.3 %collective-permute-start.21 = (bf16[96,1024]{1,0:T(8,128)(2,1)S(1)}, bf16[96,1024]{1,0:T(8,128)(2,1)S(1)}, u32[]{:S(2)}, u32[]{:S(2)}) collective-permute-start(bf16[96,1024]{1,0:T(8,128)(2,1)S(1)} %get-tuple-element.60), channel_id=1, source_target_pairs={{0,48},{16,0},{32,16},{48,32},{1,49},{17,1},{33,17},{49,33},{2,50}... | collective-permute-start | bytes 589832 | tf_op jit(solution)/shard_map/ppermute | solution.py:530
  144.2 1.0 copy-done.8
  145.2 0.7 tokens.1
  145.9 0.3 collective-permute-done.28.refs_7_
  146.3 3.7 %collective-permute-done.19.refs_1_ = bf16[96,1024]{1,0:T(8,128)(2,1)S(1)} collective-permute-done((bf16[96,1024]{1,0:T(8,128)(2,1)S(1)}, bf16[96,1024]{1,0:T(8,128)(2,1)S(1)}, u32[]{:S(2)}, u32[]{:S(2)}) %collective-permute-start.19) | collective-permute-done | bytes 196640 | tf_op jit(solution)/shard_map/ppermute | solution.py:530
  150.0 0.9 collective-permute-done.21.refs_3_
  150.9 1.0 finish.1
  (57 shorter events, 0.3 us)
Async XLA Ops:
  7.2 62.7 %all-gather.3.cloned.1.call-start = ((), (), s32[]{:S(2)}) async-start(), calls=%async_computation.2 | async-start | bytes 9191424 | tf_op jit(solution)/shard_map/all_gather | solution.py:546
  7.3 25.1 %copy-start.11 = (s32[4]{0:T(128)}, s32[4]{0:T(128)S(1)}, u32[]{:S(2)}) copy-start(s32[4]{0:T(128)S(1)} %pad_add_fusion.me_ref.where) | copy-start | bytes 52
  9.8 134.4 %reduce-scatter.2.cloned.1.call-start = ((), (), s32[]{:S(2)}) async-start(), calls=%async_computation.1 | async-start | bytes 2506752 | tf_op jit(solution)/shard_map/reduce_scatter | solution.py:561
  9.9 1.0 copy-start.9
  10.8 0.9 copy-start.10
  11.8 12.1 %collective-permute-start.9 = (bf16[96,1024]{1,0:T(8,128)(2,1)S(1)}, bf16[96,1024]{1,0:T(8,128)(2,1)S(1)}, u32[]{:S(2)}, u32[]{:S(2)}) collective-permute-start(bf16[96,1024]{1,0:T(8,128)(2,1)S(1)} %get-tuple-element.42.own), channel_id=1, source_target_pairs={{0,192},{64,0},{128,64},{192,128},{1,193},{65,1},{129,65},{193,129... | collective-permute-start | bytes 589832 | tf_op jit(solution)/shard_map/ppermute | solution.py:530
  12.6 12.8 %collective-permute-start.8 = (bf16[96,1024]{1,0:T(8,128)(2,1)S(1)}, bf16[96,1024]{1,0:T(8,128)(2,1)S(1)}, u32[]{:S(2)}, u32[]{:S(2)}) collective-permute-start(bf16[96,1024]{1,0:T(8,128)(2,1)S(1)} %get-tuple-element.42.own), channel_id=1, source_target_pairs={{0,128},{64,192},{128,0},{192,64},{1,129},{65,193},{129,1},{193,65... | collective-permute-start | bytes 589832 | tf_op jit(solution)/shard_map/ppermute | solution.py:525
  15.3 10.1 %collective-permute-start.7 = (bf16[96,1024]{1,0:T(8,128)(2,1)S(1)}, bf16[96,1024]{1,0:T(8,128)(2,1)S(1)}, u32[]{:S(2)}, u32[]{:S(2)}) collective-permute-start(bf16[96,1024]{1,0:T(8,128)(2,1)S(1)} %get-tuple-element.42.own), channel_id=1, source_target_pairs={{0,64},{64,128},{128,192},{192,0},{1,65},{65,129},{129,193},{193,1... | collective-permute-start | bytes 589832 | tf_op jit(solution)/shard_map/ppermute | solution.py:530
  15.7 12.4 %collective-permute-start.2 = (bf16[96,1024]{1,0:T(8,128)(2,1)S(1)}, bf16[96,1024]{1,0:T(8,128)(2,1)S(1)}, u32[]{:S(2)}, u32[]{:S(2)}) collective-permute-start(bf16[96,1024]{1,0:T(8,128)(2,1)S(1)} %get-tuple-element.41.own), channel_id=1, source_target_pairs={{0,48},{16,0},{32,16},{48,32},{1,49},{17,1},{33,17},{49,33},{2,50}... | collective-permute-start | bytes 589832 | tf_op jit(solution)/shard_map/ppermute | solution.py:530
  18.5 9.7 %collective-permute-start.1 = (bf16[96,1024]{1,0:T(8,128)(2,1)S(1)}, bf16[96,1024]{1,0:T(8,128)(2,1)S(1)}, u32[]{:S(2)}, u32[]{:S(2)}) collective-permute-start(bf16[96,1024]{1,0:T(8,128)(2,1)S(1)} %get-tuple-element.41.own), channel_id=1, source_target_pairs={{0,32},{16,48},{32,0},{48,16},{1,33},{17,49},{33,1},{49,17},{2,34}... | collective-permute-start | bytes 589832 | tf_op jit(solution)/shard_map/ppermute | solution.py:525
  23.9 7.9 %collective-permute-start = (bf16[96,1024]{1,0:T(8,128)(2,1)S(1)}, bf16[96,1024]{1,0:T(8,128)(2,1)S(1)}, u32[]{:S(2)}, u32[]{:S(2)}) collective-permute-start(bf16[96,1024]{1,0:T(8,128)(2,1)S(1)} %get-tuple-element.41.own), channel_id=1, source_target_pairs={{0,16},{16,32},{32,48},{48,0},{1,17},{17,33},{33,49},{49,1},{2,18}... | collective-permute-start | bytes 589832 | tf_op jit(solution)/shard_map/ppermute | solution.py:530
  26.0 25.9 %copy-start = (bf16[4,96,1024]{2,1,0:T(8,128)(2,1)}, bf16[4,96,1024]{2,1,0:T(8,128)(2,1)S(1)}, u32[]{:S(2)}) copy-start(bf16[4,96,1024]{2,1,0:T(8,128)(2,1)S(1)} %place.3.refs_5_) | copy-start | bytes 2359300
  26.0 18.2 %collective-permute-start.11 = (bf16[4,96,1024]{2,1,0:T(8,128)(2,1)S(1)}, bf16[4,96,1024]{2,1,0:T(8,128)(2,1)S(1)}, u32[]{:S(2)}, u32[]{:S(2)}) collective-permute-start(bf16[4,96,1024]{2,1,0:T(8,128)(2,1)S(1)} %place.3.refs_5_), channel_id=1, source_target_pairs={{0,48},{16,0},{32,16},{48,32},{1,49},{17,1},{33,17},{49,33},{2,50}... | collective-permute-start | bytes 2359304 | tf_op jit(solution)/shard_map/ppermute | solution.py:517
  28.0 20.0 %collective-permute-start.10 = (bf16[4,96,1024]{2,1,0:T(8,128)(2,1)S(1)}, bf16[4,96,1024]{2,1,0:T(8,128)(2,1)S(1)}, u32[]{:S(2)}, u32[]{:S(2)}) collective-permute-start(bf16[4,96,1024]{2,1,0:T(8,128)(2,1)S(1)} %place.3.refs_5_), channel_id=1, source_target_pairs={{0,16},{16,32},{32,48},{48,0},{1,17},{17,33},{33,49},{49,1},{2,18}... | collective-permute-start | bytes 2359304 | tf_op jit(solution)/shard_map/ppermute | solution.py:516
  32.4 37.4 %copy-start.1 = (bf16[4,96,1024]{2,1,0:T(8,128)(2,1)}, bf16[4,96,1024]{2,1,0:T(8,128)(2,1)S(1)}, u32[]{:S(2)}) copy-start(bf16[4,96,1024]{2,1,0:T(8,128)(2,1)S(1)} %place.2.refs_0_) | copy-start | bytes 2359300
  32.4 18.5 %collective-permute-start.4 = (bf16[4,96,1024]{2,1,0:T(8,128)(2,1)S(1)}, bf16[4,96,1024]{2,1,0:T(8,128)(2,1)S(1)}, u32[]{:S(2)}, u32[]{:S(2)}) collective-permute-start(bf16[4,96,1024]{2,1,0:T(8,128)(2,1)S(1)} %place.2.refs_0_), channel_id=1, source_target_pairs={{0,192},{64,0},{128,64},{192,128},{1,193},{65,1},{129,65},{193,129... | collective-permute-start | bytes 2359304 | tf_op jit(solution)/shard_map/ppermute | solution.py:517
  32.5 19.3 %collective-permute-start.3 = (bf16[4,96,1024]{2,1,0:T(8,128)(2,1)S(1)}, bf16[4,96,1024]{2,1,0:T(8,128)(2,1)S(1)}, u32[]{:S(2)}, u32[]{:S(2)}) collective-permute-start(bf16[4,96,1024]{2,1,0:T(8,128)(2,1)S(1)} %place.2.refs_0_), channel_id=1, source_target_pairs={{0,64},{64,128},{128,192},{192,0},{1,65},{65,129},{129,193},{193,1... | collective-permute-start | bytes 2359304 | tf_op jit(solution)/shard_map/ppermute | solution.py:516
  44.2 25.6 %copy-start.12 = (bf16[4,96,1024]{2,1,0:T(8,128)(2,1)}, bf16[4,96,1024]{2,1,0:T(8,128)(2,1)S(1)}, u32[]{:S(2)}) copy-start(bf16[4,96,1024]{2,1,0:T(8,128)(2,1)S(1)} %collective-permute-done.11.refs_7_) | copy-start | bytes 2359300
  44.3 10.3 %collective-permute-start.13 = (bf16[2,96,1024]{2,1,0:T(8,128)(2,1)S(1)}, bf16[2,96,1024]{2,1,0:T(8,128)(2,1)S(1)}, u32[]{:S(2)}, u32[]{:S(2)}) collective-permute-start(bf16[2,96,1024]{2,1,0:T(8,128)(2,1)S(1)} %slice.19), channel_id=1, source_target_pairs={{0,48},{16,0},{32,16},{48,32},{1,49},{17,1},{33,17},{49,33},{2,50}... | collective-permute-start | bytes 1179656 | tf_op jit(solution)/shard_map/ppermute | solution.py:519
  48.0 21.8 %copy-start.13 = (bf16[4,96,1024]{2,1,0:T(8,128)(2,1)}, bf16[4,96,1024]{2,1,0:T(8,128)(2,1)S(1)}, u32[]{:S(2)}) copy-start(bf16[4,96,1024]{2,1,0:T(8,128)(2,1)S(1)} %collective-permute-done.10.refs_6_) | copy-start | bytes 2359300
  48.1 10.9 %collective-permute-start.12 = (bf16[2,96,1024]{2,1,0:T(8,128)(2,1)S(1)}, bf16[2,96,1024]{2,1,0:T(8,128)(2,1)S(1)}, u32[]{:S(2)}, u32[]{:S(2)}) collective-permute-start(bf16[2,96,1024]{2,1,0:T(8,128)(2,1)S(1)} %slice.18), channel_id=1, source_target_pairs={{0,16},{16,32},{32,48},{48,0},{1,17},{17,33},{33,49},{49,1},{2,18}... | collective-permute-start | bytes 1179656 | tf_op jit(solution)/shard_map/ppermute | solution.py:518
  51.0 0.9 copy-start.14
  51.0 9.3 %collective-permute-start.6 = (bf16[2,96,1024]{2,1,0:T(8,128)(2,1)S(1)}, bf16[2,96,1024]{2,1,0:T(8,128)(2,1)S(1)}, u32[]{:S(2)}, u32[]{:S(2)}) collective-permute-start(bf16[2,96,1024]{2,1,0:T(8,128)(2,1)S(1)} %slice.17), channel_id=1, source_target_pairs={{0,192},{64,0},{128,64},{192,128},{1,193},{65,1},{129,65},{193,129... | collective-permute-start | bytes 1179656 | tf_op jit(solution)/shard_map/ppermute | solution.py:519
  51.9 8.4 %copy-start.15 = (bf16[4,96,1024]{2,1,0:T(8,128)(2,1)}, bf16[4,96,1024]{2,1,0:T(8,128)(2,1)S(1)}, u32[]{:S(2)}) copy-start(bf16[4,96,1024]{2,1,0:T(8,128)(2,1)S(1)} %collective-permute-done.3.refs_1_) | copy-start | bytes 2359300
  51.9 8.5 %collective-permute-start.5 = (bf16[2,96,1024]{2,1,0:T(8,128)(2,1)S(1)}, bf16[2,96,1024]{2,1,0:T(8,128)(2,1)}, u32[]{:S(2)}, u32[]{:S(2)}) collective-permute-start(bf16[2,96,1024]{2,1,0:T(8,128)(2,1)S(1)} %slice.16), channel_id=1, source_target_pairs={{0,64},{64,128},{128,192},{192,0},{1,65},{65,129},{129,193},{193,1... | collective-permute-start | bytes 1179656 | tf_op jit(solution)/shard_map/ppermute | solution.py:518
  54.6 15.2 %copy-start.17 = (bf16[2,96,1024]{2,1,0:T(8,128)(2,1)}, bf16[2,96,1024]{2,1,0:T(8,128)(2,1)S(1)}, u32[]{:S(2)}) copy-start(bf16[2,96,1024]{2,1,0:T(8,128)(2,1)S(1)} %collective-permute-done.13.refs_9_) | copy-start | bytes 1179652
  58.9 10.9 %copy-start.18 = (bf16[2,96,1024]{2,1,0:T(8,128)(2,1)}, bf16[2,96,1024]{2,1,0:T(8,128)(2,1)S(1)}, u32[]{:S(2)}) copy-start(bf16[2,96,1024]{2,1,0:T(8,128)(2,1)S(1)} %collective-permute-done.12.refs_8_) | copy-start | bytes 1179652
  60.3 9.6 %copy-start.19 = (bf16[2,96,1024]{2,1,0:T(8,128)(2,1)}, bf16[2,96,1024]{2,1,0:T(8,128)(2,1)S(1)}, u32[]{:S(2)}) copy-start(bf16[2,96,1024]{2,1,0:T(8,128)(2,1)S(1)} %collective-permute-done.6.refs_4_) | copy-start | bytes 1179652
  92.6 4.6 %collective-permute-start.18 = (bf16[8,136,1024]{2,1,0:T(8,128)(2,1)}, bf16[8,136,1024]{2,1,0:T(8,128)(2,1)S(1)}, u32[]{:S(2)}, u32[]{:S(2)}) collective-permute-start(bf16[8,136,1024]{2,1,0:T(8,128)(2,1)} %get-tuple-element.52), channel_id=1, source_target_pairs={{0,1},{1,0},{2,3},{3,2},{4,5},{5,4},{6,7},{7,6},{8,9},{9,8},{10,11... | collective-permute-start | bytes 6684680 | tf_op jit(solution)/shard_map/ppermute | solution.py:555
  99.1 3.9 %copy-start.16 = (bf16[2,96,1024]{2,1,0:T(8,128)(2,1)S(1)}, bf16[2,96,1024]{2,1,0:T(8,128)(2,1)}, u32[]{:S(2)}) copy-start(bf16[2,96,1024]{2,1,0:T(8,128)(2,1)} %get-tuple-element.47) | copy-start | bytes 1179652
  99.1 12.8 %copy-start.6 = (bf16[4,96,1024]{2,1,0:T(8,128)(2,1)S(1)}, bf16[4,96,1024]{2,1,0:T(8,128)(2,1)}, u32[]{:S(2)}) copy-start(bf16[4,96,1024]{2,1,0:T(8,128)(2,1)} %get-tuple-element.62.up) | copy-start | bytes 2359300
  99.1 12.8 %copy-start.7 = (bf16[4,96,1024]{2,1,0:T(8,128)(2,1)S(1)}, bf16[4,96,1024]{2,1,0:T(8,128)(2,1)}, u32[]{:S(2)}) copy-start(bf16[4,96,1024]{2,1,0:T(8,128)(2,1)} %get-tuple-element.63.down) | copy-start | bytes 2359300
  99.1 17.5 %copy-start.4 = (bf16[4,96,1024]{2,1,0:T(8,128)(2,1)S(1)}, bf16[4,96,1024]{2,1,0:T(8,128)(2,1)}, u32[]{:S(2)}) copy-start(bf16[4,96,1024]{2,1,0:T(8,128)(2,1)} %get-tuple-element.44.up) | copy-start | bytes 2359300
  99.1 17.5 %copy-start.5 = (bf16[4,96,1024]{2,1,0:T(8,128)(2,1)S(1)}, bf16[4,96,1024]{2,1,0:T(8,128)(2,1)}, u32[]{:S(2)}) copy-start(bf16[4,96,1024]{2,1,0:T(8,128)(2,1)} %get-tuple-element.45.down) | copy-start | bytes 2359300
  99.1 12.8 %collective-permute-start.22 = (bf16[2,96,1024]{2,1,0:T(8,128)(2,1)}, bf16[2,96,1024]{2,1,0:T(8,128)(2,1)S(1)}, u32[]{:S(2)}, u32[]{:S(2)}) collective-permute-start(bf16[2,96,1024]{2,1,0:T(8,128)(2,1)} %get-tuple-element.64), channel_id=1, source_target_pairs={{0,16},{16,32},{32,48},{48,0},{1,17},{17,33},{33,49},{49,1},{2,18}... | collective-permute-start | bytes 1179656 | tf_op jit(solution)/shard_map/ppermute | solution.py:530
  100.7 11.2 %collective-permute-start.23 = (bf16[2,96,1024]{2,1,0:T(8,128)(2,1)}, bf16[2,96,1024]{2,1,0:T(8,128)(2,1)S(1)}, u32[]{:S(2)}, u32[]{:S(2)}) collective-permute-start(bf16[2,96,1024]{2,1,0:T(8,128)(2,1)} %get-tuple-element.65), channel_id=1, source_target_pairs={{0,48},{16,0},{32,16},{48,32},{1,49},{17,1},{33,17},{49,33},{2,50}... | collective-permute-start | bytes 1179656 | tf_op jit(solution)/shard_map/ppermute | solution.py:530
  102.4 14.2 %collective-permute-start.14 = (bf16[2,96,1024]{2,1,0:T(8,128)(2,1)}, bf16[2,96,1024]{2,1,0:T(8,128)(2,1)S(1)}, u32[]{:S(2)}, u32[]{:S(2)}) collective-permute-start(bf16[2,96,1024]{2,1,0:T(8,128)(2,1)} %get-tuple-element.46), channel_id=1, source_target_pairs={{0,64},{64,128},{128,192},{192,0},{1,65},{65,129},{129,193},{193,1... | collective-permute-start | bytes 1179656 | tf_op jit(solution)/shard_map/ppermute | solution.py:530
  103.0 13.7 %collective-permute-start.15 = (bf16[2,96,1024]{2,1,0:T(8,128)(2,1)S(1)}, bf16[2,96,1024]{2,1,0:T(8,128)(2,1)S(1)}, u32[]{:S(2)}, u32[]{:S(2)}) collective-permute-start(bf16[2,96,1024]{2,1,0:T(8,128)(2,1)S(1)} %copy-done.16), channel_id=1, source_target_pairs={{0,192},{64,0},{128,64},{192,128},{1,193},{65,1},{129,65},{193,129... | collective-permute-start | bytes 1179656 | tf_op jit(solution)/shard_map/ppermute | solution.py:530
  111.9 21.5 %copy-start.3 = (bf16[4,96,1024]{2,1,0:T(8,128)(2,1)S(1)}, bf16[4,96,1024]{2,1,0:T(8,128)(2,1)}, u32[]{:S(2)}) copy-start(bf16[4,96,1024]{2,1,0:T(8,128)(2,1)} %get-tuple-element.61.own) | copy-start | bytes 2359300
  113.3 20.1 %collective-permute-start.24 = (bf16[4,96,1024]{2,1,0:T(8,128)(2,1)S(1)}, bf16[4,96,1024]{2,1,0:T(8,128)(2,1)S(1)}, u32[]{:S(2)}, u32[]{:S(2)}) collective-permute-start(bf16[4,96,1024]{2,1,0:T(8,128)(2,1)S(1)} %get-tuple-element.66), channel_id=1, source_target_pairs={{0,16},{16,32},{32,48},{48,0},{1,17},{17,33},{33,49},{49,1},{2,18}... | collective-permute-start | bytes 2359304 | tf_op jit(solution)/shard_map/ppermute | solution.py:530
  114.8 18.6 %collective-permute-start.25 = (bf16[4,96,1024]{2,1,0:T(8,128)(2,1)S(1)}, bf16[4,96,1024]{2,1,0:T(8,128)(2,1)S(1)}, u32[]{:S(2)}, u32[]{:S(2)}) collective-permute-start(bf16[4,96,1024]{2,1,0:T(8,128)(2,1)S(1)} %get-tuple-element.67), channel_id=1, source_target_pairs={{0,48},{16,0},{32,16},{48,32},{1,49},{17,1},{33,17},{49,33},{2,50}... | collective-permute-start | bytes 2359304 | tf_op jit(solution)/shard_map/ppermute | solution.py:530
  116.6 24.0 %copy-start.2 = (bf16[4,96,1024]{2,1,0:T(8,128)(2,1)S(1)}, bf16[4,96,1024]{2,1,0:T(8,128)(2,1)}, u32[]{:S(2)}) copy-start(bf16[4,96,1024]{2,1,0:T(8,128)(2,1)} %get-tuple-element.43.own) | copy-start | bytes 2359300
  118.0 19.7 %collective-permute-start.16 = (bf16[4,96,1024]{2,1,0:T(8,128)(2,1)S(1)}, bf16[4,96,1024]{2,1,0:T(8,128)(2,1)S(1)}, u32[]{:S(2)}, u32[]{:S(2)}) collective-permute-start(bf16[4,96,1024]{2,1,0:T(8,128)(2,1)S(1)} %get-tuple-element.48), channel_id=1, source_target_pairs={{0,64},{64,128},{128,192},{192,0},{1,65},{65,129},{129,193},{193,1... | collective-permute-start | bytes 2359304 | tf_op jit(solution)/shard_map/ppermute | solution.py:530
  118.6 22.0 %collective-permute-start.17 = (bf16[4,96,1024]{2,1,0:T(8,128)(2,1)S(1)}, bf16[4,96,1024]{2,1,0:T(8,128)(2,1)S(1)}, u32[]{:S(2)}, u32[]{:S(2)}) collective-permute-start(bf16[4,96,1024]{2,1,0:T(8,128)(2,1)S(1)} %get-tuple-element.49), channel_id=1, source_target_pairs={{0,192},{64,0},{128,64},{192,128},{1,193},{65,1},{129,65},{193,129... | collective-permute-start | bytes 2359304 | tf_op jit(solution)/shard_map/ppermute | solution.py:530
  133.7 8.2 %collective-permute-start.26 = (bf16[96,1024]{1,0:T(8,128)(2,1)S(1)}, bf16[96,1024]{1,0:T(8,128)(2,1)S(1)}, u32[]{:S(2)}, u32[]{:S(2)}) collective-permute-start(bf16[96,1024]{1,0:T(8,128)(2,1)S(1)} %get-tuple-element.69), channel_id=1, source_target_pairs={{0,64},{64,128},{128,192},{192,0},{1,65},{65,129},{129,193},{193,1... | collective-permute-start | bytes 589832 | tf_op jit(solution)/shard_map/ppermute | solution.py:530
  134.3 11.6 %collective-permute-start.27 = (bf16[96,1024]{1,0:T(8,128)(2,1)S(1)}, bf16[96,1024]{1,0:T(8,128)(2,1)S(1)}, u32[]{:S(2)}, u32[]{:S(2)}) collective-permute-start(bf16[96,1024]{1,0:T(8,128)(2,1)S(1)} %get-tuple-element.70), channel_id=1, source_target_pairs={{0,128},{64,192},{128,0},{192,64},{1,129},{65,193},{129,1},{193,65... | collective-permute-start | bytes 589832 | tf_op jit(solution)/shard_map/ppermute | solution.py:536
  136.7 9.5 %collective-permute-start.28 = (bf16[96,1024]{1,0:T(8,128)(2,1)S(1)}, bf16[96,1024]{1,0:T(8,128)(2,1)S(1)}, u32[]{:S(2)}, u32[]{:S(2)}) collective-permute-start(bf16[96,1024]{1,0:T(8,128)(2,1)S(1)} %get-tuple-element.71), channel_id=1, source_target_pairs={{0,192},{64,0},{128,64},{192,128},{1,193},{65,1},{129,65},{193,129... | collective-permute-start | bytes 589832 | tf_op jit(solution)/shard_map/ppermute | solution.py:530
  140.9 9.1 %collective-permute-start.19 = (bf16[96,1024]{1,0:T(8,128)(2,1)S(1)}, bf16[96,1024]{1,0:T(8,128)(2,1)S(1)}, u32[]{:S(2)}, u32[]{:S(2)}) collective-permute-start(bf16[96,1024]{1,0:T(8,128)(2,1)S(1)} %get-tuple-element.58), channel_id=1, source_target_pairs={{0,16},{16,32},{32,48},{48,0},{1,17},{17,33},{33,49},{49,1},{2,18}... | collective-permute-start | bytes 589832 | tf_op jit(solution)/shard_map/ppermute | solution.py:530
  141.0 9.0 %collective-permute-start.20 = (bf16[96,1024]{1,0:T(8,128)(2,1)S(1)}, bf16[96,1024]{1,0:T(8,128)(2,1)S(1)}, u32[]{:S(2)}, u32[]{:S(2)}) collective-permute-start(bf16[96,1024]{1,0:T(8,128)(2,1)S(1)} %get-tuple-element.59), channel_id=1, source_target_pairs={{0,32},{16,48},{32,0},{48,16},{1,33},{17,49},{33,1},{49,17},{2,34}... | collective-permute-start | bytes 589832 | tf_op jit(solution)/shard_map/ppermute | solution.py:536
  141.9 9.0 %collective-permute-start.21 = (bf16[96,1024]{1,0:T(8,128)(2,1)S(1)}, bf16[96,1024]{1,0:T(8,128)(2,1)S(1)}, u32[]{:S(2)}, u32[]{:S(2)}) collective-permute-start(bf16[96,1024]{1,0:T(8,128)(2,1)S(1)} %get-tuple-element.60), channel_id=1, source_target_pairs={{0,48},{16,0},{32,16},{48,32},{1,49},{17,1},{33,17},{49,33},{2,50}... | collective-permute-start | bytes 589832 | tf_op jit(solution)/shard_map/ppermute | solution.py:530
  144.2 1.0 copy-start.8
Sparse Core Ops, SparseCore 0:
  10.0 59.8 all-gather.2
  99.2 41.1 reduce-scatter.1

commit v3 on v2

--- a/solution.py
+++ b/solution.py
@@ -142,7 +142,7 @@
 
 
 TILE = 256
-BACK_TILE = 512
+BACK_TILE = 1024
 START_AT = 2
 
 
@@ -327,7 +327,7 @@
         route_pair(p, first, pay, x, dy, gate, sel, upper, slot)
         return 0
 
-    lax.fori_loop(0, CHIPS, pair_in, 0)
+    lax.fori_loop(0, CHIPS, pair_in, 0, unroll=2)
 
     def one(e, _):
         for n in range(10):
@@ -369,7 +369,7 @@
             copy.start()
         return 0
 
-    lax.fori_loop(0, CHIPS, pair_out, 0)
+    lax.fori_loop(0, CHIPS, pair_out, 0, unroll=2)
     outs = [copy for p in range(CHIPS) for copy in sends(p)]
     for e in range(2):
         outs += stores_of(held.at[e], grads[e], gsem.at[e])

time: 159 us -> 159 us (level)
  no operation moved by 1% of the time
where the time goes in v3:
time: 159 us
  waiting for transfers between devices  69.5 us (44%)
  starting transfers between devices  38 us (24%)
  Pallas kernels  33.1 us (21%)
  between operations  14.3 us (9%)
  local copies, waits for them, and re-layouts  3.74 us (2%)
    ppermute x16, waiting for transfers between devices, swap(): return (lax.ppermute(a, axis, UP), lax.ppermute(b, axis, DOWN))  38.3 us
    pallas_call x12, Pallas kernels, call(): pl.pallas_call(kernel, name=name, in_specs=[smem] * scalars + (specs or [...  33.1 us
    ppermute x16, starting transfers between devices, swap(): return (lax.ppermute(a, axis, UP), lax.ppermute(b, axis, DOWN))  19.4 us
    ppermute x2, waiting for transfers between devices, gather_ring(): above = lax.ppermute(block, axis, DOWN)  11.3 us
    all_gather x1, waiting for transfers between devices, body(): pay = lax.all_gather(pay, ('z', 'core'), axis=0, tiled=False)  9.45 us
    ppermute x2, waiting for transfers between devices, gather_ring(): far_a = lax.ppermute(below[:half], axis, UP)  4.43 us
    ppermute x1, waiting for transfers between devices, body(): got = lax.ppermute(send, 'core', [(0, 1), (1, 0)])  4.31 us
    unnamed x40, local copies, waits for them, and re-layouts  3.64 us
  transfers between devices with their start and end apart: 31, of which 18 were waited for; matrix products, arithmetic and copies ran while one was open for 0% of the time, Pallas kernels for 3%

profile of v3, /device:TPU:24, one launch (start us, length us, event | category | flops | bytes accessed | tf_op | source)
XLA Modules:
  0.0 158.8 jit_solution(13784592969939793635)
XLA Ops:
  7.2 0.0 all-gather.3.cloned.1.call-start
  7.2 0.1 pad_add_fusion.me_ref.where
  7.3 2.5 %pack.1 = bf16[264,1024]{1,0:T(8,128)(2,1)} custom-call(bf16[128,1024]{1,0:T(8,128)(2,1)} %tok.1, bf16[128,1024]{1,0:T(8,128)(2,1)} %cot.1, s32[8,128]{1,0:T(8,128)} %bitcast.9, bf16[8,128]{1,0:T(8,128)(2,1)} %bitcast.10), custom_call_target="tpu_custom_call" | custom-call | bytes 2000000 | tf_op jit(solution)/shard_map/pack/pallas_call | solution.py:45
  9.8 0.0 reduce-scatter.2.cloned.1.call-start
  9.9 0.9 copy-done.9
  10.8 0.9 copy-done.10
  11.8 0.8 collective-permute-start.9
  12.6 2.7 %collective-permute-start.8 = (bf16[96,1024]{1,0:T(8,128)(2,1)S(1)}, bf16[96,1024]{1,0:T(8,128)(2,1)S(1)}, u32[]{:S(2)}, u32[]{:S(2)}) collective-permute-start(bf16[96,1024]{1,0:T(8,128)(2,1)S(1)} %get-tuple-element.42.own), channel_id=1, source_target_pairs={{0,128},{64,192},{128,0},{192,64},{1,129},{65,193},{129,1},{193,65... | collective-permute-start | bytes 589832 | tf_op jit(solution)/shard_map/ppermute | solution.py:525
  15.3 0.4 collective-permute-start.7
  15.7 2.8 %collective-permute-start.2 = (bf16[96,1024]{1,0:T(8,128)(2,1)S(1)}, bf16[96,1024]{1,0:T(8,128)(2,1)S(1)}, u32[]{:S(2)}, u32[]{:S(2)}) collective-permute-start(bf16[96,1024]{1,0:T(8,128)(2,1)S(1)} %get-tuple-element.41.own), channel_id=1, source_target_pairs={{0,48},{16,0},{32,16},{48,32},{1,49},{17,1},{33,17},{49,33},{2,50}... | collective-permute-start | bytes 589832 | tf_op jit(solution)/shard_map/ppermute | solution.py:530
  18.5 0.8 collective-permute-start.1
  19.3 4.6 %collective-permute-done.9.above = bf16[96,1024]{1,0:T(8,128)(2,1)S(1)} collective-permute-done((bf16[96,1024]{1,0:T(8,128)(2,1)S(1)}, bf16[96,1024]{1,0:T(8,128)(2,1)S(1)}, u32[]{:S(2)}, u32[]{:S(2)}) %collective-permute-start.9) | collective-permute-done | bytes 196640 | tf_op jit(solution)/shard_map/ppermute | solution.py:530
  23.9 1.5 collective-permute-start
  25.4 0.6 place.3.refs_5_
  26.0 2.0 %collective-permute-start.11 = (bf16[4,96,1024]{2,1,0:T(8,128)(2,1)S(1)}, bf16[4,96,1024]{2,1,0:T(8,128)(2,1)S(1)}, u32[]{:S(2)}, u32[]{:S(2)}) collective-permute-start(bf16[4,96,1024]{2,1,0:T(8,128)(2,1)S(1)} %place.3.refs_5_), channel_id=1, source_target_pairs={{0,48},{16,0},{32,16},{48,32},{1,49},{17,1},{33,17},{49,33},{2,50}... | collective-permute-start | bytes 2359304 | tf_op jit(solution)/shard_map/ppermute | solution.py:517
  28.0 0.1 collective-permute-start.10
  28.1 3.7 %collective-permute-done.below = bf16[96,1024]{1,0:T(8,128)(2,1)S(1)} collective-permute-done((bf16[96,1024]{1,0:T(8,128)(2,1)S(1)}, bf16[96,1024]{1,0:T(8,128)(2,1)S(1)}, u32[]{:S(2)}, u32[]{:S(2)}) %collective-permute-start) | collective-permute-done | bytes 196640 | tf_op jit(solution)/shard_map/ppermute | solution.py:530
  31.8 0.6 place.2.refs_0_
  32.4 0.1 collective-permute-start.4
  32.5 3.2 %collective-permute-start.3 = (bf16[4,96,1024]{2,1,0:T(8,128)(2,1)S(1)}, bf16[4,96,1024]{2,1,0:T(8,128)(2,1)S(1)}, u32[]{:S(2)}, u32[]{:S(2)}) collective-permute-start(bf16[4,96,1024]{2,1,0:T(8,128)(2,1)S(1)} %place.2.refs_0_), channel_id=1, source_target_pairs={{0,64},{64,128},{128,192},{192,0},{1,65},{65,129},{129,193},{193,1... | collective-permute-start | bytes 2359304 | tf_op jit(solution)/shard_map/ppermute | solution.py:516
  35.7 8.5 %collective-permute-done.11.refs_7_ = bf16[4,96,1024]{2,1,0:T(8,128)(2,1)S(1)} collective-permute-done((bf16[4,96,1024]{2,1,0:T(8,128)(2,1)S(1)}, bf16[4,96,1024]{2,1,0:T(8,128)(2,1)S(1)}, u32[]{:S(2)}, u32[]{:S(2)}) %collective-permute-start.11) | collective-permute-done | bytes 786464 | tf_op jit(solution)/shard_map/ppermute | solution.py:517
  44.3 3.4 %collective-permute-start.13 = (bf16[2,96,1024]{2,1,0:T(8,128)(2,1)S(1)}, bf16[2,96,1024]{2,1,0:T(8,128)(2,1)S(1)}, u32[]{:S(2)}, u32[]{:S(2)}) collective-permute-start(bf16[2,96,1024]{2,1,0:T(8,128)(2,1)S(1)} %slice.19), channel_id=1, source_target_pairs={{0,48},{16,0},{32,16},{48,32},{1,49},{17,1},{33,17},{49,33},{2,50}... | collective-permute-start | bytes 1179656 | tf_op jit(solution)/shard_map/ppermute | solution.py:519
  47.7 0.3 collective-permute-done.10.refs_6_
  48.1 0.1 collective-permute-start.12
  48.2 2.8 %collective-permute-done.4.refs_2_ = bf16[4,96,1024]{2,1,0:T(8,128)(2,1)S(1)} collective-permute-done((bf16[4,96,1024]{2,1,0:T(8,128)(2,1)S(1)}, bf16[4,96,1024]{2,1,0:T(8,128)(2,1)S(1)}, u32[]{:S(2)}, u32[]{:S(2)}) %collective-permute-start.4) | collective-permute-done | bytes 786464 | tf_op jit(solution)/shard_map/ppermute | solution.py:517
  51.0 0.1 collective-permute-start.6
  51.1 0.8 copy-done.14
  51.9 2.7 %collective-permute-start.5 = (bf16[2,96,1024]{2,1,0:T(8,128)(2,1)S(1)}, bf16[2,96,1024]{2,1,0:T(8,128)(2,1)}, u32[]{:S(2)}, u32[]{:S(2)}) collective-permute-start(bf16[2,96,1024]{2,1,0:T(8,128)(2,1)S(1)} %slice.16), channel_id=1, source_target_pairs={{0,64},{64,128},{128,192},{192,0},{1,65},{65,129},{129,193},{193,1... | collective-permute-start | bytes 1179656 | tf_op jit(solution)/shard_map/ppermute | solution.py:518
  54.6 4.3 %collective-permute-done.12.refs_8_ = bf16[2,96,1024]{2,1,0:T(8,128)(2,1)S(1)} collective-permute-done((bf16[2,96,1024]{2,1,0:T(8,128)(2,1)S(1)}, bf16[2,96,1024]{2,1,0:T(8,128)(2,1)S(1)}, u32[]{:S(2)}, u32[]{:S(2)}) %collective-permute-start.12) | collective-permute-done | bytes 393248 | tf_op jit(solution)/shard_map/ppermute | solution.py:518
  58.9 1.3 collective-permute-done.6.refs_4_
  60.3 0.1 collective-permute-done.5.refs_3_
  60.4 9.4 %all-gather.3.cloned.1.call-done = bf16[4224,1024]{1,0:T(8,128)(2,1)} async-done(((bf16[264,1024]{1,0:T(8,128)(2,1)}), bf16[4224,1024]{1,0:T(8,128)(2,1)}) %all-gather.3.cloned.1.call-update) | async-done | bytes 8650768 | tf_op jit(solution)/shard_map/all_gather | solution.py:546
  69.9 22.5 %experts.1 = (bf16[4,96,1024]{2,1,0:T(8,128)(2,1)}, bf16[4,96,1024]{2,1,0:T(8,128)(2,1)}, bf16[4,96,1024]{2,1,0:T(8,128)(2,1)}, bf16[2,96,1024]{2,1,0:T(8,128)(2...) custom-call(s32[4]{0:T(128)} %copy-done.11, ...), custom_call_target="tpu_custom_call" | custom-call | flops 10737418240 | bytes 20000000 | tf_op jit(solution)/shard_map/experts/pallas_call | solution.py:45
  92.4 0.3 collective-permute-start.18
  92.7 4.3 %collective-permute-done.18.b = bf16[8,136,1024]{2,1,0:T(8,128)(2,1)S(1)} collective-permute-done((bf16[8,136,1024]{2,1,0:T(8,128)(2,1)}, bf16[8,136,1024]{2,1,0:T(8,128)(2,1)S(1)}, u32[]{:S(2)}, u32[]{:S(2)}) %collective-permute-start.18) | collective-permute-done | bytes 2228256 | tf_op jit(solution)/shard_map/ppermute | solution.py:555
  97.0 1.9 %join.1 = bf16[8,136,1024]{2,1,0:T(8,128)(2,1)} custom-call(bf16[8,136,1024]{2,1,0:T(8,128)(2,1)S(1)} %get-tuple-element.51.a, bf16[8,136,1024]{2,1,0:T(8,128)(2,1)S(1)} %collective-permute-done.18.b), custom_call_target="tpu_custom_call" | custom-call | bytes 1024 | tf_op jit(solution)/shard_map/join/pallas_call | solution.py:45
  98.9 1.5 collective-permute-start.22
  100.5 1.8 %collective-permute-start.23 = (bf16[2,96,1024]{2,1,0:T(8,128)(2,1)}, bf16[2,96,1024]{2,1,0:T(8,128)(2,1)S(1)}, u32[]{:S(2)}, u32[]{:S(2)}) collective-permute-start(bf16[2,96,1024]{2,1,0:T(8,128)(2,1)} %get-tuple-element.65), channel_id=1, source_target_pairs={{0,48},{16,0},{32,16},{48,32},{1,49},{17,1},{33,17},{49,33},{2,50}... | collective-permute-start | bytes 1179656 | tf_op jit(solution)/shard_map/ppermute | solution.py:530
  102.3 0.5 collective-permute-start.14
  102.8 1.5 collective-permute-start.15
  104.3 7.4 %collective-permute-done.22.below = bf16[2,96,1024]{2,1,0:T(8,128)(2,1)S(1)} collective-permute-done((bf16[2,96,1024]{2,1,0:T(8,128)(2,1)}, bf16[2,96,1024]{2,1,0:T(8,128)(2,1)S(1)}, u32[]{:S(2)}, u32[]{:S(2)}) %collective-permute-start.22) | collective-permute-done | bytes 393248 | tf_op jit(solution)/shard_map/ppermute | solution.py:530
  111.7 1.4 fold.3
  113.1 1.7 %collective-permute-start.24 = (bf16[4,96,1024]{2,1,0:T(8,128)(2,1)S(1)}, bf16[4,96,1024]{2,1,0:T(8,128)(2,1)S(1)}, u32[]{:S(2)}, u32[]{:S(2)}) collective-permute-start(bf16[4,96,1024]{2,1,0:T(8,128)(2,1)S(1)} %get-tuple-element.66), channel_id=1, source_target_pairs={{0,16},{16,32},{32,48},{48,0},{1,17},{17,33},{33,49},{49,1},{2,18}... | collective-permute-start | bytes 2359304 | tf_op jit(solution)/shard_map/ppermute | solution.py:530
  114.8 1.8 %collective-permute-start.25 = (bf16[4,96,1024]{2,1,0:T(8,128)(2,1)S(1)}, bf16[4,96,1024]{2,1,0:T(8,128)(2,1)S(1)}, u32[]{:S(2)}, u32[]{:S(2)}) collective-permute-start(bf16[4,96,1024]{2,1,0:T(8,128)(2,1)S(1)} %get-tuple-element.67), channel_id=1, source_target_pairs={{0,48},{16,0},{32,16},{48,32},{1,49},{17,1},{33,17},{49,33},{2,50}... | collective-permute-start | bytes 2359304 | tf_op jit(solution)/shard_map/ppermute | solution.py:530
  116.7 1.4 fold.2
  118.1 0.6 collective-permute-start.16
  118.6 1.5 collective-permute-start.17
  120.2 13.3 %collective-permute-done.24.below = bf16[4,96,1024]{2,1,0:T(8,128)(2,1)S(1)} collective-permute-done((bf16[4,96,1024]{2,1,0:T(8,128)(2,1)S(1)}, bf16[4,96,1024]{2,1,0:T(8,128)(2,1)S(1)}, u32[]{:S(2)}, u32[]{:S(2)}) %collective-permute-start.24) | collective-permute-done | bytes 786464 | tf_op jit(solution)/shard_map/ppermute | solution.py:530
  133.5 0.3 total.3
  133.8 0.6 collective-permute-start.26
  134.4 2.4 %collective-permute-start.27 = (bf16[96,1024]{1,0:T(8,128)(2,1)S(1)}, bf16[96,1024]{1,0:T(8,128)(2,1)S(1)}, u32[]{:S(2)}, u32[]{:S(2)}) collective-permute-start(bf16[96,1024]{1,0:T(8,128)(2,1)S(1)} %get-tuple-element.70), channel_id=1, source_target_pairs={{0,128},{64,192},{128,0},{192,64},{1,129},{65,193},{129,1},{193,65... | collective-permute-start | bytes 589832 | tf_op jit(solution)/shard_map/ppermute | solution.py:536
  136.8 1.0 collective-permute-done.16.below
  137.8 2.9 %collective-permute-done.17.above = bf16[4,96,1024]{2,1,0:T(8,128)(2,1)S(1)} collective-permute-done((bf16[4,96,1024]{2,1,0:T(8,128)(2,1)S(1)}, bf16[4,96,1024]{2,1,0:T(8,128)(2,1)S(1)}, u32[]{:S(2)}, u32[]{:S(2)}) %collective-permute-start.17) | collective-permute-done | bytes 786464 | tf_op jit(solution)/shard_map/ppermute | solution.py:530
  140.7 0.3 total.2
  141.0 0.1 collective-permute-start.19
  141.1 0.6 collective-permute-start.20
  141.6 0.4 collective-permute-done.26.refs_5_
  142.0 2.3 %collective-permute-start.21 = (bf16[96,1024]{1,0:T(8,128)(2,1)S(1)}, bf16[96,1024]{1,0:T(8,128)(2,1)S(1)}, u32[]{:S(2)}, u32[]{:S(2)}) collective-permute-start(bf16[96,1024]{1,0:T(8,128)(2,1)S(1)} %get-tuple-element.60), channel_id=1, source_target_pairs={{0,48},{16,0},{32,16},{48,32},{1,49},{17,1},{33,17},{49,33},{2,50}... | collective-permute-start | bytes 589832 | tf_op jit(solution)/shard_map/ppermute | solution.py:530
  144.3 1.0 copy-done.8
  145.2 0.7 tokens.1
  146.0 0.3 collective-permute-done.28.refs_7_
  146.3 3.7 %collective-permute-done.19.refs_1_ = bf16[96,1024]{1,0:T(8,128)(2,1)S(1)} collective-permute-done((bf16[96,1024]{1,0:T(8,128)(2,1)S(1)}, bf16[96,1024]{1,0:T(8,128)(2,1)S(1)}, u32[]{:S(2)}, u32[]{:S(2)}) %collective-permute-start.19) | collective-permute-done | bytes 196640 | tf_op jit(solution)/shard_map/ppermute | solution.py:530
  150.0 0.9 collective-permute-done.21.refs_3_
  150.9 1.0 finish.1
  (57 shorter events, 0.3 us)
Async XLA Ops:
  7.2 62.7 %all-gather.3.cloned.1.call-start = ((), (), s32[]{:S(2)}) async-start(), calls=%async_computation.2 | async-start | bytes 9191424 | tf_op jit(solution)/shard_map/all_gather | solution.py:546
  7.3 25.1 %copy-start.11 = (s32[4]{0:T(128)}, s32[4]{0:T(128)S(1)}, u32[]{:S(2)}) copy-start(s32[4]{0:T(128)S(1)} %pad_add_fusion.me_ref.where) | copy-start | bytes 52
  9.8 134.4 %reduce-scatter.2.cloned.1.call-start = ((), (), s32[]{:S(2)}) async-start(), calls=%async_computation.1 | async-start | bytes 2506752 | tf_op jit(solution)/shard_map/reduce_scatter | solution.py:561
  9.9 1.0 copy-start.9
  10.8 0.9 copy-start.10
  11.8 12.1 %collective-permute-start.9 = (bf16[96,1024]{1,0:T(8,128)(2,1)S(1)}, bf16[96,1024]{1,0:T(8,128)(2,1)S(1)}, u32[]{:S(2)}, u32[]{:S(2)}) collective-permute-start(bf16[96,1024]{1,0:T(8,128)(2,1)S(1)} %get-tuple-element.42.own), channel_id=1, source_target_pairs={{0,192},{64,0},{128,64},{192,128},{1,193},{65,1},{129,65},{193,129... | collective-permute-start | bytes 589832 | tf_op jit(solution)/shard_map/ppermute | solution.py:530
  12.6 12.8 %collective-permute-start.8 = (bf16[96,1024]{1,0:T(8,128)(2,1)S(1)}, bf16[96,1024]{1,0:T(8,128)(2,1)S(1)}, u32[]{:S(2)}, u32[]{:S(2)}) collective-permute-start(bf16[96,1024]{1,0:T(8,128)(2,1)S(1)} %get-tuple-element.42.own), channel_id=1, source_target_pairs={{0,128},{64,192},{128,0},{192,64},{1,129},{65,193},{129,1},{193,65... | collective-permute-start | bytes 589832 | tf_op jit(solution)/shard_map/ppermute | solution.py:525
  15.3 10.1 %collective-permute-start.7 = (bf16[96,1024]{1,0:T(8,128)(2,1)S(1)}, bf16[96,1024]{1,0:T(8,128)(2,1)S(1)}, u32[]{:S(2)}, u32[]{:S(2)}) collective-permute-start(bf16[96,1024]{1,0:T(8,128)(2,1)S(1)} %get-tuple-element.42.own), channel_id=1, source_target_pairs={{0,64},{64,128},{128,192},{192,0},{1,65},{65,129},{129,193},{193,1... | collective-permute-start | bytes 589832 | tf_op jit(solution)/shard_map/ppermute | solution.py:530
  15.7 12.4 %collective-permute-start.2 = (bf16[96,1024]{1,0:T(8,128)(2,1)S(1)}, bf16[96,1024]{1,0:T(8,128)(2,1)S(1)}, u32[]{:S(2)}, u32[]{:S(2)}) collective-permute-start(bf16[96,1024]{1,0:T(8,128)(2,1)S(1)} %get-tuple-element.41.own), channel_id=1, source_target_pairs={{0,48},{16,0},{32,16},{48,32},{1,49},{17,1},{33,17},{49,33},{2,50}... | collective-permute-start | bytes 589832 | tf_op jit(solution)/shard_map/ppermute | solution.py:530
  18.5 9.7 %collective-permute-start.1 = (bf16[96,1024]{1,0:T(8,128)(2,1)S(1)}, bf16[96,1024]{1,0:T(8,128)(2,1)S(1)}, u32[]{:S(2)}, u32[]{:S(2)}) collective-permute-start(bf16[96,1024]{1,0:T(8,128)(2,1)S(1)} %get-tuple-element.41.own), channel_id=1, source_target_pairs={{0,32},{16,48},{32,0},{48,16},{1,33},{17,49},{33,1},{49,17},{2,34}... | collective-permute-start | bytes 589832 | tf_op jit(solution)/shard_map/ppermute | solution.py:525
  23.9 7.9 %collective-permute-start = (bf16[96,1024]{1,0:T(8,128)(2,1)S(1)}, bf16[96,1024]{1,0:T(8,128)(2,1)S(1)}, u32[]{:S(2)}, u32[]{:S(2)}) collective-permute-start(bf16[96,1024]{1,0:T(8,128)(2,1)S(1)} %get-tuple-element.41.own), channel_id=1, source_target_pairs={{0,16},{16,32},{32,48},{48,0},{1,17},{17,33},{33,49},{49,1},{2,18}... | collective-permute-start | bytes 589832 | tf_op jit(solution)/shard_map/ppermute | solution.py:530
  26.0 25.9 %copy-start = (bf16[4,96,1024]{2,1,0:T(8,128)(2,1)}, bf16[4,96,1024]{2,1,0:T(8,128)(2,1)S(1)}, u32[]{:S(2)}) copy-start(bf16[4,96,1024]{2,1,0:T(8,128)(2,1)S(1)} %place.3.refs_5_) | copy-start | bytes 2359300
  26.0 18.2 %collective-permute-start.11 = (bf16[4,96,1024]{2,1,0:T(8,128)(2,1)S(1)}, bf16[4,96,1024]{2,1,0:T(8,128)(2,1)S(1)}, u32[]{:S(2)}, u32[]{:S(2)}) collective-permute-start(bf16[4,96,1024]{2,1,0:T(8,128)(2,1)S(1)} %place.3.refs_5_), channel_id=1, source_target_pairs={{0,48},{16,0},{32,16},{48,32},{1,49},{17,1},{33,17},{49,33},{2,50}... | collective-permute-start | bytes 2359304 | tf_op jit(solution)/shard_map/ppermute | solution.py:517
  28.0 20.0 %collective-permute-start.10 = (bf16[4,96,1024]{2,1,0:T(8,128)(2,1)S(1)}, bf16[4,96,1024]{2,1,0:T(8,128)(2,1)S(1)}, u32[]{:S(2)}, u32[]{:S(2)}) collective-permute-start(bf16[4,96,1024]{2,1,0:T(8,128)(2,1)S(1)} %place.3.refs_5_), channel_id=1, source_target_pairs={{0,16},{16,32},{32,48},{48,0},{1,17},{17,33},{33,49},{49,1},{2,18}... | collective-permute-start | bytes 2359304 | tf_op jit(solution)/shard_map/ppermute | solution.py:516
  32.4 37.4 %copy-start.1 = (bf16[4,96,1024]{2,1,0:T(8,128)(2,1)}, bf16[4,96,1024]{2,1,0:T(8,128)(2,1)S(1)}, u32[]{:S(2)}) copy-start(bf16[4,96,1024]{2,1,0:T(8,128)(2,1)S(1)} %place.2.refs_0_) | copy-start | bytes 2359300
  32.4 18.5 %collective-permute-start.4 = (bf16[4,96,1024]{2,1,0:T(8,128)(2,1)S(1)}, bf16[4,96,1024]{2,1,0:T(8,128)(2,1)S(1)}, u32[]{:S(2)}, u32[]{:S(2)}) collective-permute-start(bf16[4,96,1024]{2,1,0:T(8,128)(2,1)S(1)} %place.2.refs_0_), channel_id=1, source_target_pairs={{0,192},{64,0},{128,64},{192,128},{1,193},{65,1},{129,65},{193,129... | collective-permute-start | bytes 2359304 | tf_op jit(solution)/shard_map/ppermute | solution.py:517
  32.5 19.3 %collective-permute-start.3 = (bf16[4,96,1024]{2,1,0:T(8,128)(2,1)S(1)}, bf16[4,96,1024]{2,1,0:T(8,128)(2,1)S(1)}, u32[]{:S(2)}, u32[]{:S(2)}) collective-permute-start(bf16[4,96,1024]{2,1,0:T(8,128)(2,1)S(1)} %place.2.refs_0_), channel_id=1, source_target_pairs={{0,64},{64,128},{128,192},{192,0},{1,65},{65,129},{129,193},{193,1... | collective-permute-start | bytes 2359304 | tf_op jit(solution)/shard_map/ppermute | solution.py:516
  44.2 25.6 %copy-start.12 = (bf16[4,96,1024]{2,1,0:T(8,128)(2,1)}, bf16[4,96,1024]{2,1,0:T(8,128)(2,1)S(1)}, u32[]{:S(2)}) copy-start(bf16[4,96,1024]{2,1,0:T(8,128)(2,1)S(1)} %collective-permute-done.11.refs_7_) | copy-start | bytes 2359300
  44.3 10.3 %collective-permute-start.13 = (bf16[2,96,1024]{2,1,0:T(8,128)(2,1)S(1)}, bf16[2,96,1024]{2,1,0:T(8,128)(2,1)S(1)}, u32[]{:S(2)}, u32[]{:S(2)}) collective-permute-start(bf16[2,96,1024]{2,1,0:T(8,128)(2,1)S(1)} %slice.19), channel_id=1, source_target_pairs={{0,48},{16,0},{32,16},{48,32},{1,49},{17,1},{33,17},{49,33},{2,50}... | collective-permute-start | bytes 1179656 | tf_op jit(solution)/shard_map/ppermute | solution.py:519
  48.0 21.8 %copy-start.13 = (bf16[4,96,1024]{2,1,0:T(8,128)(2,1)}, bf16[4,96,1024]{2,1,0:T(8,128)(2,1)S(1)}, u32[]{:S(2)}) copy-start(bf16[4,96,1024]{2,1,0:T(8,128)(2,1)S(1)} %collective-permute-done.10.refs_6_) | copy-start | bytes 2359300
  48.1 10.9 %collective-permute-start.12 = (bf16[2,96,1024]{2,1,0:T(8,128)(2,1)S(1)}, bf16[2,96,1024]{2,1,0:T(8,128)(2,1)S(1)}, u32[]{:S(2)}, u32[]{:S(2)}) collective-permute-start(bf16[2,96,1024]{2,1,0:T(8,128)(2,1)S(1)} %slice.18), channel_id=1, source_target_pairs={{0,16},{16,32},{32,48},{48,0},{1,17},{17,33},{33,49},{49,1},{2,18}... | collective-permute-start | bytes 1179656 | tf_op jit(solution)/shard_map/ppermute | solution.py:518
  51.0 0.9 copy-start.14
  51.0 9.3 %collective-permute-start.6 = (bf16[2,96,1024]{2,1,0:T(8,128)(2,1)S(1)}, bf16[2,96,1024]{2,1,0:T(8,128)(2,1)S(1)}, u32[]{:S(2)}, u32[]{:S(2)}) collective-permute-start(bf16[2,96,1024]{2,1,0:T(8,128)(2,1)S(1)} %slice.17), channel_id=1, source_target_pairs={{0,192},{64,0},{128,64},{192,128},{1,193},{65,1},{129,65},{193,129... | collective-permute-start | bytes 1179656 | tf_op jit(solution)/shard_map/ppermute | solution.py:519
  51.9 8.4 %copy-start.15 = (bf16[4,96,1024]{2,1,0:T(8,128)(2,1)}, bf16[4,96,1024]{2,1,0:T(8,128)(2,1)S(1)}, u32[]{:S(2)}) copy-start(bf16[4,96,1024]{2,1,0:T(8,128)(2,1)S(1)} %collective-permute-done.3.refs_1_) | copy-start | bytes 2359300
  51.9 8.5 %collective-permute-start.5 = (bf16[2,96,1024]{2,1,0:T(8,128)(2,1)S(1)}, bf16[2,96,1024]{2,1,0:T(8,128)(2,1)}, u32[]{:S(2)}, u32[]{:S(2)}) collective-permute-start(bf16[2,96,1024]{2,1,0:T(8,128)(2,1)S(1)} %slice.16), channel_id=1, source_target_pairs={{0,64},{64,128},{128,192},{192,0},{1,65},{65,129},{129,193},{193,1... | collective-permute-start | bytes 1179656 | tf_op jit(solution)/shard_map/ppermute | solution.py:518
  54.6 15.2 %copy-start.17 = (bf16[2,96,1024]{2,1,0:T(8,128)(2,1)}, bf16[2,96,1024]{2,1,0:T(8,128)(2,1)S(1)}, u32[]{:S(2)}) copy-start(bf16[2,96,1024]{2,1,0:T(8,128)(2,1)S(1)} %collective-permute-done.13.refs_9_) | copy-start | bytes 1179652
  58.9 10.9 %copy-start.18 = (bf16[2,96,1024]{2,1,0:T(8,128)(2,1)}, bf16[2,96,1024]{2,1,0:T(8,128)(2,1)S(1)}, u32[]{:S(2)}) copy-start(bf16[2,96,1024]{2,1,0:T(8,128)(2,1)S(1)} %collective-permute-done.12.refs_8_) | copy-start | bytes 1179652
  60.3 9.6 %copy-start.19 = (bf16[2,96,1024]{2,1,0:T(8,128)(2,1)}, bf16[2,96,1024]{2,1,0:T(8,128)(2,1)S(1)}, u32[]{:S(2)}) copy-start(bf16[2,96,1024]{2,1,0:T(8,128)(2,1)S(1)} %collective-permute-done.6.refs_4_) | copy-start | bytes 1179652
  92.4 4.6 %collective-permute-start.18 = (bf16[8,136,1024]{2,1,0:T(8,128)(2,1)}, bf16[8,136,1024]{2,1,0:T(8,128)(2,1)S(1)}, u32[]{:S(2)}, u32[]{:S(2)}) collective-permute-start(bf16[8,136,1024]{2,1,0:T(8,128)(2,1)} %get-tuple-element.52), channel_id=1, source_target_pairs={{0,1},{1,0},{2,3},{3,2},{4,5},{5,4},{6,7},{7,6},{8,9},{9,8},{10,11... | collective-permute-start | bytes 6684680 | tf_op jit(solution)/shard_map/ppermute | solution.py:555
  98.9 3.9 %copy-start.16 = (bf16[2,96,1024]{2,1,0:T(8,128)(2,1)S(1)}, bf16[2,96,1024]{2,1,0:T(8,128)(2,1)}, u32[]{:S(2)}) copy-start(bf16[2,96,1024]{2,1,0:T(8,128)(2,1)} %get-tuple-element.47) | copy-start | bytes 1179652
  98.9 12.8 %copy-start.6 = (bf16[4,96,1024]{2,1,0:T(8,128)(2,1)S(1)}, bf16[4,96,1024]{2,1,0:T(8,128)(2,1)}, u32[]{:S(2)}) copy-start(bf16[4,96,1024]{2,1,0:T(8,128)(2,1)} %get-tuple-element.62.up) | copy-start | bytes 2359300
  98.9 12.8 %copy-start.7 = (bf16[4,96,1024]{2,1,0:T(8,128)(2,1)S(1)}, bf16[4,96,1024]{2,1,0:T(8,128)(2,1)}, u32[]{:S(2)}) copy-start(bf16[4,96,1024]{2,1,0:T(8,128)(2,1)} %get-tuple-element.63.down) | copy-start | bytes 2359300
  98.9 17.7 %copy-start.4 = (bf16[4,96,1024]{2,1,0:T(8,128)(2,1)S(1)}, bf16[4,96,1024]{2,1,0:T(8,128)(2,1)}, u32[]{:S(2)}) copy-start(bf16[4,96,1024]{2,1,0:T(8,128)(2,1)} %get-tuple-element.44.up) | copy-start | bytes 2359300
  98.9 17.7 %copy-start.5 = (bf16[4,96,1024]{2,1,0:T(8,128)(2,1)S(1)}, bf16[4,96,1024]{2,1,0:T(8,128)(2,1)}, u32[]{:S(2)}) copy-start(bf16[4,96,1024]{2,1,0:T(8,128)(2,1)} %get-tuple-element.45.down) | copy-start | bytes 2359300
  98.9 12.8 %collective-permute-start.22 = (bf16[2,96,1024]{2,1,0:T(8,128)(2,1)}, bf16[2,96,1024]{2,1,0:T(8,128)(2,1)S(1)}, u32[]{:S(2)}, u32[]{:S(2)}) collective-permute-start(bf16[2,96,1024]{2,1,0:T(8,128)(2,1)} %get-tuple-element.64), channel_id=1, source_target_pairs={{0,16},{16,32},{32,48},{48,0},{1,17},{17,33},{33,49},{49,1},{2,18}... | collective-permute-start | bytes 1179656 | tf_op jit(solution)/shard_map/ppermute | solution.py:530
  100.5 11.2 %collective-permute-start.23 = (bf16[2,96,1024]{2,1,0:T(8,128)(2,1)}, bf16[2,96,1024]{2,1,0:T(8,128)(2,1)S(1)}, u32[]{:S(2)}, u32[]{:S(2)}) collective-permute-start(bf16[2,96,1024]{2,1,0:T(8,128)(2,1)} %get-tuple-element.65), channel_id=1, source_target_pairs={{0,48},{16,0},{32,16},{48,32},{1,49},{17,1},{33,17},{49,33},{2,50}... | collective-permute-start | bytes 1179656 | tf_op jit(solution)/shard_map/ppermute | solution.py:530
  102.3 14.4 %collective-permute-start.14 = (bf16[2,96,1024]{2,1,0:T(8,128)(2,1)}, bf16[2,96,1024]{2,1,0:T(8,128)(2,1)S(1)}, u32[]{:S(2)}, u32[]{:S(2)}) collective-permute-start(bf16[2,96,1024]{2,1,0:T(8,128)(2,1)} %get-tuple-element.46), channel_id=1, source_target_pairs={{0,64},{64,128},{128,192},{192,0},{1,65},{65,129},{129,193},{193,1... | collective-permute-start | bytes 1179656 | tf_op jit(solution)/shard_map/ppermute | solution.py:530
  102.8 13.9 %collective-permute-start.15 = (bf16[2,96,1024]{2,1,0:T(8,128)(2,1)S(1)}, bf16[2,96,1024]{2,1,0:T(8,128)(2,1)S(1)}, u32[]{:S(2)}, u32[]{:S(2)}) collective-permute-start(bf16[2,96,1024]{2,1,0:T(8,128)(2,1)S(1)} %copy-done.16), channel_id=1, source_target_pairs={{0,192},{64,0},{128,64},{192,128},{1,193},{65,1},{129,65},{193,129... | collective-permute-start | bytes 1179656 | tf_op jit(solution)/shard_map/ppermute | solution.py:530
  111.7 21.8 %copy-start.3 = (bf16[4,96,1024]{2,1,0:T(8,128)(2,1)S(1)}, bf16[4,96,1024]{2,1,0:T(8,128)(2,1)}, u32[]{:S(2)}) copy-start(bf16[4,96,1024]{2,1,0:T(8,128)(2,1)} %get-tuple-element.61.own) | copy-start | bytes 2359300
  113.1 20.4 %collective-permute-start.24 = (bf16[4,96,1024]{2,1,0:T(8,128)(2,1)S(1)}, bf16[4,96,1024]{2,1,0:T(8,128)(2,1)S(1)}, u32[]{:S(2)}, u32[]{:S(2)}) collective-permute-start(bf16[4,96,1024]{2,1,0:T(8,128)(2,1)S(1)} %get-tuple-element.66), channel_id=1, source_target_pairs={{0,16},{16,32},{32,48},{48,0},{1,17},{17,33},{33,49},{49,1},{2,18}... | collective-permute-start | bytes 2359304 | tf_op jit(solution)/shard_map/ppermute | solution.py:530
  114.8 18.7 %collective-permute-start.25 = (bf16[4,96,1024]{2,1,0:T(8,128)(2,1)S(1)}, bf16[4,96,1024]{2,1,0:T(8,128)(2,1)S(1)}, u32[]{:S(2)}, u32[]{:S(2)}) collective-permute-start(bf16[4,96,1024]{2,1,0:T(8,128)(2,1)S(1)} %get-tuple-element.67), channel_id=1, source_target_pairs={{0,48},{16,0},{32,16},{48,32},{1,49},{17,1},{33,17},{49,33},{2,50}... | collective-permute-start | bytes 2359304 | tf_op jit(solution)/shard_map/ppermute | solution.py:530
  116.7 24.0 %copy-start.2 = (bf16[4,96,1024]{2,1,0:T(8,128)(2,1)S(1)}, bf16[4,96,1024]{2,1,0:T(8,128)(2,1)}, u32[]{:S(2)}) copy-start(bf16[4,96,1024]{2,1,0:T(8,128)(2,1)} %get-tuple-element.43.own) | copy-start | bytes 2359300
  118.1 19.7 %collective-permute-start.16 = (bf16[4,96,1024]{2,1,0:T(8,128)(2,1)S(1)}, bf16[4,96,1024]{2,1,0:T(8,128)(2,1)S(1)}, u32[]{:S(2)}, u32[]{:S(2)}) collective-permute-start(bf16[4,96,1024]{2,1,0:T(8,128)(2,1)S(1)} %get-tuple-element.48), channel_id=1, source_target_pairs={{0,64},{64,128},{128,192},{192,0},{1,65},{65,129},{129,193},{193,1... | collective-permute-start | bytes 2359304 | tf_op jit(solution)/shard_map/ppermute | solution.py:530
  118.6 22.1 %collective-permute-start.17 = (bf16[4,96,1024]{2,1,0:T(8,128)(2,1)S(1)}, bf16[4,96,1024]{2,1,0:T(8,128)(2,1)S(1)}, u32[]{:S(2)}, u32[]{:S(2)}) collective-permute-start(bf16[4,96,1024]{2,1,0:T(8,128)(2,1)S(1)} %get-tuple-element.49), channel_id=1, source_target_pairs={{0,192},{64,0},{128,64},{192,128},{1,193},{65,1},{129,65},{193,129... | collective-permute-start | bytes 2359304 | tf_op jit(solution)/shard_map/ppermute | solution.py:530
  133.8 8.2 %collective-permute-start.26 = (bf16[96,1024]{1,0:T(8,128)(2,1)S(1)}, bf16[96,1024]{1,0:T(8,128)(2,1)S(1)}, u32[]{:S(2)}, u32[]{:S(2)}) collective-permute-start(bf16[96,1024]{1,0:T(8,128)(2,1)S(1)} %get-tuple-element.69), channel_id=1, source_target_pairs={{0,64},{64,128},{128,192},{192,0},{1,65},{65,129},{129,193},{193,1... | collective-permute-start | bytes 589832 | tf_op jit(solution)/shard_map/ppermute | solution.py:530
  134.4 11.6 %collective-permute-start.27 = (bf16[96,1024]{1,0:T(8,128)(2,1)S(1)}, bf16[96,1024]{1,0:T(8,128)(2,1)S(1)}, u32[]{:S(2)}, u32[]{:S(2)}) collective-permute-start(bf16[96,1024]{1,0:T(8,128)(2,1)S(1)} %get-tuple-element.70), channel_id=1, source_target_pairs={{0,128},{64,192},{128,0},{192,64},{1,129},{65,193},{129,1},{193,65... | collective-permute-start | bytes 589832 | tf_op jit(solution)/shard_map/ppermute | solution.py:536
  136.8 9.5 %collective-permute-start.28 = (bf16[96,1024]{1,0:T(8,128)(2,1)S(1)}, bf16[96,1024]{1,0:T(8,128)(2,1)S(1)}, u32[]{:S(2)}, u32[]{:S(2)}) collective-permute-start(bf16[96,1024]{1,0:T(8,128)(2,1)S(1)} %get-tuple-element.71), channel_id=1, source_target_pairs={{0,192},{64,0},{128,64},{192,128},{1,193},{65,1},{129,65},{193,129... | collective-permute-start | bytes 589832 | tf_op jit(solution)/shard_map/ppermute | solution.py:530
  141.0 9.1 %collective-permute-start.19 = (bf16[96,1024]{1,0:T(8,128)(2,1)S(1)}, bf16[96,1024]{1,0:T(8,128)(2,1)S(1)}, u32[]{:S(2)}, u32[]{:S(2)}) collective-permute-start(bf16[96,1024]{1,0:T(8,128)(2,1)S(1)} %get-tuple-element.58), channel_id=1, source_target_pairs={{0,16},{16,32},{32,48},{48,0},{1,17},{17,33},{33,49},{49,1},{2,18}... | collective-permute-start | bytes 589832 | tf_op jit(solution)/shard_map/ppermute | solution.py:530
  141.1 9.0 %collective-permute-start.20 = (bf16[96,1024]{1,0:T(8,128)(2,1)S(1)}, bf16[96,1024]{1,0:T(8,128)(2,1)S(1)}, u32[]{:S(2)}, u32[]{:S(2)}) collective-permute-start(bf16[96,1024]{1,0:T(8,128)(2,1)S(1)} %get-tuple-element.59), channel_id=1, source_target_pairs={{0,32},{16,48},{32,0},{48,16},{1,33},{17,49},{33,1},{49,17},{2,34}... | collective-permute-start | bytes 589832 | tf_op jit(solution)/shard_map/ppermute | solution.py:536
  142.0 8.9 %collective-permute-start.21 = (bf16[96,1024]{1,0:T(8,128)(2,1)S(1)}, bf16[96,1024]{1,0:T(8,128)(2,1)S(1)}, u32[]{:S(2)}, u32[]{:S(2)}) collective-permute-start(bf16[96,1024]{1,0:T(8,128)(2,1)S(1)} %get-tuple-element.60), channel_id=1, source_target_pairs={{0,48},{16,0},{32,16},{48,32},{1,49},{17,1},{33,17},{49,33},{2,50}... | collective-permute-start | bytes 589832 | tf_op jit(solution)/shard_map/ppermute | solution.py:530
  144.3 1.0 copy-start.8
Sparse Core Ops, SparseCore 0:
  10.0 59.8 all-gather.2
  99.1 41.1 reduce-scatter.1
